TPU v7x, 128 devices: a whole 4x4x4 slice. The times are simulated.
128 devices in a mesh: leaf: 128 (over z, x, y, core).
Axes of the slice: x: 4, y: 4, z: 4, core: 2. Of those that a mesh axis runs over, the one named last changes fastest.
Arguments:
- points: bfloat16 [64, 524288], P(None, 'leaf'), may hold values from -3 to 7
- weights: bfloat16 [32, 524288], P(None, 'leaf'), may hold values from -6 to 6
- skel_index: int32 [65536], P('leaf'), may hold values from 0 to 4095, as said below
- assign: int32 [524288], P('leaf'), may hold values from 0 to 511
- near_leaf: int32 [1024, 12], replicated, may hold values from 0 to 1023, as said below
- near_count: int32 [1024], replicated, may hold values from 6 to 12
Outputs:
- near_field: float32 [32, 524288], P(None, 'leaf')
- far_field: float32 [32, 524288], P(None, 'leaf')
Inputs may be any that keep to these rules, and one draw needn't show every extreme that they name: `skel_index`: each device's 512 entries are distinct. `near_leaf`: leaf id g belongs to device g // 8. For each device r, its 96 entries read leaf by leaf and taken in runs of 128 - 1 (the last run may be shorter) name leaves of devices other than r, of distinct devices within a run; so a device reads at most 1 block from any one device, and this is reached.
All inputs are finite; a program needn't handle non-finite values.
Results may differ from a plain program's by a relative error of at most 0.0088.
Values may be sent and summed in bfloat16 or wider, within the bound.
No kernel may reach another device: no remote copies, remote signals or barrier semaphores. Data moves between devices by JAX's collectives and lax.ppermute only.
A program may use at most 128 MiB of HBM per device.

v0:
```python
import functools
import math

import jax
import jax.numpy as jnp
from jax import lax
from jax.experimental import pallas as pl
from jax.experimental.pallas import tpu as pltpu
from jax.sharding import Mesh, PartitionSpec as P

D = 64
RHS = 32
LEAF = 512
SKEL = 512
NEAR = 12
LEAVES_DEV = 8
P_DEV = LEAF * LEAVES_DEV
ROWS = D + RHS
N_DEV = 128
SIZES = {"z": 4, "x": 4, "y": 4, "core": 2}
AXES = ("z", "x", "y", "core")
DEPTH = 2 * D + 16
UNROLL = 4
SLOTS = LEAVES_DEV * NEAR
LOG = math.log2(math.e) / D
NEAR_SCALE = 4.0 / math.sqrt(LEAF * (NEAR + 1))
FAR_SCALE = 4.0 / math.sqrt(P_DEV * N_DEV)
LINE = (2, 1, 3, 0)


def shift(block, axis, by):
    count = SIZES[axis]
    return lax.ppermute(block, axis, [(i, (i + by) % count) for i in range(count)])


def swap(block, axis, bit):
    count = SIZES[axis]
    return lax.ppermute(block, axis, [(i, i ^ bit) for i in range(count)])


def norm_rows(coords, first):
    width = coords.shape[1]
    rest = jnp.sum(coords * coords, axis=0, keepdims=True) * (-LOG)
    row = lax.broadcasted_iota(jnp.int32, (16, width), 0)
    rows = jnp.where(row < 6, 1.0, 0.0)
    for part in range(3):
        piece = rest.astype(jnp.bfloat16).astype(jnp.float32)
        rest = rest - piece
        rows = jnp.where(row == first + part, piece, rows)
    return rows.astype(jnp.bfloat16)


def put_source(aug, coords):
    aug[0:D, :] = coords
    aug[D : 2 * D, :] = coords
    aug[2 * D :, :] = norm_rows(coords.astype(jnp.float32), 0)


def put_target(aug, coords):
    wide = coords.astype(jnp.float32)
    scaled = wide * (2.0 * LOG)
    high = scaled.astype(jnp.bfloat16)
    aug[0:D, :] = high
    aug[D : 2 * D, :] = (scaled - high.astype(jnp.float32)).astype(jnp.bfloat16)
    aug[2 * D :, :] = norm_rows(wide, 3)


def tile_apply(source_aug, target_aug, source_w):
    power = lax.dot_general(
        source_aug, target_aug, (((0,), (0,)), ((), ())), preferred_element_type=jnp.float32
    )
    tile = jnp.exp2(power).astype(jnp.bfloat16)
    return jnp.dot(source_w, tile, preferred_element_type=jnp.float32)


def own_kernel(block_ref, node_ref, self_ref, far_ref, target_aug, source_aug):
    for leaf in range(LEAVES_DEV):
        cols = slice(leaf * LEAF, (leaf + 1) * LEAF)
        put_target(target_aug.at[:, cols], block_ref[0:D, cols])

    @pl.loop(0, LEAVES_DEV // UNROLL)
    def _(group):
        for unit in range(UNROLL):
            start = pl.multiple_of((group * UNROLL + unit) * LEAF, LEAF)
            cols = pl.ds(start, LEAF)
            put_source(source_aug.at[unit], block_ref[0:D, cols])
            self_ref[:, cols] = tile_apply(
                source_aug[unit], target_aug[:, cols], block_ref[D:ROWS, cols]
            )

    far_ref[...] = jnp.zeros_like(far_ref)

    @pl.loop(0, node_ref.shape[0])
    def _(level):
        put_source(source_aug.at[0], node_ref[level, 0:D])
        far_ref[...] += tile_apply(source_aug[0], target_aug[...], node_ref[level, D:ROWS])

    far_ref[...] = far_ref[...] * FAR_SCALE


def own_terms(own_block, nodes):
    shape = jax.ShapeDtypeStruct((RHS, P_DEV), jnp.float32)
    levels = nodes.shape[0]
    entries = (levels * SKEL + LEAF) * P_DEV
    return pl.pallas_call(
        own_kernel,
        out_shape=(shape, shape),
        in_specs=[pl.BlockSpec(memory_space=pltpu.VMEM)] * 2,
        out_specs=(pl.BlockSpec(memory_space=pltpu.VMEM),) * 2,
        scratch_shapes=[
            pltpu.VMEM((DEPTH, P_DEV), jnp.bfloat16),
            pltpu.VMEM((UNROLL, DEPTH, LEAF), jnp.bfloat16),
        ],
        compiler_params=pltpu.CompilerParams(vmem_limit_bytes=40 << 20),
        cost_estimate=pl.CostEstimate(
            flops=entries * 2 * (DEPTH + RHS), transcendentals=entries, bytes_accessed=3 << 20
        ),
    )(own_block, nodes)


def near_kernel(scale, pair_ref, count_ref, target_ref, source_ref, out_ref, buf, sem, target_aug, source_aug, acc):
    groups = (count_ref[0] + (UNROLL - 1)) // UNROLL

    def copy(group, slot, unit):
        code = pair_ref[group * UNROLL + unit]
        block = code % 256
        col = pl.multiple_of((block % LEAVES_DEV) * LEAF, LEAF)
        return pltpu.make_async_copy(
            source_ref.at[block // LEAVES_DEV, :, pl.ds(col, LEAF)],
            buf.at[slot, unit],
            sem.at[slot, unit],
        )

    @pl.when(groups > 0)
    def _():
        for unit in range(UNROLL):
            copy(0, 0, unit).start()

    for leaf in range(LEAVES_DEV):
        put_target(target_aug.at[leaf], target_ref[0:D, leaf * LEAF : (leaf + 1) * LEAF])
    acc[...] = jnp.zeros_like(acc)

    @pl.loop(0, groups)
    def _(group):
        slot = group % 2

        @pl.when(group + 1 < groups)
        def _():
            for unit in range(UNROLL):
                copy(group + 1, 1 - slot, unit).start()

        for unit in range(UNROLL):
            copy(group, slot, unit).wait()
        for unit in range(UNROLL):
            target = pair_ref[group * UNROLL + unit] // 256
            put_source(source_aug.at[unit], buf[slot, unit, 0:D])
            acc[target] += tile_apply(
                source_aug[unit],
                target_aug[jnp.minimum(target, LEAVES_DEV - 1)],
                buf[slot, unit, D:ROWS],
            )

    for leaf in range(LEAVES_DEV):
        out_ref[:, leaf * LEAF : (leaf + 1) * LEAF] = acc[leaf].astype(out_ref.dtype)


def near_part(pairs, count, target, sources, dtype):
    entries = 24 * LEAF * LEAF
    return pl.pallas_call(
        functools.partial(near_kernel, 1.0),
        out_shape=jax.ShapeDtypeStruct((RHS, P_DEV), dtype),
        in_specs=[
            pl.BlockSpec(memory_space=pltpu.SMEM),
            pl.BlockSpec(memory_space=pltpu.SMEM),
            pl.BlockSpec(memory_space=pltpu.VMEM),
            pl.BlockSpec(memory_space=pl.ANY),
        ],
        out_specs=pl.BlockSpec(memory_space=pltpu.VMEM),
        scratch_shapes=[
            pltpu.VMEM((2, UNROLL, ROWS, LEAF), jnp.bfloat16),
            pltpu.SemaphoreType.DMA((2, UNROLL)),
            pltpu.VMEM((LEAVES_DEV, DEPTH, LEAF), jnp.bfloat16),
            pltpu.VMEM((UNROLL, DEPTH, LEAF), jnp.bfloat16),
            pltpu.VMEM((LEAVES_DEV + 1, RHS, LEAF), jnp.float32),
        ],
        compiler_params=pltpu.CompilerParams(vmem_limit_bytes=40 << 20),
        cost_estimate=pl.CostEstimate(
            flops=entries * 2 * (DEPTH + RHS), transcendentals=entries, bytes_accessed=4 << 20
        ),
    )(pairs, count, target, sources)


def fold(weights):
    half = weights.shape[-1] // 2
    summed = weights[:, :half].astype(jnp.float32) + weights[:, half:].astype(jnp.float32)
    return summed.astype(jnp.bfloat16)


def fold_node(node):
    half = SKEL // 2
    return jnp.concatenate([node[:D, :half], fold(node[D:])], axis=0)


def sibling_nodes(base, place):
    found = []
    current = base
    steps = [("core", 1)] + [(axis, bit) for axis in ("y", "x", "z") for bit in (1, 2)]
    for level, (axis, bit) in enumerate(steps):
        partner = swap(current, axis, bit)
        found.append(partner)
        if level + 1 < len(steps):
            upper = (place[axis] // bit) % 2
            mine, theirs = fold_node(current), fold_node(partner)
            current = jnp.concatenate(
                [jnp.where(upper == 0, mine, theirs), jnp.where(upper == 0, theirs, mine)], axis=1
            )
    return jnp.stack(found)


def pair_lists(near_leaf, near_count, place):
    rows, counts = [], []
    for by in LINE:
        y = (place["y"] + by) % SIZES["y"]
        device = ((place["z"] * 4 + place["x"]) * 4 + y) * 2 + place["core"]
        rows.append(lax.dynamic_slice_in_dim(near_leaf, device * LEAVES_DEV, LEAVES_DEV))
        counts.append(lax.dynamic_slice_in_dim(near_count, device * LEAVES_DEV, LEAVES_DEV))
    leaf_ids = jnp.stack(rows)
    used = jnp.arange(NEAR, dtype=jnp.int32)[None, None, :] < jnp.stack(counts)[:, :, None]
    owner = leaf_ids // LEAVES_DEV
    here = (owner // 2) % 4 == place["y"]
    valid = (used & here).reshape(len(LINE), SLOTS)
    gathered = (owner // 8) * 2 + owner % 2
    target = jnp.arange(LEAVES_DEV, dtype=jnp.int32)[None, :, None]
    code = (target * 256 + gathered * LEAVES_DEV + leaf_ids % LEAVES_DEV).reshape(len(LINE), SLOTS)
    slot = jnp.arange(SLOTS, dtype=jnp.int32)
    before = jnp.sum(
        (valid[:, None, :] & (slot[None, None, :] < slot[None, :, None])).astype(jnp.int32), axis=2
    )
    total = jnp.sum(valid.astype(jnp.int32), axis=1)
    hit = valid[:, None, :] & (before[:, None, :] == slot[None, :, None])
    packed = jnp.sum(jnp.where(hit, code[:, None, :], 0), axis=2)
    spare = LEAVES_DEV * 256
    return jnp.where(slot[None, :] < total[:, None], packed, spare), total


def per_device(points, weights, skel_index, assign, near_leaf, near_count):
    place = {axis: lax.axis_index(axis) for axis in AXES}
    own_block = jnp.concatenate([points, weights], axis=0)
    sources = lax.all_gather(own_block, ("z", "x", "core"))
    targets = [shift(points, "y", -by) if by else points for by in LINE]

    member = (assign[None, :] == jnp.arange(SKEL, dtype=jnp.int32)[:, None]).astype(jnp.bfloat16)
    base_weights = lax.dot_general(
        weights, member, (((1,), (1,)), ((), ())), preferred_element_type=jnp.float32
    )
    base = jnp.concatenate([points[:, skel_index], base_weights.astype(jnp.bfloat16)], axis=0)
    nodes = sibling_nodes(base, place)
    self_sum, far_field = own_terms(own_block, nodes)

    pairs, total = pair_lists(near_leaf, near_count, place)
    near_sum = self_sum
    for at, by in enumerate(LINE):
        part = near_part(
            pairs[at], total[at : at + 1], targets[at], sources, jnp.bfloat16 if by else jnp.float32
        )
        near_sum = near_sum + (shift(part, "y", by) if by else part).astype(jnp.float32)
    return (near_sum * NEAR_SCALE, far_field)


def solution(mesh):
    grid = Mesh(mesh.devices.reshape([SIZES[axis] for axis in AXES]), AXES)
    split = P(None, AXES)
    return jax.shard_map(
        per_device,
        mesh=grid,
        in_specs=(split, split, P(AXES), P(AXES), P(), P()),
        out_specs=(split, split),
        check_vma=False,
    )
```

profile of v0, /device:TPU:0, one launch (start us, length us, event | category | flops | bytes accessed | tf_op | source)
XLA Modules:
  0.0 185.4 jit_solution(7183519423044750398)
XLA Ops:
  7.2 1.1 constant_dynamic-update-slice_fusion.1
  8.3 1.0 constant_dynamic-update-slice_fusion.block_ref
  9.3 1.0 copy-done.1
  10.3 3.2 %collective-permute-start.9 = (bf16[64,4096]{1,0:T(8,128)(2,1)}, bf16[64,4096]{1,0:T(8,128)(2,1)S(1)}, u32[]{:S(2)}, u32[]{:S(2)}) collective-permute-start(bf16[64,4096]{1,0:T(8,128)(2,1)} %target_ref.1), channel_id=1, source_target_pairs={{0,6},{2,0},{4,2},{6,4},{1,7},{3,1},{5,3},{7,5},{8,14},{10,8},{12,... | collective-permute-start | bytes 1572872 | tf_op jit(solution)/shard_map/ppermute | solution.py:33
  13.4 2.2 %collective-permute-start.7 = (bf16[64,4096]{1,0:T(8,128)(2,1)}, bf16[64,4096]{1,0:T(8,128)(2,1)S(1)}, u32[]{:S(2)}, u32[]{:S(2)}) collective-permute-start(bf16[64,4096]{1,0:T(8,128)(2,1)} %target_ref.1), channel_id=1, source_target_pairs={{0,4},{2,6},{4,0},{6,2},{1,5},{3,7},{5,1},{7,3},{8,12},{10,14},{12... | collective-permute-start | bytes 1572872 | tf_op jit(solution)/shard_map/ppermute | solution.py:33
  15.6 1.6 copy.14
  17.2 0.7 compare_select_fusion
  17.9 1.3 gather_fusion
  19.2 0.1 copy.15
  19.3 2.5 %fusion.3 = bf16[32,512]{1,0:T(8,128)(2,1)S(1)} fusion(bf16[32,4096]{1,0:T(8,128)(2,1)} %param.7, s32[4096]{0:T(1024)} %param.9), kind=kOutput, calls=%fused_computation.5 | convolution fusion | flops 136331264 | bytes 311296 | tf_op jit(solution)/shard_map/dot_general | solution.py:253
  21.9 0.1 collective-permute-start
  22.2 0.1 constant_dynamic-slice_fusion.3
  22.2 0.1 copy.20
  22.3 0.1 copy.21
  22.4 0.1 copy.22
  22.6 0.1 dynamic-slice_bitcast_fusion.3
  22.7 0.1 lt.166
  22.9 0.1 stack.83
  23.0 0.1 stack.84
  23.1 0.1 stack.85
  23.1 0.1 lt.164
  23.3 0.1 add.271
  23.5 0.2 convert_reduce_fusion
  23.6 0.1 select_reduce_fusion
  23.8 0.2 convert_reduce_fusion.1
  24.1 0.7 fusion.24
  24.9 2.0 %collective-permute-start.1 = (bf16[96,512]{1,0:T(8,128)(2,1)S(1)}, bf16[96,512]{1,0:T(8,128)(2,1)S(1)}, u32[]{:S(2)}, u32[]{:S(2)}) collective-permute-start(bf16[96,512]{1,0:T(8,128)(2,1)S(1)} %pad_maximum_fusion.1), channel_id=1, source_target_pairs={{0,2},{2,0},{4,6},{6,4},{1,3},{3,1},{5,7},{7,5},{8,10},{10,8},{12,... | collective-permute-start | bytes 294920 | tf_op jit(solution)/shard_map/ppermute | solution.py:38
  26.9 11.3 %collective-permute-done.1 = bf16[96,512]{1,0:T(8,128)(2,1)S(1)} collective-permute-done((bf16[96,512]{1,0:T(8,128)(2,1)S(1)}, bf16[96,512]{1,0:T(8,128)(2,1)S(1)}, u32[]{:S(2)}, u32[]{:S(2)}) %collective-permute-start.1) | collective-permute-done | bytes 98336 | tf_op jit(solution)/shard_map/ppermute | solution.py:38
  38.3 2.7 %collective-permute-start.2 = (bf16[96,512]{1,0:T(8,128)(2,1)S(1)}, bf16[96,512]{1,0:T(8,128)(2,1)S(1)}, u32[]{:S(2)}, u32[]{:S(2)}) collective-permute-start(bf16[96,512]{1,0:T(8,128)(2,1)S(1)} %pad_maximum_fusion.2), channel_id=1, source_target_pairs={{0,4},{2,6},{4,0},{6,2},{1,5},{3,7},{5,1},{7,3},{8,12},{10,14},{12... | collective-permute-start | bytes 294920 | tf_op jit(solution)/shard_map/ppermute | solution.py:38
  41.0 3.5 %collective-permute-done.2 = bf16[96,512]{1,0:T(8,128)(2,1)S(1)} collective-permute-done((bf16[96,512]{1,0:T(8,128)(2,1)S(1)}, bf16[96,512]{1,0:T(8,128)(2,1)S(1)}, u32[]{:S(2)}, u32[]{:S(2)}) %collective-permute-start.2) | collective-permute-done | bytes 98336 | tf_op jit(solution)/shard_map/ppermute | solution.py:38
  44.5 1.6 collective-permute-start.3
  46.1 3.1 %collective-permute-done.3 = bf16[96,512]{1,0:T(8,128)(2,1)S(1)} collective-permute-done((bf16[96,512]{1,0:T(8,128)(2,1)S(1)}, bf16[96,512]{1,0:T(8,128)(2,1)S(1)}, u32[]{:S(2)}, u32[]{:S(2)}) %collective-permute-start.3) | collective-permute-done | bytes 98336 | tf_op jit(solution)/shard_map/ppermute | solution.py:38
  49.3 3.1 %collective-permute-start.4 = (bf16[96,512]{1,0:T(8,128)(2,1)S(1)}, bf16[96,512]{1,0:T(8,128)(2,1)S(1)}, u32[]{:S(2)}, u32[]{:S(2)}) collective-permute-start(bf16[96,512]{1,0:T(8,128)(2,1)S(1)} %pad_maximum_fusion.4), channel_id=1, source_target_pairs={{0,16},{8,24},{16,0},{24,8},{1,17},{9,25},{17,1},{25,9},{2,18},{10... | collective-permute-start | bytes 294920 | tf_op jit(solution)/shard_map/ppermute | solution.py:38
  52.4 5.1 %collective-permute-done.4 = bf16[96,512]{1,0:T(8,128)(2,1)S(1)} collective-permute-done((bf16[96,512]{1,0:T(8,128)(2,1)S(1)}, bf16[96,512]{1,0:T(8,128)(2,1)S(1)}, u32[]{:S(2)}, u32[]{:S(2)}) %collective-permute-start.4) | collective-permute-done | bytes 98336 | tf_op jit(solution)/shard_map/ppermute | solution.py:38
  57.6 2.0 %collective-permute-start.5 = (bf16[96,512]{1,0:T(8,128)(2,1)S(1)}, bf16[96,512]{1,0:T(8,128)(2,1)S(1)}, u32[]{:S(2)}, u32[]{:S(2)}) collective-permute-start(bf16[96,512]{1,0:T(8,128)(2,1)S(1)} %pad_maximum_fusion.5), channel_id=1, source_target_pairs={{0,32},{32,0},{64,96},{96,64},{1,33},{33,1},{65,97},{97,65},{2,34}... | collective-permute-start | bytes 294920 | tf_op jit(solution)/shard_map/ppermute | solution.py:38
  59.6 4.7 %collective-permute-done.5 = bf16[96,512]{1,0:T(8,128)(2,1)S(1)} collective-permute-done((bf16[96,512]{1,0:T(8,128)(2,1)S(1)}, bf16[96,512]{1,0:T(8,128)(2,1)S(1)}, u32[]{:S(2)}, u32[]{:S(2)}) %collective-permute-start.5) | collective-permute-done | bytes 98336 | tf_op jit(solution)/shard_map/ppermute | solution.py:38
  64.5 5.2 %collective-permute-start.6 = (bf16[96,512]{1,0:T(8,128)(2,1)S(1)}, bf16[96,512]{1,0:T(8,128)(2,1)S(1)}, u32[]{:S(2)}, u32[]{:S(2)}) collective-permute-start(bf16[96,512]{1,0:T(8,128)(2,1)S(1)} %pad_maximum_fusion.6), channel_id=1, source_target_pairs={{0,64},{32,96},{64,0},{96,32},{1,65},{33,97},{65,1},{97,33},{2,66}... | collective-permute-start | bytes 294920 | tf_op jit(solution)/shard_map/ppermute | solution.py:38
  69.7 4.7 %collective-permute-done.6 = bf16[96,512]{1,0:T(8,128)(2,1)S(1)} collective-permute-done((bf16[96,512]{1,0:T(8,128)(2,1)S(1)}, bf16[96,512]{1,0:T(8,128)(2,1)S(1)}, u32[]{:S(2)}, u32[]{:S(2)}) %collective-permute-start.6) | collective-permute-done | bytes 98336 | tf_op jit(solution)/shard_map/ppermute | solution.py:38
  74.4 33.3 %all-gather.3.cloned.1.call-done = bf16[3072,4096]{1,0:T(8,128)(2,1)} async-done(((bf16[96,4096]{1,0:T(8,128)(2,1)}), bf16[3072,4096]{1,0:T(8,128)(2,1)}) %all-gather.3.cloned.1.call-update) | async-done | bytes 25165840 | tf_op jit(solution)/shard_map/all_gather | solution.py:249
  107.7 9.8 %shard_map.79 = bf16[32,4096]{1,0:T(8,128)(2,1)S(1)} custom-call(s32[96]{0:T(128)S(1)} %get-tuple-element.29.pair_ref, s32[1]{0:T(128)} %get-tuple-element.33.count_ref, bf16[64,4096]{1,0:T(8,128)(2,1)S(1)} %collective-permute-done.9.target_ref, bf16[32,96,4096]{2,1,0:T(8,128)(2,1)} %bitcast.39), custom_call_target="tpu_custom_call" | custom-call | flops 2214592512 | bytes 4194304 | tf_op jit(solution)/shard_map/pallas_call | solution.py:169
  117.5 3.0 %collective-permute-start.10 = (bf16[32,4096]{1,0:T(8,128)(2,1)S(1)}, bf16[32,4096]{1,0:T(8,128)(2,1)S(1)}, u32[]{:S(2)}, u32[]{:S(2)}) collective-permute-start(bf16[32,4096]{1,0:T(8,128)(2,1)S(1)} %shard_map.79), channel_id=1, source_target_pairs={{0,2},{2,4},{4,6},{6,0},{1,3},{3,5},{5,7},{7,1},{8,10},{10,12},{12... | collective-permute-start | bytes 786440 | tf_op jit(solution)/shard_map/ppermute | solution.py:33
  120.6 8.3 %shard_map.80 = bf16[32,4096]{1,0:T(8,128)(2,1)S(1)} custom-call(s32[96]{0:T(128)S(1)} %get-tuple-element.28.pair_ref, s32[1]{0:T(128)} %get-tuple-element.32.count_ref, bf16[64,4096]{1,0:T(8,128)(2,1)S(1)} %collective-permute-done.11.target_ref, bf16[32,96,4096]{2,1,0:T(8,128)(2,1)} %bitcast.40), custom_call_target="tpu_custom_call" | custom-call | flops 2214592512 | bytes 4194304 | tf_op jit(solution)/shard_map/pallas_call | solution.py:169
  128.8 5.8 %collective-permute-start.12 = (bf16[32,4096]{1,0:T(8,128)(2,1)S(1)}, bf16[32,4096]{1,0:T(8,128)(2,1)S(1)}, u32[]{:S(2)}, u32[]{:S(2)}) collective-permute-start(bf16[32,4096]{1,0:T(8,128)(2,1)S(1)} %shard_map.80), channel_id=1, source_target_pairs={{0,6},{2,0},{4,2},{6,4},{1,7},{3,1},{5,3},{7,5},{8,14},{10,8},{12,... | collective-permute-start | bytes 786440 | tf_op jit(solution)/shard_map/ppermute | solution.py:33
  134.6 12.8 %shard_map.78 = bf16[32,4096]{1,0:T(8,128)(2,1)S(1)} custom-call(s32[96]{0:T(128)S(1)} %get-tuple-element.26.pair_ref, s32[1]{0:T(128)} %get-tuple-element.30.count_ref, bf16[64,4096]{1,0:T(8,128)(2,1)S(1)} %collective-permute-done.7.target_ref, bf16[32,96,4096]{2,1,0:T(8,128)(2,1)} %bitcast.41), custom_call_target="tpu_custom_call" | custom-call | flops 2214592512 | bytes 4194304 | tf_op jit(solution)/shard_map/pallas_call | solution.py:169
  147.4 0.9 collective-permute-start.8
  148.3 18.0 %shard_map.77 = (f32[32,4096]{1,0:T(8,128)S(1)}, f32[32,4096]{1,0:T(8,128)}) custom-call(bf16[96,4096]{1,0:T(8,128)(2,1)S(1)} %copy-done.2, bf16[7,96,512]{2,1,0:T(8,128)(2,1)S(1)} %bitcast_dynamic-update-slice_fusion.node_ref), custom_call_target="tpu_custom_call" | custom-call | flops 5905580032 | bytes 3145728 | tf_op jit(solution)/shard_map/pallas_call | solution.py:105
  166.3 11.2 %shard_map.81 = f32[32,4096]{1,0:T(8,128)S(1)} custom-call(s32[96]{0:T(128)S(1)} %get-tuple-element.27.pair_ref, s32[1]{0:T(128)} %get-tuple-element.31.count_ref, bf16[64,4096]{1,0:T(8,128)(2,1)S(1)} %copy-done, bf16[32,96,4096]{2,1,0:T(8,128)(2,1)} %bitcast.42), custom_call_target="tpu_custom_call" | custom-call | flops 2214592512 | bytes 4194304 | tf_op jit(solution)/shard_map/pallas_call | solution.py:169
  177.6 1.0 add_multiply_fusion
  (76 shorter events, 1.0 us)
Async XLA Ops:
  7.2 15.0 %copy-start.3 = (s32[1024,12]{0,1:T(8,128)S(1)}, s32[1024,12]{0,1:T(8,128)}, u32[]{:S(2)}) copy-start(s32[1024,12]{0,1:T(8,128)} %param.10) | copy-start | bytes 147460
  7.2 15.4 %copy-start.4 = (s32[1024]{0:T(1024)S(1)}, s32[1024]{0:T(1024)}, u32[]{:S(2)}) copy-start(s32[1024]{0:T(1024)} %param.11) | copy-start | bytes 12292
  7.2 100.5 %all-gather.3.cloned.1.call-start = ((), (), s32[]{:S(2)}) async-start(), calls=%async_computation | async-start | bytes 25952256 | tf_op jit(solution)/shard_map/all_gather | solution.py:249
  9.3 1.0 copy-start.1
  10.3 64.1 %collective-permute-start.9 = (bf16[64,4096]{1,0:T(8,128)(2,1)}, bf16[64,4096]{1,0:T(8,128)(2,1)S(1)}, u32[]{:S(2)}, u32[]{:S(2)}) collective-permute-start(bf16[64,4096]{1,0:T(8,128)(2,1)} %target_ref.1), channel_id=1, source_target_pairs={{0,6},{2,0},{4,2},{6,4},{1,7},{3,1},{5,3},{7,5},{8,14},{10,8},{12,... | collective-permute-start | bytes 1572872 | tf_op jit(solution)/shard_map/ppermute | solution.py:33
  13.4 107.1 %collective-permute-start.11 = (bf16[64,4096]{1,0:T(8,128)(2,1)}, bf16[64,4096]{1,0:T(8,128)(2,1)S(1)}, u32[]{:S(2)}, u32[]{:S(2)}) collective-permute-start(bf16[64,4096]{1,0:T(8,128)(2,1)} %target_ref.1), channel_id=1, source_target_pairs={{0,2},{2,4},{4,6},{6,0},{1,3},{3,5},{5,7},{7,1},{8,10},{10,12},{12... | collective-permute-start | bytes 1572872 | tf_op jit(solution)/shard_map/ppermute | solution.py:33
  13.4 121.2 %collective-permute-start.7 = (bf16[64,4096]{1,0:T(8,128)(2,1)}, bf16[64,4096]{1,0:T(8,128)(2,1)S(1)}, u32[]{:S(2)}, u32[]{:S(2)}) collective-permute-start(bf16[64,4096]{1,0:T(8,128)(2,1)} %target_ref.1), channel_id=1, source_target_pairs={{0,4},{2,6},{4,0},{6,2},{1,5},{3,7},{5,1},{7,3},{8,12},{10,14},{12... | collective-permute-start | bytes 1572872 | tf_op jit(solution)/shard_map/ppermute | solution.py:33
  21.9 2.9 %collective-permute-start = (bf16[96,512]{1,0:T(8,128)(2,1)S(1)}, bf16[96,512]{1,0:T(8,128)(2,1)S(1)}, u32[]{:S(2)}, u32[]{:S(2)}) collective-permute-start(bf16[96,512]{1,0:T(8,128)(2,1)S(1)} %pad_maximum_fusion), channel_id=1, source_target_pairs={{0,1},{1,0},{2,3},{3,2},{4,5},{5,4},{6,7},{7,6},{8,9},{9,8},{10,11... | collective-permute-start | bytes 294920 | tf_op jit(solution)/shard_map/ppermute | solution.py:38
  24.9 13.3 %collective-permute-start.1 = (bf16[96,512]{1,0:T(8,128)(2,1)S(1)}, bf16[96,512]{1,0:T(8,128)(2,1)S(1)}, u32[]{:S(2)}, u32[]{:S(2)}) collective-permute-start(bf16[96,512]{1,0:T(8,128)(2,1)S(1)} %pad_maximum_fusion.1), channel_id=1, source_target_pairs={{0,2},{2,0},{4,6},{6,4},{1,3},{3,1},{5,7},{7,5},{8,10},{10,8},{12,... | collective-permute-start | bytes 294920 | tf_op jit(solution)/shard_map/ppermute | solution.py:38
  38.3 6.2 %collective-permute-start.2 = (bf16[96,512]{1,0:T(8,128)(2,1)S(1)}, bf16[96,512]{1,0:T(8,128)(2,1)S(1)}, u32[]{:S(2)}, u32[]{:S(2)}) collective-permute-start(bf16[96,512]{1,0:T(8,128)(2,1)S(1)} %pad_maximum_fusion.2), channel_id=1, source_target_pairs={{0,4},{2,6},{4,0},{6,2},{1,5},{3,7},{5,1},{7,3},{8,12},{10,14},{12... | collective-permute-start | bytes 294920 | tf_op jit(solution)/shard_map/ppermute | solution.py:38
  44.5 4.7 %collective-permute-start.3 = (bf16[96,512]{1,0:T(8,128)(2,1)S(1)}, bf16[96,512]{1,0:T(8,128)(2,1)S(1)}, u32[]{:S(2)}, u32[]{:S(2)}) collective-permute-start(bf16[96,512]{1,0:T(8,128)(2,1)S(1)} %pad_maximum_fusion.3), channel_id=1, source_target_pairs={{0,8},{8,0},{16,24},{24,16},{1,9},{9,1},{17,25},{25,17},{2,10},{10... | collective-permute-start | bytes 294920 | tf_op jit(solution)/shard_map/ppermute | solution.py:38
  49.3 8.3 %collective-permute-start.4 = (bf16[96,512]{1,0:T(8,128)(2,1)S(1)}, bf16[96,512]{1,0:T(8,128)(2,1)S(1)}, u32[]{:S(2)}, u32[]{:S(2)}) collective-permute-start(bf16[96,512]{1,0:T(8,128)(2,1)S(1)} %pad_maximum_fusion.4), channel_id=1, source_target_pairs={{0,16},{8,24},{16,0},{24,8},{1,17},{9,25},{17,1},{25,9},{2,18},{10... | collective-permute-start | bytes 294920 | tf_op jit(solution)/shard_map/ppermute | solution.py:38
  57.6 6.8 %collective-permute-start.5 = (bf16[96,512]{1,0:T(8,128)(2,1)S(1)}, bf16[96,512]{1,0:T(8,128)(2,1)S(1)}, u32[]{:S(2)}, u32[]{:S(2)}) collective-permute-start(bf16[96,512]{1,0:T(8,128)(2,1)S(1)} %pad_maximum_fusion.5), channel_id=1, source_target_pairs={{0,32},{32,0},{64,96},{96,64},{1,33},{33,1},{65,97},{97,65},{2,34}... | collective-permute-start | bytes 294920 | tf_op jit(solution)/shard_map/ppermute | solution.py:38
  64.5 9.9 %collective-permute-start.6 = (bf16[96,512]{1,0:T(8,128)(2,1)S(1)}, bf16[96,512]{1,0:T(8,128)(2,1)S(1)}, u32[]{:S(2)}, u32[]{:S(2)}) collective-permute-start(bf16[96,512]{1,0:T(8,128)(2,1)S(1)} %pad_maximum_fusion.6), channel_id=1, source_target_pairs={{0,64},{32,96},{64,0},{96,32},{1,65},{33,97},{65,1},{97,33},{2,66}... | collective-permute-start | bytes 294920 | tf_op jit(solution)/shard_map/ppermute | solution.py:38
  117.5 60.0 %collective-permute-start.10 = (bf16[32,4096]{1,0:T(8,128)(2,1)S(1)}, bf16[32,4096]{1,0:T(8,128)(2,1)S(1)}, u32[]{:S(2)}, u32[]{:S(2)}) collective-permute-start(bf16[32,4096]{1,0:T(8,128)(2,1)S(1)} %shard_map.79), channel_id=1, source_target_pairs={{0,2},{2,4},{4,6},{6,0},{1,3},{3,5},{5,7},{7,1},{8,10},{10,12},{12... | collective-permute-start | bytes 786440 | tf_op jit(solution)/shard_map/ppermute | solution.py:33
  128.8 48.7 %collective-permute-start.12 = (bf16[32,4096]{1,0:T(8,128)(2,1)S(1)}, bf16[32,4096]{1,0:T(8,128)(2,1)S(1)}, u32[]{:S(2)}, u32[]{:S(2)}) collective-permute-start(bf16[32,4096]{1,0:T(8,128)(2,1)S(1)} %shard_map.80), channel_id=1, source_target_pairs={{0,6},{2,0},{4,2},{6,4},{1,7},{3,1},{5,3},{7,5},{8,14},{10,8},{12,... | collective-permute-start | bytes 786440 | tf_op jit(solution)/shard_map/ppermute | solution.py:33
  134.6 13.7 %copy-start.2 = (bf16[96,4096]{1,0:T(8,128)(2,1)S(1)}, bf16[96,4096]{1,0:T(8,128)(2,1)}, u32[]{:S(2)}) copy-start(bf16[96,4096]{1,0:T(8,128)(2,1)} %copy-done.1) | copy-start | bytes 2359300
  147.4 18.9 %copy-start = (bf16[64,4096]{1,0:T(8,128)(2,1)S(1)}, bf16[64,4096]{1,0:T(8,128)(2,1)}, u32[]{:S(2)}) copy-start(bf16[64,4096]{1,0:T(8,128)(2,1)} %target_ref.1) | copy-start | bytes 1572868
  147.4 30.1 %collective-permute-start.8 = (bf16[32,4096]{1,0:T(8,128)(2,1)S(1)}, bf16[32,4096]{1,0:T(8,128)(2,1)S(1)}, u32[]{:S(2)}, u32[]{:S(2)}) collective-permute-start(bf16[32,4096]{1,0:T(8,128)(2,1)S(1)} %shard_map.78), channel_id=1, source_target_pairs={{0,4},{2,6},{4,0},{6,2},{1,5},{3,7},{5,1},{7,3},{8,12},{10,14},{12... | collective-permute-start | bytes 786440 | tf_op jit(solution)/shard_map/ppermute | solution.py:33
Sparse Core Ops, SparseCore 0:
  10.4 97.2 all-gather.2
where the time goes:
time: 187 us; the launch traced here: 185 us
  waiting for transfers between devices  65.8 us (35%)
  Pallas kernels  60.1 us (32%)
  starting transfers between devices  31.8 us (17%)
  between operations  14.6 us (8%)
  local copies, waits for them, and re-layouts  7.97 us (4%)
  other arithmetic  2.66 us (1%)
  matrix products  2.51 us (1%)
    pallas_call x4, Pallas kernels, near_part(): pl.pallas_call(functools.partial(near_kernel, 1.0), out_shape=jax.ShapeDt...  42 us
    all_gather x1, waiting for transfers between devices, per_device(): sources = lax.all_gather(own_block, ('z', 'x', 'core'))  33.3 us
    ppermute x7, waiting for transfers between devices, swap(): return lax.ppermute(block, axis, [(i, i ^ bit) for i in range(count)])  32.4 us
    pallas_call x1, Pallas kernels, own_terms(): pl.pallas_call(own_kernel, out_shape=(shape, shape), in_specs=[pl.BlockSp...  18 us
    ppermute x7, starting transfers between devices, swap(): return lax.ppermute(block, axis, [(i, i ^ bit) for i in range(count)])  16.7 us
    ppermute x6, starting transfers between devices, shift(): lax.ppermute(block, axis, [(i, (i + by) % count) for i in range(count)])  15.1 us
    unnamed x22, local copies, waits for them, and re-layouts  3.97 us
  transfers between devices with their start and end apart: 14, of which 7 were waited for; matrix products, arithmetic and copies ran while one was open for 5% of the time, Pallas kernels for 32%

commit v1 on v0

--- a/solution.py
+++ b/solution.py
@@ -256,6 +256,7 @@
     base = jnp.concatenate([points[:, skel_index], base_weights.astype(jnp.bfloat16)], axis=0)
     nodes = sibling_nodes(base, place)
     self_sum, far_field = own_terms(own_block, nodes)
+    sources, self_sum, far_field = lax.optimization_barrier((sources, self_sum, far_field))
 
     pairs, total = pair_lists(near_leaf, near_count, place)
     near_sum = self_sum

time: 187 us -> 169 us (0.904)
  waiting for transfers between devices: 65.8 us -> 46.9 us
  Pallas kernels: 60.1 us -> 55.5 us
  starting transfers between devices: 31.8 us -> 34.8 us
    all_gather x1, waiting for transfers between devices: 33.3 us -> 15.2 us  [per_device(): sources = lax.all_gather(own_block, ('z', 'x', 'core'))]
    pallas_call x4, Pallas kernels: 42 us -> 37.5 us  [near_part(): pl.pallas_call(functools.partial(near_kernel, 1.0), out_shape=jax.ShapeDt...]
    ppermute x6, starting transfers between devices: 15.1 us -> 18 us  [shift(): lax.ppermute(block, axis, [(i, (i + by) % count) for i in range(count)])]
    unnamed x22 -> x20, local copies, waits for them, and re-layouts: 3.97 us -> 3.96 us
  transfers between devices with their start and end apart: 14 -> 14, of which waited for: 7 -> 7; matrix products, arithmetic and copies ran while one was open for 5% -> 6% of each run, Pallas kernels for 32% -> 34%
where the time goes in v1:
time: 169 us; the launch traced here: 166 us
  Pallas kernels  55.5 us (33%)
  waiting for transfers between devices  46.9 us (28%)
  starting transfers between devices  34.8 us (21%)
  between operations  14.6 us (9%)
  local copies, waits for them, and re-layouts  8.81 us (5%)
  other arithmetic  2.65 us (2%)
  matrix products  2.51 us (1%)
    pallas_call x4, Pallas kernels, near_part(): pl.pallas_call(functools.partial(near_kernel, 1.0), out_shape=jax.ShapeDt...  37.5 us
    ppermute x7, waiting for transfers between devices, swap(): return lax.ppermute(block, axis, [(i, i ^ bit) for i in range(count)])  31.6 us
    ppermute x6, starting transfers between devices, shift(): lax.ppermute(block, axis, [(i, (i + by) % count) for i in range(count)])  18 us
    pallas_call x1, Pallas kernels, own_terms(): pl.pallas_call(own_kernel, out_shape=(shape, shape), in_specs=[pl.BlockSp...  18 us
    ppermute x7, starting transfers between devices, swap(): return lax.ppermute(block, axis, [(i, i ^ bit) for i in range(count)])  16.7 us
    all_gather x1, waiting for transfers between devices, per_device(): sources = lax.all_gather(own_block, ('z', 'x', 'core'))  15.2 us
    unnamed x20, local copies, waits for them, and re-layouts  3.96 us
  transfers between devices with their start and end apart: 14, of which 7 were waited for; matrix products, arithmetic and copies ran while one was open for 6% of the time, Pallas kernels for 34%

profile of v1, /device:TPU:0, one launch (start us, length us, event | category | flops | bytes accessed | tf_op | source)
XLA Modules:
  0.0 165.7 jit_solution(5908150092119579867)
XLA Ops:
  7.2 1.1 constant_dynamic-update-slice_fusion.1
  8.3 1.0 constant_dynamic-update-slice_fusion.block_ref
  9.3 1.0 copy-done.1
  10.3 3.2 %collective-permute-start.9 = (bf16[64,4096]{1,0:T(8,128)(2,1)}, bf16[64,4096]{1,0:T(8,128)(2,1)S(1)}, u32[]{:S(2)}, u32[]{:S(2)}) collective-permute-start(bf16[64,4096]{1,0:T(8,128)(2,1)} %target_ref.1), channel_id=1, source_target_pairs={{0,6},{2,0},{4,2},{6,4},{1,7},{3,1},{5,3},{7,5},{8,14},{10,8},{12,... | collective-permute-start | bytes 1572872 | tf_op jit(solution)/shard_map/ppermute | solution.py:33
  13.4 2.2 %collective-permute-start.7 = (bf16[64,4096]{1,0:T(8,128)(2,1)}, bf16[64,4096]{1,0:T(8,128)(2,1)S(1)}, u32[]{:S(2)}, u32[]{:S(2)}) collective-permute-start(bf16[64,4096]{1,0:T(8,128)(2,1)} %target_ref.1), channel_id=1, source_target_pairs={{0,4},{2,6},{4,0},{6,2},{1,5},{3,7},{5,1},{7,3},{8,12},{10,14},{12... | collective-permute-start | bytes 1572872 | tf_op jit(solution)/shard_map/ppermute | solution.py:33
  15.6 1.6 copy.14
  17.2 0.7 compare_select_fusion
  17.9 1.3 gather_fusion
  19.2 0.1 copy.15
  19.3 2.5 %fusion.3 = bf16[32,512]{1,0:T(8,128)(2,1)S(1)} fusion(bf16[32,4096]{1,0:T(8,128)(2,1)} %param.7, s32[4096]{0:T(1024)} %param.9), kind=kOutput, calls=%fused_computation.5 | convolution fusion | flops 136331264 | bytes 311296 | tf_op jit(solution)/shard_map/dot_general | solution.py:253
  21.9 0.1 collective-permute-start
  22.2 0.9 constant_dynamic-slice_fusion.3
  23.1 0.1 copy.20
  23.2 0.1 copy.21
  23.2 0.1 copy.22
  23.4 0.1 dynamic-slice_bitcast_fusion.3
  23.6 0.1 lt.166
  23.7 0.1 stack.83
  23.8 0.1 stack.84
  23.9 0.1 stack.85
  24.0 0.1 lt.164
  24.1 0.1 add.271
  24.3 0.2 convert_reduce_fusion
  24.5 0.1 select_reduce_fusion
  24.6 0.2 convert_reduce_fusion.1
  25.0 0.7 fusion.24
  25.7 2.0 %collective-permute-start.1 = (bf16[96,512]{1,0:T(8,128)(2,1)S(1)}, bf16[96,512]{1,0:T(8,128)(2,1)S(1)}, u32[]{:S(2)}, u32[]{:S(2)}) collective-permute-start(bf16[96,512]{1,0:T(8,128)(2,1)S(1)} %pad_maximum_fusion.1), channel_id=1, source_target_pairs={{0,2},{2,0},{4,6},{6,4},{1,3},{3,1},{5,7},{7,5},{8,10},{10,8},{12,... | collective-permute-start | bytes 294920 | tf_op jit(solution)/shard_map/ppermute | solution.py:38
  27.7 10.5 %collective-permute-done.1 = bf16[96,512]{1,0:T(8,128)(2,1)S(1)} collective-permute-done((bf16[96,512]{1,0:T(8,128)(2,1)S(1)}, bf16[96,512]{1,0:T(8,128)(2,1)S(1)}, u32[]{:S(2)}, u32[]{:S(2)}) %collective-permute-start.1) | collective-permute-done | bytes 98336 | tf_op jit(solution)/shard_map/ppermute | solution.py:38
  38.3 2.7 %collective-permute-start.2 = (bf16[96,512]{1,0:T(8,128)(2,1)S(1)}, bf16[96,512]{1,0:T(8,128)(2,1)S(1)}, u32[]{:S(2)}, u32[]{:S(2)}) collective-permute-start(bf16[96,512]{1,0:T(8,128)(2,1)S(1)} %pad_maximum_fusion.2), channel_id=1, source_target_pairs={{0,4},{2,6},{4,0},{6,2},{1,5},{3,7},{5,1},{7,3},{8,12},{10,14},{12... | collective-permute-start | bytes 294920 | tf_op jit(solution)/shard_map/ppermute | solution.py:38
  41.0 3.5 %collective-permute-done.2 = bf16[96,512]{1,0:T(8,128)(2,1)S(1)} collective-permute-done((bf16[96,512]{1,0:T(8,128)(2,1)S(1)}, bf16[96,512]{1,0:T(8,128)(2,1)S(1)}, u32[]{:S(2)}, u32[]{:S(2)}) %collective-permute-start.2) | collective-permute-done | bytes 98336 | tf_op jit(solution)/shard_map/ppermute | solution.py:38
  44.5 1.6 collective-permute-start.3
  46.1 3.1 %collective-permute-done.3 = bf16[96,512]{1,0:T(8,128)(2,1)S(1)} collective-permute-done((bf16[96,512]{1,0:T(8,128)(2,1)S(1)}, bf16[96,512]{1,0:T(8,128)(2,1)S(1)}, u32[]{:S(2)}, u32[]{:S(2)}) %collective-permute-start.3) | collective-permute-done | bytes 98336 | tf_op jit(solution)/shard_map/ppermute | solution.py:38
  49.3 3.1 %collective-permute-start.4 = (bf16[96,512]{1,0:T(8,128)(2,1)S(1)}, bf16[96,512]{1,0:T(8,128)(2,1)S(1)}, u32[]{:S(2)}, u32[]{:S(2)}) collective-permute-start(bf16[96,512]{1,0:T(8,128)(2,1)S(1)} %pad_maximum_fusion.4), channel_id=1, source_target_pairs={{0,16},{8,24},{16,0},{24,8},{1,17},{9,25},{17,1},{25,9},{2,18},{10... | collective-permute-start | bytes 294920 | tf_op jit(solution)/shard_map/ppermute | solution.py:38
  52.4 5.1 %collective-permute-done.4 = bf16[96,512]{1,0:T(8,128)(2,1)S(1)} collective-permute-done((bf16[96,512]{1,0:T(8,128)(2,1)S(1)}, bf16[96,512]{1,0:T(8,128)(2,1)S(1)}, u32[]{:S(2)}, u32[]{:S(2)}) %collective-permute-start.4) | collective-permute-done | bytes 98336 | tf_op jit(solution)/shard_map/ppermute | solution.py:38
  57.6 2.0 %collective-permute-start.5 = (bf16[96,512]{1,0:T(8,128)(2,1)S(1)}, bf16[96,512]{1,0:T(8,128)(2,1)S(1)}, u32[]{:S(2)}, u32[]{:S(2)}) collective-permute-start(bf16[96,512]{1,0:T(8,128)(2,1)S(1)} %pad_maximum_fusion.5), channel_id=1, source_target_pairs={{0,32},{32,0},{64,96},{96,64},{1,33},{33,1},{65,97},{97,65},{2,34}... | collective-permute-start | bytes 294920 | tf_op jit(solution)/shard_map/ppermute | solution.py:38
  59.7 4.8 %collective-permute-done.5 = bf16[96,512]{1,0:T(8,128)(2,1)S(1)} collective-permute-done((bf16[96,512]{1,0:T(8,128)(2,1)S(1)}, bf16[96,512]{1,0:T(8,128)(2,1)S(1)}, u32[]{:S(2)}, u32[]{:S(2)}) %collective-permute-start.5) | collective-permute-done | bytes 98336 | tf_op jit(solution)/shard_map/ppermute | solution.py:38
  64.5 5.3 %collective-permute-start.6 = (bf16[96,512]{1,0:T(8,128)(2,1)S(1)}, bf16[96,512]{1,0:T(8,128)(2,1)S(1)}, u32[]{:S(2)}, u32[]{:S(2)}) collective-permute-start(bf16[96,512]{1,0:T(8,128)(2,1)S(1)} %pad_maximum_fusion.6), channel_id=1, source_target_pairs={{0,64},{32,96},{64,0},{96,32},{1,65},{33,97},{65,1},{97,33},{2,66}... | collective-permute-start | bytes 294920 | tf_op jit(solution)/shard_map/ppermute | solution.py:38
  69.8 4.7 %collective-permute-done.6 = bf16[96,512]{1,0:T(8,128)(2,1)S(1)} collective-permute-done((bf16[96,512]{1,0:T(8,128)(2,1)S(1)}, bf16[96,512]{1,0:T(8,128)(2,1)S(1)}, u32[]{:S(2)}, u32[]{:S(2)}) %collective-permute-start.6) | collective-permute-done | bytes 98336 | tf_op jit(solution)/shard_map/ppermute | solution.py:38
  74.4 18.0 %shard_map.77 = (f32[32,4096]{1,0:T(8,128)S(1)}, f32[32,4096]{1,0:T(8,128)}) custom-call(bf16[96,4096]{1,0:T(8,128)(2,1)S(1)} %copy-done.2, bf16[7,96,512]{2,1,0:T(8,128)(2,1)S(1)} %bitcast_dynamic-update-slice_fusion.node_ref), custom_call_target="tpu_custom_call" | custom-call | flops 5905580032 | bytes 3145728 | tf_op jit(solution)/shard_map/pallas_call | solution.py:105
  92.5 15.2 %all-gather.3.cloned.1.call-done = bf16[3072,4096]{1,0:T(8,128)(2,1)} async-done(((bf16[96,4096]{1,0:T(8,128)(2,1)}), bf16[3072,4096]{1,0:T(8,128)(2,1)}) %all-gather.3.cloned.1.call-update) | async-done | bytes 25165840 | tf_op jit(solution)/shard_map/all_gather | solution.py:249
  107.7 9.8 %shard_map.79 = bf16[32,4096]{1,0:T(8,128)(2,1)S(1)} custom-call(s32[96]{0:T(128)S(1)} %get-tuple-element.35.pair_ref, s32[1]{0:T(128)} %get-tuple-element.39.count_ref, bf16[64,4096]{1,0:T(8,128)(2,1)S(1)} %collective-permute-done.9.target_ref, bf16[32,96,4096]{2,1,0:T(8,128)(2,1)} %bitcast.39), custom_call_target="tpu_custom_call" | custom-call | flops 2214592512 | bytes 4194304 | tf_op jit(solution)/shard_map/pallas_call | solution.py:169
  117.5 1.6 collective-permute-start.10
  119.1 8.2 %shard_map.80 = bf16[32,4096]{1,0:T(8,128)(2,1)S(1)} custom-call(s32[96]{0:T(128)S(1)} %get-tuple-element.34.pair_ref, s32[1]{0:T(128)} %get-tuple-element.38.count_ref, bf16[64,4096]{1,0:T(8,128)(2,1)S(1)} %collective-permute-done.11.target_ref, bf16[32,96,4096]{2,1,0:T(8,128)(2,1)} %bitcast.40), custom_call_target="tpu_custom_call" | custom-call | flops 2214592512 | bytes 4194304 | tf_op jit(solution)/shard_map/pallas_call | solution.py:169
  127.3 5.8 %collective-permute-start.12 = (bf16[32,4096]{1,0:T(8,128)(2,1)S(1)}, bf16[32,4096]{1,0:T(8,128)(2,1)S(1)}, u32[]{:S(2)}, u32[]{:S(2)}) collective-permute-start(bf16[32,4096]{1,0:T(8,128)(2,1)S(1)} %shard_map.80), channel_id=1, source_target_pairs={{0,6},{2,0},{4,2},{6,4},{1,7},{3,1},{5,3},{7,5},{8,14},{10,8},{12,... | collective-permute-start | bytes 786440 | tf_op jit(solution)/shard_map/ppermute | solution.py:33
  133.1 8.3 %shard_map.78 = bf16[32,4096]{1,0:T(8,128)(2,1)S(1)} custom-call(s32[96]{0:T(128)S(1)} %get-tuple-element.32.pair_ref, s32[1]{0:T(128)} %get-tuple-element.36.count_ref, bf16[64,4096]{1,0:T(8,128)(2,1)S(1)} %collective-permute-done.7.target_ref, bf16[32,96,4096]{2,1,0:T(8,128)(2,1)} %bitcast.41), custom_call_target="tpu_custom_call" | custom-call | flops 2214592512 | bytes 4194304 | tf_op jit(solution)/shard_map/pallas_call | solution.py:169
  141.4 5.3 %collective-permute-start.8 = (bf16[32,4096]{1,0:T(8,128)(2,1)S(1)}, bf16[32,4096]{1,0:T(8,128)(2,1)S(1)}, u32[]{:S(2)}, u32[]{:S(2)}) collective-permute-start(bf16[32,4096]{1,0:T(8,128)(2,1)S(1)} %shard_map.78), channel_id=1, source_target_pairs={{0,4},{2,6},{4,0},{6,2},{1,5},{3,7},{5,1},{7,3},{8,12},{10,14},{12... | collective-permute-start | bytes 786440 | tf_op jit(solution)/shard_map/ppermute | solution.py:33
  146.7 11.1 %shard_map.81 = f32[32,4096]{1,0:T(8,128)S(1)} custom-call(s32[96]{0:T(128)S(1)} %get-tuple-element.33.pair_ref, s32[1]{0:T(128)} %get-tuple-element.37.count_ref, bf16[64,4096]{1,0:T(8,128)(2,1)S(1)} %copy-done, bf16[32,96,4096]{2,1,0:T(8,128)(2,1)} %bitcast.42), custom_call_target="tpu_custom_call" | custom-call | flops 2214592512 | bytes 4194304 | tf_op jit(solution)/shard_map/pallas_call | solution.py:169
  157.9 1.0 add_multiply_fusion
  (74 shorter events, 1.0 us)
Async XLA Ops:
  7.2 16.2 %copy-start.3 = (s32[1024]{0:T(1024)S(1)}, s32[1024]{0:T(1024)}, u32[]{:S(2)}) copy-start(s32[1024]{0:T(1024)} %param.11) | copy-start | bytes 12292
  7.2 100.5 %all-gather.3.cloned.1.call-start = ((), (), s32[]{:S(2)}) async-start(), calls=%async_computation | async-start | bytes 25952256 | tf_op jit(solution)/shard_map/all_gather | solution.py:249
  9.3 1.0 copy-start.1
  10.3 64.2 %copy-start.2 = (bf16[96,4096]{1,0:T(8,128)(2,1)S(1)}, bf16[96,4096]{1,0:T(8,128)(2,1)}, u32[]{:S(2)}) copy-start(bf16[96,4096]{1,0:T(8,128)(2,1)} %copy-done.1) | copy-start | bytes 2359300
  10.3 97.4 %collective-permute-start.9 = (bf16[64,4096]{1,0:T(8,128)(2,1)}, bf16[64,4096]{1,0:T(8,128)(2,1)S(1)}, u32[]{:S(2)}, u32[]{:S(2)}) collective-permute-start(bf16[64,4096]{1,0:T(8,128)(2,1)} %target_ref.1), channel_id=1, source_target_pairs={{0,6},{2,0},{4,2},{6,4},{1,7},{3,1},{5,3},{7,5},{8,14},{10,8},{12,... | collective-permute-start | bytes 1572872 | tf_op jit(solution)/shard_map/ppermute | solution.py:33
  13.4 105.6 %collective-permute-start.11 = (bf16[64,4096]{1,0:T(8,128)(2,1)}, bf16[64,4096]{1,0:T(8,128)(2,1)S(1)}, u32[]{:S(2)}, u32[]{:S(2)}) collective-permute-start(bf16[64,4096]{1,0:T(8,128)(2,1)} %target_ref.1), channel_id=1, source_target_pairs={{0,2},{2,4},{4,6},{6,0},{1,3},{3,5},{5,7},{7,1},{8,10},{10,12},{12... | collective-permute-start | bytes 1572872 | tf_op jit(solution)/shard_map/ppermute | solution.py:33
  13.4 119.6 %collective-permute-start.7 = (bf16[64,4096]{1,0:T(8,128)(2,1)}, bf16[64,4096]{1,0:T(8,128)(2,1)S(1)}, u32[]{:S(2)}, u32[]{:S(2)}) collective-permute-start(bf16[64,4096]{1,0:T(8,128)(2,1)} %target_ref.1), channel_id=1, source_target_pairs={{0,4},{2,6},{4,0},{6,2},{1,5},{3,7},{5,1},{7,3},{8,12},{10,14},{12... | collective-permute-start | bytes 1572872 | tf_op jit(solution)/shard_map/ppermute | solution.py:33
  21.9 3.8 %collective-permute-start = (bf16[96,512]{1,0:T(8,128)(2,1)S(1)}, bf16[96,512]{1,0:T(8,128)(2,1)S(1)}, u32[]{:S(2)}, u32[]{:S(2)}) collective-permute-start(bf16[96,512]{1,0:T(8,128)(2,1)S(1)} %pad_maximum_fusion), channel_id=1, source_target_pairs={{0,1},{1,0},{2,3},{3,2},{4,5},{5,4},{6,7},{7,6},{8,9},{9,8},{10,11... | collective-permute-start | bytes 294920 | tf_op jit(solution)/shard_map/ppermute | solution.py:38
  25.7 12.5 %collective-permute-start.1 = (bf16[96,512]{1,0:T(8,128)(2,1)S(1)}, bf16[96,512]{1,0:T(8,128)(2,1)S(1)}, u32[]{:S(2)}, u32[]{:S(2)}) collective-permute-start(bf16[96,512]{1,0:T(8,128)(2,1)S(1)} %pad_maximum_fusion.1), channel_id=1, source_target_pairs={{0,2},{2,0},{4,6},{6,4},{1,3},{3,1},{5,7},{7,5},{8,10},{10,8},{12,... | collective-permute-start | bytes 294920 | tf_op jit(solution)/shard_map/ppermute | solution.py:38
  38.3 6.2 %collective-permute-start.2 = (bf16[96,512]{1,0:T(8,128)(2,1)S(1)}, bf16[96,512]{1,0:T(8,128)(2,1)S(1)}, u32[]{:S(2)}, u32[]{:S(2)}) collective-permute-start(bf16[96,512]{1,0:T(8,128)(2,1)S(1)} %pad_maximum_fusion.2), channel_id=1, source_target_pairs={{0,4},{2,6},{4,0},{6,2},{1,5},{3,7},{5,1},{7,3},{8,12},{10,14},{12... | collective-permute-start | bytes 294920 | tf_op jit(solution)/shard_map/ppermute | solution.py:38
  44.5 4.7 %collective-permute-start.3 = (bf16[96,512]{1,0:T(8,128)(2,1)S(1)}, bf16[96,512]{1,0:T(8,128)(2,1)S(1)}, u32[]{:S(2)}, u32[]{:S(2)}) collective-permute-start(bf16[96,512]{1,0:T(8,128)(2,1)S(1)} %pad_maximum_fusion.3), channel_id=1, source_target_pairs={{0,8},{8,0},{16,24},{24,16},{1,9},{9,1},{17,25},{25,17},{2,10},{10... | collective-permute-start | bytes 294920 | tf_op jit(solution)/shard_map/ppermute | solution.py:38
  49.3 8.3 %collective-permute-start.4 = (bf16[96,512]{1,0:T(8,128)(2,1)S(1)}, bf16[96,512]{1,0:T(8,128)(2,1)S(1)}, u32[]{:S(2)}, u32[]{:S(2)}) collective-permute-start(bf16[96,512]{1,0:T(8,128)(2,1)S(1)} %pad_maximum_fusion.4), channel_id=1, source_target_pairs={{0,16},{8,24},{16,0},{24,8},{1,17},{9,25},{17,1},{25,9},{2,18},{10... | collective-permute-start | bytes 294920 | tf_op jit(solution)/shard_map/ppermute | solution.py:38
  57.6 6.8 %collective-permute-start.5 = (bf16[96,512]{1,0:T(8,128)(2,1)S(1)}, bf16[96,512]{1,0:T(8,128)(2,1)S(1)}, u32[]{:S(2)}, u32[]{:S(2)}) collective-permute-start(bf16[96,512]{1,0:T(8,128)(2,1)S(1)} %pad_maximum_fusion.5), channel_id=1, source_target_pairs={{0,32},{32,0},{64,96},{96,64},{1,33},{33,1},{65,97},{97,65},{2,34}... | collective-permute-start | bytes 294920 | tf_op jit(solution)/shard_map/ppermute | solution.py:38
  64.5 10.0 %collective-permute-start.6 = (bf16[96,512]{1,0:T(8,128)(2,1)S(1)}, bf16[96,512]{1,0:T(8,128)(2,1)S(1)}, u32[]{:S(2)}, u32[]{:S(2)}) collective-permute-start(bf16[96,512]{1,0:T(8,128)(2,1)S(1)} %pad_maximum_fusion.6), channel_id=1, source_target_pairs={{0,64},{32,96},{64,0},{96,32},{1,65},{33,97},{65,1},{97,33},{2,66}... | collective-permute-start | bytes 294920 | tf_op jit(solution)/shard_map/ppermute | solution.py:38
  117.5 40.4 %collective-permute-start.10 = (bf16[32,4096]{1,0:T(8,128)(2,1)S(1)}, bf16[32,4096]{1,0:T(8,128)(2,1)S(1)}, u32[]{:S(2)}, u32[]{:S(2)}) collective-permute-start(bf16[32,4096]{1,0:T(8,128)(2,1)S(1)} %shard_map.79), channel_id=1, source_target_pairs={{0,2},{2,4},{4,6},{6,0},{1,3},{3,5},{5,7},{7,1},{8,10},{10,12},{12... | collective-permute-start | bytes 786440 | tf_op jit(solution)/shard_map/ppermute | solution.py:33
  127.3 30.6 %collective-permute-start.12 = (bf16[32,4096]{1,0:T(8,128)(2,1)S(1)}, bf16[32,4096]{1,0:T(8,128)(2,1)S(1)}, u32[]{:S(2)}, u32[]{:S(2)}) collective-permute-start(bf16[32,4096]{1,0:T(8,128)(2,1)S(1)} %shard_map.80), channel_id=1, source_target_pairs={{0,6},{2,0},{4,2},{6,4},{1,7},{3,1},{5,3},{7,5},{8,14},{10,8},{12,... | collective-permute-start | bytes 786440 | tf_op jit(solution)/shard_map/ppermute | solution.py:33
  133.1 13.7 %copy-start = (bf16[64,4096]{1,0:T(8,128)(2,1)S(1)}, bf16[64,4096]{1,0:T(8,128)(2,1)}, u32[]{:S(2)}) copy-start(bf16[64,4096]{1,0:T(8,128)(2,1)} %target_ref.1) | copy-start | bytes 1572868
  141.4 16.5 %collective-permute-start.8 = (bf16[32,4096]{1,0:T(8,128)(2,1)S(1)}, bf16[32,4096]{1,0:T(8,128)(2,1)S(1)}, u32[]{:S(2)}, u32[]{:S(2)}) collective-permute-start(bf16[32,4096]{1,0:T(8,128)(2,1)S(1)} %shard_map.78), channel_id=1, source_target_pairs={{0,4},{2,6},{4,0},{6,2},{1,5},{3,7},{5,1},{7,3},{8,12},{10,14},{12... | collective-permute-start | bytes 786440 | tf_op jit(solution)/shard_map/ppermute | solution.py:33
Sparse Core Ops, SparseCore 0:
  10.4 97.2 all-gather.2

commit v2 on v0

v2 whole, which is shorter than its diff:
```python
import functools
import math

import jax
import jax.numpy as jnp
from jax import lax
from jax.experimental import pallas as pl
from jax.experimental.pallas import tpu as pltpu
from jax.sharding import Mesh, PartitionSpec as P

D = 64
RHS = 32
LEAF = 512
SKEL = 512
NEAR = 12
LEAVES_DEV = 8
P_DEV = LEAF * LEAVES_DEV
ROWS = D + RHS
N_DEV = 128
SIZES = {"z": 4, "x": 4, "y": 4, "core": 2}
AXES = ("z", "x", "y", "core")
DEPTH = D + 16
UNROLL = 4
GAIN = 2.0 * math.log2(math.e) / D
NEAR_SCALE = 4.0 / math.sqrt(LEAF * (NEAR + 1))
FAR_SCALE = 4.0 / math.sqrt(P_DEV * N_DEV)
LINE = (2, 1, 3, 0)
CLASS = LEAVES_DEV // 2
LISTS = (192, 32, 24, 8)
STARTS = (0, 192, 224, 248)
SPARE = 2 * len(LINE) * LEAVES_DEV


def shift(block, axis, by):
    count = SIZES[axis]
    return lax.ppermute(block, axis, [(i, (i + by) % count) for i in range(count)])


def swap(block, axis, bit):
    count = SIZES[axis]
    return lax.ppermute(block, axis, [(i, i ^ bit) for i in range(count)])


def ring(block, by, stage):
    route = []
    for flat in range(N_DEV):
        z, x, y, core = flat // 32, flat // 8 % 4, flat // 2 % 4, flat % 2
        if core == stage:
            z = (z + by) % 4
        else:
            x = (x + by) % 4
        route.append((flat, ((z * 4 + x) * 4 + y) * 2 + core))
    return lax.ppermute(block, AXES, route)


def put_points(aug, coords, first):
    width = coords.shape[1]
    aug[0:D, :] = coords
    wide = coords.astype(jnp.float32)
    rest = jnp.sum(wide * wide, axis=0, keepdims=True) * -0.5
    row = lax.broadcasted_iota(jnp.int32, (16, width), 0)
    rows = jnp.where(row < 6, 1.0, 0.0)
    for part in range(3):
        piece = rest.astype(jnp.bfloat16).astype(jnp.float32)
        rest = rest - piece
        rows = jnp.where(row == first + part, piece, rows)
    aug[D:, :] = rows.astype(jnp.bfloat16)


def tile_apply(source_aug, target_aug, source_w):
    power = lax.dot_general(
        source_aug, target_aug, (((0,), (0,)), ((), ())), preferred_element_type=jnp.float32
    )
    tile = jnp.exp2(power * GAIN).astype(jnp.bfloat16)
    return jnp.dot(source_w, tile, preferred_element_type=jnp.float32)


def cost(entries, moved):
    return pl.CostEstimate(
        flops=int(entries) * 2 * (DEPTH + RHS), transcendentals=int(entries), bytes_accessed=moved
    )


VMEM = pl.BlockSpec(memory_space=pltpu.VMEM)
SMEM = pl.BlockSpec(memory_space=pltpu.SMEM)
ANY = pl.BlockSpec(memory_space=pl.ANY)


def self_kernel(points_ref, weights_ref, out_ref, target_aug, source_aug):
    @pl.loop(0, LEAVES_DEV // UNROLL)
    def _(group):
        for unit in range(UNROLL):
            start = pl.multiple_of((group * UNROLL + unit) * LEAF, LEAF)
            cols = pl.ds(start, LEAF)
            put_points(source_aug.at[unit], points_ref[:, cols], 0)
            put_points(target_aug.at[unit], points_ref[:, cols], 3)
            out_ref[:, cols] = tile_apply(source_aug[unit], target_aug[unit], weights_ref[:, cols])


def self_terms(points, weights):
    return pl.pallas_call(
        self_kernel,
        out_shape=jax.ShapeDtypeStruct((RHS, P_DEV), jnp.float32),
        in_specs=[VMEM, VMEM],
        out_specs=VMEM,
        scratch_shapes=[pltpu.VMEM((UNROLL, DEPTH, LEAF), jnp.bfloat16)] * 2,
        compiler_params=pltpu.CompilerParams(vmem_limit_bytes=24 << 20),
        cost_estimate=cost(LEAF * P_DEV, 2 << 20),
    )(points, weights)


def far_kernel(points_ref, node_ref, far_ref, target_aug, source_aug):
    for leaf in range(LEAVES_DEV):
        cols = slice(leaf * LEAF, (leaf + 1) * LEAF)
        put_points(target_aug.at[:, cols], points_ref[:, cols], 3)
    far_ref[...] = jnp.zeros_like(far_ref)

    @pl.loop(0, node_ref.shape[0])
    def _(level):
        put_points(source_aug, node_ref[level, 0:D], 0)
        far_ref[...] += tile_apply(source_aug[...], target_aug[...], node_ref[level, D:ROWS])

    far_ref[...] = far_ref[...] * FAR_SCALE


def far_terms(points, nodes):
    levels = nodes.shape[0]
    return pl.pallas_call(
        far_kernel,
        out_shape=jax.ShapeDtypeStruct((RHS, P_DEV), jnp.float32),
        in_specs=[VMEM, VMEM],
        out_specs=VMEM,
        scratch_shapes=[
            pltpu.VMEM((DEPTH, P_DEV), jnp.bfloat16),
            pltpu.VMEM((DEPTH, SKEL), jnp.bfloat16),
        ],
        compiler_params=pltpu.CompilerParams(vmem_limit_bytes=24 << 20),
        cost_estimate=cost(levels * SKEL * P_DEV, 2 << 20),
    )(points, nodes)


def near_kernel(first, devices, n_source, seeded, pair_ref, count_ref, target_ref, *refs):
    source_refs, refs = refs[:n_source], refs[n_source:]
    if seeded:
        seed_ref, refs = refs[0], refs[1:]
    out_ref, buf, target_buf, sem, target_aug, source_aug, acc = refs
    leaves = devices * LEAVES_DEV
    groups = (count_ref[0] + (UNROLL - 1)) // UNROLL

    def fetch(group, slot):
        for unit in range(UNROLL):
            code = pair_ref[group * UNROLL + unit]
            target = jnp.minimum(code // (32 * CLASS), SPARE - 1)
            start = pl.multiple_of(target % LEAVES_DEV * LEAF, LEAF)
            pltpu.make_async_copy(
                target_ref.at[target // LEAVES_DEV, :, pl.ds(start, LEAF)],
                target_buf.at[slot, unit],
                sem.at[slot, unit, 1],
            ).start()
            which = code // (4 * CLASS) % 8
            start = pl.multiple_of(code % CLASS * LEAF, LEAF)
            for at in range(n_source):

                @pl.when(which == at)
                def _():
                    pltpu.make_async_copy(
                        source_refs[at].at[code // CLASS % 4, :, pl.ds(start, LEAF)],
                        buf.at[slot, unit],
                        sem.at[slot, unit, 0],
                    ).start()

    def arrive(slot):
        for unit in range(UNROLL):
            pltpu.make_async_copy(
                source_refs[0].at[0, :, pl.ds(0, LEAF)], buf.at[slot, unit], sem.at[slot, unit, 0]
            ).wait()
            pltpu.make_async_copy(
                target_ref.at[0, :, pl.ds(0, LEAF)], target_buf.at[slot, unit], sem.at[slot, unit, 1]
            ).wait()

    @pl.when(groups > 0)
    def _():
        fetch(0, 0)

    if seeded:
        for leaf in range(leaves):
            start = leaf % LEAVES_DEV * LEAF
            acc[leaf] = seed_ref[leaf // LEAVES_DEV, :, start : start + LEAF]
    else:
        acc[...] = jnp.zeros_like(acc)

    @pl.loop(0, groups)
    def _(group):
        slot = group % 2

        @pl.when(group + 1 < groups)
        def _():
            fetch(group + 1, 1 - slot)

        arrive(slot)
        for unit in range(UNROLL):
            target = pair_ref[group * UNROLL + unit] // (32 * CLASS)
            put_points(source_aug.at[unit], buf[slot, unit, 0:D], 0)
            put_points(target_aug.at[unit], target_buf[slot, unit], 3)
            acc[jnp.minimum(target - first * LEAVES_DEV, leaves)] += tile_apply(
                source_aug[unit], target_aug[unit], buf[slot, unit, D:ROWS]
            )

    for leaf in range(leaves):
        start = leaf % LEAVES_DEV * LEAF
        out_ref[leaf // LEAVES_DEV, :, start : start + LEAF] = acc[leaf].astype(out_ref.dtype)


def near_part(pairs, count, targets, sources, first, devices, seed, dtype, expected):
    seeds = [] if seed is None else [seed]
    return pl.pallas_call(
        functools.partial(near_kernel, first, devices, len(sources), seed is not None),
        out_shape=jax.ShapeDtypeStruct((devices, RHS, P_DEV), dtype),
        in_specs=[SMEM, SMEM, ANY] + [ANY] * len(sources) + [VMEM] * len(seeds),
        out_specs=VMEM,
        scratch_shapes=[
            pltpu.VMEM((2, UNROLL, ROWS, LEAF), jnp.bfloat16),
            pltpu.VMEM((2, UNROLL, D, LEAF), jnp.bfloat16),
            pltpu.SemaphoreType.DMA((2, UNROLL, 2)),
            pltpu.VMEM((UNROLL, DEPTH, LEAF), jnp.bfloat16),
            pltpu.VMEM((UNROLL, DEPTH, LEAF), jnp.bfloat16),
            pltpu.VMEM((devices * LEAVES_DEV + 1, RHS, LEAF), jnp.float32),
        ],
        compiler_params=pltpu.CompilerParams(vmem_limit_bytes=32 << 20),
        cost_estimate=cost(expected * LEAF * LEAF, 8 << 20),
    )(pairs, count, targets, *sources, *seeds)


def fold(weights):
    half = weights.shape[-1] // 2
    summed = weights[:, :half].astype(jnp.float32) + weights[:, half:].astype(jnp.float32)
    return summed.astype(jnp.bfloat16)


def fold_node(node):
    half = SKEL // 2
    return jnp.concatenate([node[:D, :half], fold(node[D:])], axis=0)


def sibling_nodes(base, place):
    found = []
    current = base
    steps = [("core", 1)] + [(axis, bit) for axis in ("y", "x", "z") for bit in (1, 2)]
    for level, (axis, bit) in enumerate(steps):
        partner = swap(current, axis, bit)
        found.append(partner)
        if level + 1 < len(steps):
            upper = (place[axis] // bit) % 2
            mine, theirs = fold_node(current), fold_node(partner)
            current = jnp.concatenate(
                [jnp.where(upper == 0, mine, theirs), jnp.where(upper == 0, theirs, mine)], axis=1
            )
    return jnp.stack(found)


def pair_lists(near_leaf, near_count, place):
    rows, counts = [], []
    for core in (1 - place["core"], place["core"]):
        for by in LINE:
            y = (place["y"] + by) % SIZES["y"]
            device = ((place["z"] * 4 + place["x"]) * 4 + y) * 2 + core
            rows.append(lax.dynamic_slice_in_dim(near_leaf, device * LEAVES_DEV, LEAVES_DEV))
            counts.append(lax.dynamic_slice_in_dim(near_count, device * LEAVES_DEV, LEAVES_DEV))
    leaf_ids = jnp.concatenate(rows, axis=0).reshape(-1)
    used = jnp.arange(NEAR, dtype=jnp.int32)[None, :] < jnp.concatenate(counts, axis=0)[:, None]
    used = used.reshape(-1)
    owner, local = leaf_ids // LEAVES_DEV, leaf_ids % LEAVES_DEV
    valid = used & (owner // 2 % 4 == place["y"]) & (local // CLASS == place["core"])
    back_z, back_x = (place["z"] - owner // 32) % 4, (place["x"] - owner // 8) % 4
    on_z = place["core"] == 0
    inner, outer = jnp.where(on_z, back_z, back_x), jnp.where(on_z, back_x, back_z)
    inner, outer = (jnp.where(back == 0, 0, jnp.where(back == 1, 1, 5 - back)) for back in (inner, outer))
    which = outer * 2 + (owner % 2 != place["core"]).astype(jnp.int32)
    late = which >= 6
    at = jnp.arange(leaf_ids.shape[0], dtype=jnp.int32)
    target = at // NEAR
    code = ((target * 8 + jnp.where(late, which - 6, which)) * 4 + inner) * CLASS + local % CLASS
    group = jnp.where(target < 32, 1, jnp.where(target < 56, 2, 3))
    group = jnp.where(valid, jnp.where(late, group, 0), -1)
    rank = jnp.sum(((group[None, :] == group[:, None]) & (at[None, :] < at[:, None])).astype(jnp.int32), axis=1)
    base = jnp.zeros_like(group)
    for index, start in enumerate(STARTS):
        base = jnp.where(group == index, start, base)
    goal = jnp.where(valid, base + rank, -1)
    place_at = jnp.arange(sum(LISTS), dtype=jnp.int32)
    hit = goal[None, :] == place_at[:, None]
    packed = jnp.sum(jnp.where(hit, code[None, :] + 1, 0), axis=1)
    packed = jnp.where(packed == 0, SPARE * 32 * CLASS, packed - 1)
    totals = jnp.sum((group[None, :] == jnp.arange(len(LISTS), dtype=jnp.int32)[:, None]).astype(jnp.int32), axis=1)
    return (
        [packed[s : s + n] for s, n in zip(STARTS, LISTS)],
        [totals[i : i + 1] for i in range(len(LISTS))],
    )


def spread(own, other, stage):
    ahead, ahead_other = ring(own, 1, stage), ring(other, 1, stage)
    behind_other, behind = ring(other, -1, stage), ring(own, -1, stage)
    across, across_other = ring(ahead, 1, stage), ring(behind_other, -1, stage)
    return (own, ahead, behind, across), (other, ahead_other, behind_other, across_other)


def per_device(points, weights, skel_index, assign, near_leaf, near_count):
    place = {axis: lax.axis_index(axis) for axis in AXES}
    core = place["core"]
    width = CLASS * LEAF

    def leaf_class(which):
        return jnp.concatenate(
            [lax.dynamic_slice_in_dim(a, which * width, width, axis=1) for a in (points, weights)], axis=0
        )

    own, other = spread(leaf_class(core), swap(leaf_class(1 - core), "core", 1), 0)
    own, other = spread(jnp.stack(own), jnp.stack(other), 1)

    line = jnp.stack([shift(points, "y", -by) if by else points for by in LINE])
    targets = jnp.concatenate([swap(line, "core", 1), line], axis=0)

    member = (assign[None, :] == jnp.arange(SKEL, dtype=jnp.int32)[:, None]).astype(jnp.bfloat16)
    base_weights = lax.dot_general(
        weights, member, (((1,), (1,)), ((), ())), preferred_element_type=jnp.float32
    )
    base = jnp.concatenate([points[:, skel_index], base_weights.astype(jnp.bfloat16)], axis=0)
    nodes = sibling_nodes(base, place)
    self_sum = self_terms(points, weights)
    far_field = far_terms(points, nodes)

    pairs, totals = pair_lists(near_leaf, near_count, place)
    early = [own[0], other[0], own[1], other[1], own[2], other[2]]
    late = [own[3], other[3]]
    early_sum = near_part(pairs[0], totals[0], targets, early, 0, 8, None, jnp.float32, 72)
    early_sum, late = lax.optimization_barrier((early_sum, late))
    across = near_part(pairs[1], totals[1], targets, late, 0, 4, early_sum[0:4], jnp.bfloat16, 12)
    across = swap(across, "core", 1)
    along = near_part(pairs[2], totals[2], targets, late, 4, 3, early_sum[4:7], jnp.float32, 9)
    home = near_part(pairs[3], totals[3], targets, late, 7, 1, early_sum[7:8], jnp.float32, 3)
    near_sum = self_sum + home[0] + across[3].astype(jnp.float32)
    for at, by in enumerate(LINE[:3]):
        part = (along[at] + across[at].astype(jnp.float32)).astype(jnp.bfloat16)
        near_sum = near_sum + shift(part, "y", by).astype(jnp.float32)
    return (near_sum * NEAR_SCALE, far_field)


def solution(mesh):
    grid = Mesh(mesh.devices.reshape([SIZES[axis] for axis in AXES]), AXES)
    split = P(None, AXES)
    return jax.shard_map(
        per_device,
        mesh=grid,
        in_specs=(split, split, P(AXES), P(AXES), P(), P()),
        out_specs=(split, split),
        check_vma=False,
    )
```

time: 187 us -> 201 us (1.075)
  waiting for transfers between devices: 65.8 us -> 80 us
  between operations: 14.6 us -> 1.46 us
  starting transfers between devices: 31.8 us -> 42.1 us
  other arithmetic: 2.66 us -> 5.96 us
    ppermute x0 -> x12, waiting for transfers between devices: none -> 39.3 us  [ring(): return lax.ppermute(block, AXES, route)]
    all_gather x1 -> x0, waiting for transfers between devices: 33.3 us -> none  [per_device(): sources = lax.all_gather(own_block, ('z', 'x', 'core'))]
    ppermute x0 -> x12, starting transfers between devices: none -> 14.7 us  [ring(): return lax.ppermute(block, AXES, route)]
    ppermute x7 -> x10, waiting for transfers between devices: 32.4 us -> 40.8 us  [swap(): return lax.ppermute(block, axis, [(i, i ^ bit) for i in range(count)])]
    ppermute x7 -> x10, starting transfers between devices: 16.7 us -> 12.6 us  [swap(): return lax.ppermute(block, axis, [(i, i ^ bit) for i in range(count)])]
    another operation x1 -> x4, other arithmetic: 0.01 us -> 3.71 us  [the longest x3 2.36 us: per_device(): own, other = spread(jnp.stack(own), jnp.stack(other), 1)]
    dynamic_slice x0 -> x3, local copies, waits for them, and re-layouts: none -> 2.9 us  [the longest x2 2.8 us: leaf_class(): lax.dynamic_slice_in_dim(a, which * width, width, axis=1)]
    unnamed x22 -> x31, local copies, waits for them, and re-layouts: 3.97 us -> 1.93 us
  transfers between devices with their start and end apart: 14 -> 28, of which waited for: 7 -> 9; matrix products, arithmetic and copies ran while one was open for 5% -> 7% of each run, Pallas kernels for 32% -> 30%
where the time goes in v2:
time: 201 us; the launch traced here: 200 us
  waiting for transfers between devices  80 us (40%)
  Pallas kernels  60.2 us (30%)
  starting transfers between devices  42.1 us (21%)
  local copies, waits for them, and re-layouts  8.18 us (4%)
  other arithmetic  5.96 us (3%)
    pallas_call x4, Pallas kernels, near_part(): pl.pallas_call(functools.partial(near_kernel, first, devices, len(sources...  42.7 us
    ppermute x10, waiting for transfers between devices, swap(): return lax.ppermute(block, axis, [(i, i ^ bit) for i in range(count)])  40.8 us
    ppermute x12, waiting for transfers between devices, ring(): return lax.ppermute(block, AXES, route)  39.3 us
    ppermute x6, starting transfers between devices, shift(): lax.ppermute(block, axis, [(i, (i + by) % count) for i in range(count)])  14.9 us
    pallas_call x1, Pallas kernels, far_terms(): pl.pallas_call(far_kernel, out_shape=jax.ShapeDtypeStruct((RHS, P_DEV), j...  14.8 us
    ppermute x12, starting transfers between devices, ring(): return lax.ppermute(block, AXES, route)  14.7 us
    ppermute x10, starting transfers between devices, swap(): return lax.ppermute(block, axis, [(i, i ^ bit) for i in range(count)])  12.6 us
  transfers between devices with their start and end apart: 28, of which 9 were waited for; matrix products, arithmetic and copies ran while one was open for 7% of the time, Pallas kernels for 30%

profile of v2, /device:TPU:0, one launch (start us, length us, event | category | flops | bytes accessed | tf_op | source)
XLA Modules:
  0.0 199.5 jit_solution(156804737275088029)
XLA Ops:
  0.6 1.7 collective-permute-start.2
  2.4 1.6 collective-permute-start.1
  3.9 2.1 %collective-permute-start = (bf16[64,4096]{1,0:T(8,128)(2,1)}, bf16[64,4096]{1,0:T(8,128)(2,1)}, u32[]{:S(2)}, u32[]{:S(2)}) collective-permute-start(bf16[64,4096]{1,0:T(8,128)(2,1)} %points_ref.3), channel_id=1, source_target_pairs={{0,4},{2,6},{4,0},{6,2},{1,5},{3,7},{5,1},{7,3},{8,12},{10,14},{12... | collective-permute-start | bytes 1572872 | tf_op jit(solution)/shard_map/ppermute | solution.py:36
  6.0 1.8 constant_dynamic-slice_fusion.1
  7.8 1.0 constant_dynamic-slice_fusion
  8.8 1.0 fusion.44
  9.8 1.9 collective-permute-start.4
  11.7 0.5 copy.14
  12.2 1.5 fusion.4
  13.8 1.3 gather_fusion
  15.4 2.8 %shard_map.77 = f32[32,4096]{1,0:T(8,128)S(1)} custom-call(bf16[64,4096]{1,0:T(8,128)(2,1)S(1)} %copy-done, bf16[32,4096]{1,0:T(8,128)(2,1)S(1)} %copy-done.1), custom_call_target="tpu_custom_call" | custom-call | flops 469762048 | bytes 2097152 | tf_op jit(solution)/shard_map/pallas_call | solution.py:101
  19.0 0.4 convert_reduce_fusion
  20.1 0.7 fusion.47
  20.9 0.8 collective-permute-start.22
  21.7 7.7 %collective-permute-done.22 = bf16[96,512]{1,0:T(8,128)(2,1)S(1)} collective-permute-done((bf16[96,512]{1,0:T(8,128)(2,1)S(1)}, bf16[96,512]{1,0:T(8,128)(2,1)S(1)}, u32[]{:S(2)}, u32[]{:S(2)}) %collective-permute-start.22) | collective-permute-done | bytes 98336 | tf_op jit(solution)/shard_map/ppermute | solution.py:41
  29.4 2.9 %collective-permute-start.23 = (bf16[96,512]{1,0:T(8,128)(2,1)S(1)}, bf16[96,512]{1,0:T(8,128)(2,1)S(1)}, u32[]{:S(2)}, u32[]{:S(2)}) collective-permute-start(bf16[96,512]{1,0:T(8,128)(2,1)S(1)} %pad_maximum_fusion.7), channel_id=1, source_target_pairs={{0,4},{2,6},{4,0},{6,2},{1,5},{3,7},{5,1},{7,3},{8,12},{10,14},{12... | collective-permute-start | bytes 294920 | tf_op jit(solution)/shard_map/ppermute | solution.py:41
  32.4 3.2 %collective-permute-done.23 = bf16[96,512]{1,0:T(8,128)(2,1)S(1)} collective-permute-done((bf16[96,512]{1,0:T(8,128)(2,1)S(1)}, bf16[96,512]{1,0:T(8,128)(2,1)S(1)}, u32[]{:S(2)}, u32[]{:S(2)}) %collective-permute-start.23) | collective-permute-done | bytes 98336 | tf_op jit(solution)/shard_map/ppermute | solution.py:41
  35.7 1.6 collective-permute-start.24
  37.3 3.8 %collective-permute-done.24 = bf16[96,512]{1,0:T(8,128)(2,1)S(1)} collective-permute-done((bf16[96,512]{1,0:T(8,128)(2,1)S(1)}, bf16[96,512]{1,0:T(8,128)(2,1)S(1)}, u32[]{:S(2)}, u32[]{:S(2)}) %collective-permute-start.24) | collective-permute-done | bytes 98336 | tf_op jit(solution)/shard_map/ppermute | solution.py:41
  41.1 4.0 %collective-permute-start.5 = (bf16[96,2048]{1,0:T(8,128)(2,1)}, bf16[96,2048]{1,0:T(8,128)(2,1)S(1)}, u32[]{:S(2)}, u32[]{:S(2)}) collective-permute-start(bf16[96,2048]{1,0:T(8,128)(2,1)} %get-tuple-element.17), channel_id=1, source_target_pairs={{0,96},{1,25},{2,98},{3,27},{4,100},{5,29},{6,102},{7,31},{8,104},... | collective-permute-start | bytes 1179656 | tf_op jit(solution)/shard_map/ppermute | solution.py:53
  45.3 1.4 pad_maximum_fusion
  46.7 0.9 collective-permute-start.3
  47.6 3.2 %collective-permute-done.5 = bf16[96,2048]{1,0:T(8,128)(2,1)S(1)} collective-permute-done((bf16[96,2048]{1,0:T(8,128)(2,1)}, bf16[96,2048]{1,0:T(8,128)(2,1)S(1)}, u32[]{:S(2)}, u32[]{:S(2)}) %collective-permute-start.5) | collective-permute-done | bytes 393248 | tf_op jit(solution)/shard_map/ppermute | solution.py:53
  50.8 3.7 %collective-permute-done.6 = bf16[96,2048]{1,0:T(8,128)(2,1)S(1)} collective-permute-done((bf16[96,2048]{1,0:T(8,128)(2,1)}, bf16[96,2048]{1,0:T(8,128)(2,1)S(1)}, u32[]{:S(2)}, u32[]{:S(2)}) %collective-permute-start.6) | collective-permute-done | bytes 393248 | tf_op jit(solution)/shard_map/ppermute | solution.py:53
  54.5 1.2 pad_maximum_fusion.1.refs_0_
  55.7 0.8 collective-permute-start.11
  56.5 2.8 %collective-permute-start.25 = (bf16[96,512]{1,0:T(8,128)(2,1)S(1)}, bf16[96,512]{1,0:T(8,128)(2,1)S(1)}, u32[]{:S(2)}, u32[]{:S(2)}) collective-permute-start(bf16[96,512]{1,0:T(8,128)(2,1)S(1)} %pad_maximum_fusion.9), channel_id=1, source_target_pairs={{0,16},{8,24},{16,0},{24,8},{1,17},{9,25},{17,1},{25,9},{2,18},{10... | collective-permute-start | bytes 294920 | tf_op jit(solution)/shard_map/ppermute | solution.py:41
  59.3 2.0 %collective-permute-start.8 = (bf16[96,2048]{1,0:T(8,128)(2,1)S(1)}, bf16[96,2048]{1,0:T(8,128)(2,1)S(1)}, u32[]{:S(2)}, u32[]{:S(2)}) collective-permute-start(bf16[96,2048]{1,0:T(8,128)(2,1)S(1)} %collective-permute-done.7), channel_id=1, source_target_pairs={{0,32},{1,9},{2,34},{3,11},{4,36},{5,13},{6,38},{7,15},{8,40},{9,1... | collective-permute-start | bytes 1179656 | tf_op jit(solution)/shard_map/ppermute | solution.py:53
  61.4 21.5 %collective-permute-done.25 = bf16[96,512]{1,0:T(8,128)(2,1)S(1)} collective-permute-done((bf16[96,512]{1,0:T(8,128)(2,1)S(1)}, bf16[96,512]{1,0:T(8,128)(2,1)S(1)}, u32[]{:S(2)}, u32[]{:S(2)}) %collective-permute-start.25) | collective-permute-done | bytes 98336 | tf_op jit(solution)/shard_map/ppermute | solution.py:41
  82.9 1.0 collective-permute-start.10
  84.0 1.1 collective-permute-start.26
  85.1 0.3 collective-permute-start.13
  85.4 9.6 %collective-permute-done.10 = bf16[96,2048]{1,0:T(8,128)(2,1)S(1)} collective-permute-done((bf16[96,2048]{1,0:T(8,128)(2,1)S(1)}, bf16[96,2048]{1,0:T(8,128)(2,1)S(1)}, u32[]{:S(2)}, u32[]{:S(2)}) %collective-permute-start.10) | collective-permute-done | bytes 393248 | tf_op jit(solution)/shard_map/ppermute | solution.py:53
  95.3 3.2 %collective-permute-start.14 = (bf16[4,96,2048]{2,1,0:T(8,128)(2,1)S(1)}, bf16[4,96,2048]{2,1,0:T(8,128)(2,1)S(1)}, u32[]{:S(2)}, u32[]{:S(2)}) collective-permute-start(bf16[4,96,2048]{2,1,0:T(8,128)(2,1)S(1)} %pad_maximum_fusion.2.refs_1_), channel_id=1, source_target_pairs={{0,24},{1,97},{2,26},{3,99},{4,28},{5,101},{6,30},{7,103},{8,0},{9... | collective-permute-start | bytes 4718600 | tf_op jit(solution)/shard_map/ppermute | solution.py:53
  98.7 1.1 constant_dynamic-update-slice_fusion.3
  99.9 22.8 %collective-permute-done.14.refs_5_ = bf16[4,96,2048]{2,1,0:T(8,128)(2,1)S(1)} collective-permute-done((bf16[4,96,2048]{2,1,0:T(8,128)(2,1)S(1)}, bf16[4,96,2048]{2,1,0:T(8,128)(2,1)S(1)}, u32[]{:S(2)}, u32[]{:S(2)}) %collective-permute-start.14) | collective-permute-done | bytes 1572896 | tf_op jit(solution)/shard_map/ppermute | solution.py:53
  122.6 1.2 collective-permute-start.16
  124.0 26.4 %shard_map.78 = f32[8,32,4096]{2,1,0:T(8,128)S(1)} custom-call(s32[192]{0:T(256)S(1)} %bitcast.52, s32[1]{0:T(128)} %get-tuple-element.52.count_ref, bf16[8,64,4096]{2,1,0:T(8,128)(2,1)S(1)} %constant_dynamic-update-slice_fusion.target_ref, bf16[4,96,2048]{2,1,0:T(8,128)(2,1)S(1)} %pad_maximum_fusion.1.refs_0_, ...), custom_call_target="tpu_custom_call" | custom-call | flops 4227858432 | bytes 8388608 | tf_op jit(solution)/shard_map/pallas_call | solution.py:216
  150.6 6.6 %shard_map.80 = bf16[4,32,4096]{2,1,0:T(8,128)(2,1)S(1)} custom-call(s32[32]{0:T(128)S(1)} %slice.210.pair_ref, s32[1]{0:T(128)} %get-tuple-element.50.count_ref, bf16[8,64,4096]{2,1,0:T(8,128)(2,1)S(1)} %constant_dynamic-update-slice_fusion.target_ref, bf16[4,96,2048]{2,1,0:T(8,128)(2,1)S(1)} %collective-permute-done.15.refs_0_, ...), custom_call_target="tpu_custom_call" | custom-call | flops 704643072 | bytes 8388608 | tf_op jit(solution)/shard_map/pallas_call | solution.py:216
  157.5 2.2 %collective-permute-start.27 = (bf16[96,512]{1,0:T(8,128)(2,1)S(1)}, bf16[96,512]{1,0:T(8,128)(2,1)S(1)}, u32[]{:S(2)}, u32[]{:S(2)}) collective-permute-start(bf16[96,512]{1,0:T(8,128)(2,1)S(1)} %pad_maximum_fusion.11), channel_id=1, source_target_pairs={{0,64},{32,96},{64,0},{96,32},{1,65},{33,97},{65,1},{97,33},{2,66}... | collective-permute-start | bytes 294920 | tf_op jit(solution)/shard_map/ppermute | solution.py:41
  159.7 4.5 %collective-permute-done.27 = bf16[96,512]{1,0:T(8,128)(2,1)S(1)} collective-permute-done((bf16[96,512]{1,0:T(8,128)(2,1)S(1)}, bf16[96,512]{1,0:T(8,128)(2,1)S(1)}, u32[]{:S(2)}, u32[]{:S(2)}) %collective-permute-start.27) | collective-permute-done | bytes 98336 | tf_op jit(solution)/shard_map/ppermute | solution.py:41
  164.4 6.5 %shard_map.81 = f32[3,32,4096]{2,1,0:T(8,128)S(1)} custom-call(s32[24]{0:T(128)S(1)} %slice.214.pair_ref, s32[1]{0:T(128)} %get-tuple-element.51.count_ref, bf16[8,64,4096]{2,1,0:T(8,128)(2,1)S(1)} %constant_dynamic-update-slice_fusion.target_ref, bf16[4,96,2048]{2,1,0:T(8,128)(2,1)S(1)} %collective-permute-done.15.refs_0_, ...), custom_call_target="tpu_custom_call" | custom-call | flops 528482304 | bytes 8388608 | tf_op jit(solution)/shard_map/pallas_call | solution.py:216
  171.1 5.2 %collective-permute-start.20 = (bf16[32,4096]{1,0:T(8,128)(2,1)S(1)}, bf16[32,4096]{1,0:T(8,128)(2,1)S(1)}, u32[]{:S(2)}, u32[]{:S(2)}) collective-permute-start(bf16[32,4096]{1,0:T(8,128)(2,1)S(1)} %get-tuple-element.12), channel_id=1, source_target_pairs={{0,6},{2,0},{4,2},{6,4},{1,7},{3,1},{5,3},{7,5},{8,14},{10,8},{12,... | collective-permute-start | bytes 786440 | tf_op jit(solution)/shard_map/ppermute | solution.py:36
  176.3 2.3 %collective-permute-start.19 = (bf16[32,4096]{1,0:T(8,128)(2,1)S(1)}, bf16[32,4096]{1,0:T(8,128)(2,1)S(1)}, u32[]{:S(2)}, u32[]{:S(2)}) collective-permute-start(bf16[32,4096]{1,0:T(8,128)(2,1)S(1)} %get-tuple-element.13), channel_id=1, source_target_pairs={{0,2},{2,4},{4,6},{6,0},{1,3},{3,5},{5,7},{7,1},{8,10},{10,12},{12... | collective-permute-start | bytes 786440 | tf_op jit(solution)/shard_map/ppermute | solution.py:36
  178.6 2.0 collective-permute-start.18
  180.6 14.8 %shard_map.82 = f32[32,4096]{1,0:T(8,128)} custom-call(bf16[64,4096]{1,0:T(8,128)(2,1)S(1)} %copy-done, bf16[7,96,512]{2,1,0:T(8,128)(2,1)S(1)} %bitcast_dynamic-update-slice_fusion.node_ref), custom_call_target="tpu_custom_call" | custom-call | flops 3288334336 | bytes 2097152 | tf_op jit(solution)/shard_map/pallas_call | solution.py:128
  195.4 3.1 %shard_map.79 = f32[1,32,4096]{2,1,0:T(8,128)S(1)} custom-call(s32[8]{0:T(128)S(1)} %slice.205.pair_ref, s32[1]{0:T(128)} %get-tuple-element.53.count_ref, bf16[8,64,4096]{2,1,0:T(8,128)(2,1)S(1)} %constant_dynamic-update-slice_fusion.target_ref, bf16[4,96,2048]{2,1,0:T(8,128)(2,1)S(1)} %collective-permute-done.15.refs_0_, ...), custom_call_target="tpu_custom_call" | custom-call | flops 176160768 | bytes 8388608 | tf_op jit(solution)/shard_map/pallas_call | solution.py:216
  198.5 1.0 fusion.11
  (119 shorter events, 3.3 us)
Async XLA Ops:
  0.6 11.1 %copy-start = (bf16[64,4096]{1,0:T(8,128)(2,1)S(1)}, bf16[64,4096]{1,0:T(8,128)(2,1)}, u32[]{:S(2)}) copy-start(bf16[64,4096]{1,0:T(8,128)(2,1)} %points_ref.3) | copy-start | bytes 1572868
  0.6 44.5 %collective-permute-start.2 = (bf16[64,4096]{1,0:T(8,128)(2,1)}, bf16[64,4096]{1,0:T(8,128)(2,1)S(1)}, u32[]{:S(2)}, u32[]{:S(2)}) collective-permute-start(bf16[64,4096]{1,0:T(8,128)(2,1)} %points_ref.3), channel_id=1, source_target_pairs={{0,2},{2,4},{4,6},{6,0},{1,3},{3,5},{5,7},{7,1},{8,10},{10,12},{12... | collective-permute-start | bytes 1572872 | tf_op jit(solution)/shard_map/ppermute | solution.py:36
  2.4 42.9 %collective-permute-start.1 = (bf16[64,4096]{1,0:T(8,128)(2,1)}, bf16[64,4096]{1,0:T(8,128)(2,1)S(1)}, u32[]{:S(2)}, u32[]{:S(2)}) collective-permute-start(bf16[64,4096]{1,0:T(8,128)(2,1)} %points_ref.3), channel_id=1, source_target_pairs={{0,6},{2,0},{4,2},{6,4},{1,7},{3,1},{5,3},{7,5},{8,14},{10,8},{12,... | collective-permute-start | bytes 1572872 | tf_op jit(solution)/shard_map/ppermute | solution.py:36
  3.9 41.3 %collective-permute-start = (bf16[64,4096]{1,0:T(8,128)(2,1)}, bf16[64,4096]{1,0:T(8,128)(2,1)}, u32[]{:S(2)}, u32[]{:S(2)}) collective-permute-start(bf16[64,4096]{1,0:T(8,128)(2,1)} %points_ref.3), channel_id=1, source_target_pairs={{0,4},{2,6},{4,0},{6,2},{1,5},{3,7},{5,1},{7,3},{8,12},{10,14},{12... | collective-permute-start | bytes 1572872 | tf_op jit(solution)/shard_map/ppermute | solution.py:36
  6.0 6.2 %copy-start.1 = (bf16[32,4096]{1,0:T(8,128)(2,1)S(1)}, bf16[32,4096]{1,0:T(8,128)(2,1)}, u32[]{:S(2)}) copy-start(bf16[32,4096]{1,0:T(8,128)(2,1)} %weights_ref.1) | copy-start | bytes 786436
  6.0 6.2 %copy-start.9 = (s32[4096]{0:T(1024)S(1)}, s32[4096]{0:T(1024)}, u32[]{:S(2)}) copy-start(s32[4096]{0:T(1024)} %param.9) | copy-start | bytes 49156
  9.8 35.4 %collective-permute-start.4 = (bf16[96,2048]{1,0:T(8,128)(2,1)}, bf16[96,2048]{1,0:T(8,128)(2,1)}, u32[]{:S(2)}, u32[]{:S(2)}) collective-permute-start(bf16[96,2048]{1,0:T(8,128)(2,1)} %get-tuple-element.17), channel_id=1, source_target_pairs={{0,32},{1,9},{2,34},{3,11},{4,36},{5,13},{6,38},{7,15},{8,40},{9,1... | collective-permute-start | bytes 1179656 | tf_op jit(solution)/shard_map/ppermute | solution.py:53
  12.2 1.6 copy-start.8
  13.8 1.5 copy-start.4
  15.3 2.9 %copy-start.7 = (s32[1024]{0:T(1024)S(1)}, s32[1024]{0:T(1024)}, u32[]{:S(2)}) copy-start(s32[1024]{0:T(1024)} %param.11) | copy-start | bytes 12292
  15.3 3.3 %copy-start.6 = (s32[1024,12]{0,1:T(8,128)S(1)}, s32[1024,12]{0,1:T(8,128)}, u32[]{:S(2)}) copy-start(s32[1024,12]{0,1:T(8,128)} %param.10) | copy-start | bytes 147460
  15.3 4.8 %copy-start.3 = (bf16[64,2048]{1,0:T(8,128)(2,1)S(1)}, bf16[64,2048]{1,0:T(8,128)(2,1)}, u32[]{:S(2)}) copy-start(bf16[64,2048]{1,0:T(8,128)(2,1)} %get-tuple-element.14) | copy-start | bytes 786436
  15.3 5.5 %collective-permute-start.21 = (bf16[96,512]{1,0:T(8,128)(2,1)S(1)}, bf16[96,512]{1,0:T(8,128)(2,1)S(1)}, u32[]{:S(2)}, u32[]{:S(2)}) collective-permute-start(bf16[96,512]{1,0:T(8,128)(2,1)S(1)} %pad_maximum_fusion.5), channel_id=1, source_target_pairs={{0,1},{1,0},{2,3},{3,2},{4,5},{5,4},{6,7},{7,6},{8,9},{9,8},{10,11... | collective-permute-start | bytes 294920 | tf_op jit(solution)/shard_map/ppermute | solution.py:41
  15.4 4.6 %copy-start.5 = (bf16[32,512]{1,0:T(8,128)(2,1)S(1)}, bf16[32,512]{1,0:T(8,128)(2,1)}, u32[]{:S(2)}) copy-start(bf16[32,512]{1,0:T(8,128)(2,1)} %copy-done.4) | copy-start | bytes 98308
  20.9 8.5 %collective-permute-start.22 = (bf16[96,512]{1,0:T(8,128)(2,1)S(1)}, bf16[96,512]{1,0:T(8,128)(2,1)S(1)}, u32[]{:S(2)}, u32[]{:S(2)}) collective-permute-start(bf16[96,512]{1,0:T(8,128)(2,1)S(1)} %pad_maximum_fusion.6), channel_id=1, source_target_pairs={{0,2},{2,0},{4,6},{6,4},{1,3},{3,1},{5,7},{7,5},{8,10},{10,8},{12,... | collective-permute-start | bytes 294920 | tf_op jit(solution)/shard_map/ppermute | solution.py:41
  29.4 6.2 %collective-permute-start.23 = (bf16[96,512]{1,0:T(8,128)(2,1)S(1)}, bf16[96,512]{1,0:T(8,128)(2,1)S(1)}, u32[]{:S(2)}, u32[]{:S(2)}) collective-permute-start(bf16[96,512]{1,0:T(8,128)(2,1)S(1)} %pad_maximum_fusion.7), channel_id=1, source_target_pairs={{0,4},{2,6},{4,0},{6,2},{1,5},{3,7},{5,1},{7,3},{8,12},{10,14},{12... | collective-permute-start | bytes 294920 | tf_op jit(solution)/shard_map/ppermute | solution.py:41
  35.7 5.4 %collective-permute-start.24 = (bf16[96,512]{1,0:T(8,128)(2,1)S(1)}, bf16[96,512]{1,0:T(8,128)(2,1)S(1)}, u32[]{:S(2)}, u32[]{:S(2)}) collective-permute-start(bf16[96,512]{1,0:T(8,128)(2,1)S(1)} %pad_maximum_fusion.8), channel_id=1, source_target_pairs={{0,8},{8,0},{16,24},{24,16},{1,9},{9,1},{17,25},{25,17},{2,10},{10... | collective-permute-start | bytes 294920 | tf_op jit(solution)/shard_map/ppermute | solution.py:41
  41.1 9.6 %collective-permute-start.5 = (bf16[96,2048]{1,0:T(8,128)(2,1)}, bf16[96,2048]{1,0:T(8,128)(2,1)S(1)}, u32[]{:S(2)}, u32[]{:S(2)}) collective-permute-start(bf16[96,2048]{1,0:T(8,128)(2,1)} %get-tuple-element.17), channel_id=1, source_target_pairs={{0,96},{1,25},{2,98},{3,27},{4,100},{5,29},{6,102},{7,31},{8,104},... | collective-permute-start | bytes 1179656 | tf_op jit(solution)/shard_map/ppermute | solution.py:53
  45.2 14.2 %collective-permute-start.7 = (bf16[96,2048]{1,0:T(8,128)(2,1)S(1)}, bf16[96,2048]{1,0:T(8,128)(2,1)S(1)}, u32[]{:S(2)}, u32[]{:S(2)}) collective-permute-start(bf16[96,2048]{1,0:T(8,128)(2,1)S(1)} %pad_maximum_fusion.4), channel_id=1, source_target_pairs={{0,1},{1,0},{2,3},{3,2},{4,5},{5,4},{6,7},{7,6},{8,9},{9,8},{10,11... | collective-permute-start | bytes 1179656 | tf_op jit(solution)/shard_map/ppermute | solution.py:41
  45.2 9.3 %collective-permute-start.6 = (bf16[96,2048]{1,0:T(8,128)(2,1)}, bf16[96,2048]{1,0:T(8,128)(2,1)S(1)}, u32[]{:S(2)}, u32[]{:S(2)}) collective-permute-start(bf16[96,2048]{1,0:T(8,128)(2,1)} %collective-permute-done.4), channel_id=1, source_target_pairs={{0,32},{1,9},{2,34},{3,11},{4,36},{5,13},{6,38},{7,15},{8,40},{9,1... | collective-permute-start | bytes 1179656 | tf_op jit(solution)/shard_map/ppermute | solution.py:53
  45.3 9.2 %copy-start.2 = (bf16[1,96,2048]{2,1,0:T(8,128)(2,1)S(1)}, bf16[1,96,2048]{2,1,0:T(8,128)(2,1)}, u32[]{:S(2)}) copy-start(bf16[1,96,2048]{2,1,0:T(8,128)(2,1)} %get-tuple-element.16) | copy-start | bytes 1179652
  46.7 51.9 %collective-permute-start.3 = (bf16[4,64,4096]{2,1,0:T(8,128)(2,1)S(1)}, bf16[4,64,4096]{2,1,0:T(8,128)(2,1)S(1)}, u32[]{:S(2)}, u32[]{:S(2)}) collective-permute-start(bf16[4,64,4096]{2,1,0:T(8,128)(2,1)S(1)} %pad_maximum_fusion), channel_id=1, source_target_pairs={{0,1},{1,0},{2,3},{3,2},{4,5},{5,4},{6,7},{7,6},{8,9},{9,8},{10,11... | collective-permute-start | bytes 6291464 | tf_op jit(solution)/shard_map/ppermute | solution.py:41
  55.7 39.6 %collective-permute-start.11 = (bf16[4,96,2048]{2,1,0:T(8,128)(2,1)S(1)}, bf16[4,96,2048]{2,1,0:T(8,128)(2,1)S(1)}, u32[]{:S(2)}, u32[]{:S(2)}) collective-permute-start(bf16[4,96,2048]{2,1,0:T(8,128)(2,1)S(1)} %pad_maximum_fusion.1.refs_0_), channel_id=1, source_target_pairs={{0,8},{1,33},{2,10},{3,35},{4,12},{5,37},{6,14},{7,39},{8,16},{9,4... | collective-permute-start | bytes 4718600 | tf_op jit(solution)/shard_map/ppermute | solution.py:53
  56.5 26.3 %collective-permute-start.25 = (bf16[96,512]{1,0:T(8,128)(2,1)S(1)}, bf16[96,512]{1,0:T(8,128)(2,1)S(1)}, u32[]{:S(2)}, u32[]{:S(2)}) collective-permute-start(bf16[96,512]{1,0:T(8,128)(2,1)S(1)} %pad_maximum_fusion.9), channel_id=1, source_target_pairs={{0,16},{8,24},{16,0},{24,8},{1,17},{9,25},{17,1},{25,9},{2,18},{10... | collective-permute-start | bytes 294920 | tf_op jit(solution)/shard_map/ppermute | solution.py:41
  59.3 23.6 %collective-permute-start.9 = (bf16[96,2048]{1,0:T(8,128)(2,1)S(1)}, bf16[96,2048]{1,0:T(8,128)(2,1)S(1)}, u32[]{:S(2)}, u32[]{:S(2)}) collective-permute-start(bf16[96,2048]{1,0:T(8,128)(2,1)S(1)} %collective-permute-done.7), channel_id=1, source_target_pairs={{0,96},{1,25},{2,98},{3,27},{4,100},{5,29},{6,102},{7,31},{8,104},... | collective-permute-start | bytes 1179656 | tf_op jit(solution)/shard_map/ppermute | solution.py:53
  59.3 25.8 %collective-permute-start.8 = (bf16[96,2048]{1,0:T(8,128)(2,1)S(1)}, bf16[96,2048]{1,0:T(8,128)(2,1)S(1)}, u32[]{:S(2)}, u32[]{:S(2)}) collective-permute-start(bf16[96,2048]{1,0:T(8,128)(2,1)S(1)} %collective-permute-done.7), channel_id=1, source_target_pairs={{0,32},{1,9},{2,34},{3,11},{4,36},{5,13},{6,38},{7,15},{8,40},{9,1... | collective-permute-start | bytes 1179656 | tf_op jit(solution)/shard_map/ppermute | solution.py:53
  82.9 12.1 %collective-permute-start.10 = (bf16[96,2048]{1,0:T(8,128)(2,1)S(1)}, bf16[96,2048]{1,0:T(8,128)(2,1)S(1)}, u32[]{:S(2)}, u32[]{:S(2)}) collective-permute-start(bf16[96,2048]{1,0:T(8,128)(2,1)S(1)} %collective-permute-done.9), channel_id=1, source_target_pairs={{0,96},{1,25},{2,98},{3,27},{4,100},{5,29},{6,102},{7,31},{8,104},... | collective-permute-start | bytes 1179656 | tf_op jit(solution)/shard_map/ppermute | solution.py:53
  84.0 73.4 %collective-permute-start.26 = (bf16[96,512]{1,0:T(8,128)(2,1)S(1)}, bf16[96,512]{1,0:T(8,128)(2,1)S(1)}, u32[]{:S(2)}, u32[]{:S(2)}) collective-permute-start(bf16[96,512]{1,0:T(8,128)(2,1)S(1)} %pad_maximum_fusion.10), channel_id=1, source_target_pairs={{0,32},{32,0},{64,96},{96,64},{1,33},{33,1},{65,97},{97,65},{2,34}... | collective-permute-start | bytes 294920 | tf_op jit(solution)/shard_map/ppermute | solution.py:41
  85.1 38.8 %collective-permute-start.13 = (bf16[4,96,2048]{2,1,0:T(8,128)(2,1)S(1)}, bf16[4,96,2048]{2,1,0:T(8,128)(2,1)S(1)}, u32[]{:S(2)}, u32[]{:S(2)}) collective-permute-start(bf16[4,96,2048]{2,1,0:T(8,128)(2,1)S(1)} %pad_maximum_fusion.1.refs_0_), channel_id=1, source_target_pairs={{0,24},{1,97},{2,26},{3,99},{4,28},{5,101},{6,30},{7,103},{8,0},{9... | collective-permute-start | bytes 4718600 | tf_op jit(solution)/shard_map/ppermute | solution.py:53
  95.2 28.7 %collective-permute-start.12 = (bf16[4,96,2048]{2,1,0:T(8,128)(2,1)S(1)}, bf16[4,96,2048]{2,1,0:T(8,128)(2,1)S(1)}, u32[]{:S(2)}, u32[]{:S(2)}) collective-permute-start(bf16[4,96,2048]{2,1,0:T(8,128)(2,1)S(1)} %pad_maximum_fusion.2.refs_1_), channel_id=1, source_target_pairs={{0,8},{1,33},{2,10},{3,35},{4,12},{5,37},{6,14},{7,39},{8,16},{9,4... | collective-permute-start | bytes 4718600 | tf_op jit(solution)/shard_map/ppermute | solution.py:53
  95.3 27.3 %collective-permute-start.14 = (bf16[4,96,2048]{2,1,0:T(8,128)(2,1)S(1)}, bf16[4,96,2048]{2,1,0:T(8,128)(2,1)S(1)}, u32[]{:S(2)}, u32[]{:S(2)}) collective-permute-start(bf16[4,96,2048]{2,1,0:T(8,128)(2,1)S(1)} %pad_maximum_fusion.2.refs_1_), channel_id=1, source_target_pairs={{0,24},{1,97},{2,26},{3,99},{4,28},{5,101},{6,30},{7,103},{8,0},{9... | collective-permute-start | bytes 4718600 | tf_op jit(solution)/shard_map/ppermute | solution.py:53
  98.5 51.9 %collective-permute-start.15 = (bf16[4,96,2048]{2,1,0:T(8,128)(2,1)S(1)}, bf16[4,96,2048]{2,1,0:T(8,128)(2,1)S(1)}, u32[]{:S(2)}, u32[]{:S(2)}) collective-permute-start(bf16[4,96,2048]{2,1,0:T(8,128)(2,1)S(1)} %collective-permute-done.11.refs_2_), channel_id=1, source_target_pairs={{0,8},{1,33},{2,10},{3,35},{4,12},{5,37},{6,14},{7,39},{8,16},{9,4... | collective-permute-start | bytes 4718600 | tf_op jit(solution)/shard_map/ppermute | solution.py:53
  122.6 27.8 %collective-permute-start.16 = (bf16[4,96,2048]{2,1,0:T(8,128)(2,1)S(1)}, bf16[4,96,2048]{2,1,0:T(8,128)(2,1)S(1)}, u32[]{:S(2)}, u32[]{:S(2)}) collective-permute-start(bf16[4,96,2048]{2,1,0:T(8,128)(2,1)S(1)} %collective-permute-done.14.refs_5_), channel_id=1, source_target_pairs={{0,24},{1,97},{2,26},{3,99},{4,28},{5,101},{6,30},{7,103},{8,0},{9... | collective-permute-start | bytes 4718600 | tf_op jit(solution)/shard_map/ppermute | solution.py:53
  157.3 13.7 %collective-permute-start.17 = (bf16[4,32,4096]{2,1,0:T(8,128)(2,1)S(1)}, bf16[4,32,4096]{2,1,0:T(8,128)(2,1)S(1)}, u32[]{:S(2)}, u32[]{:S(2)}) collective-permute-start(bf16[4,32,4096]{2,1,0:T(8,128)(2,1)S(1)} %shard_map.80), channel_id=1, source_target_pairs={{0,1},{1,0},{2,3},{3,2},{4,5},{5,4},{6,7},{7,6},{8,9},{9,8},{10,11... | collective-permute-start | bytes 3145736 | tf_op jit(solution)/shard_map/ppermute | solution.py:41
  157.5 6.8 %collective-permute-start.27 = (bf16[96,512]{1,0:T(8,128)(2,1)S(1)}, bf16[96,512]{1,0:T(8,128)(2,1)S(1)}, u32[]{:S(2)}, u32[]{:S(2)}) collective-permute-start(bf16[96,512]{1,0:T(8,128)(2,1)S(1)} %pad_maximum_fusion.11), channel_id=1, source_target_pairs={{0,64},{32,96},{64,0},{96,32},{1,65},{33,97},{65,1},{97,33},{2,66}... | collective-permute-start | bytes 294920 | tf_op jit(solution)/shard_map/ppermute | solution.py:41
  171.1 27.4 %collective-permute-start.20 = (bf16[32,4096]{1,0:T(8,128)(2,1)S(1)}, bf16[32,4096]{1,0:T(8,128)(2,1)S(1)}, u32[]{:S(2)}, u32[]{:S(2)}) collective-permute-start(bf16[32,4096]{1,0:T(8,128)(2,1)S(1)} %get-tuple-element.12), channel_id=1, source_target_pairs={{0,6},{2,0},{4,2},{6,4},{1,7},{3,1},{5,3},{7,5},{8,14},{10,8},{12,... | collective-permute-start | bytes 786440 | tf_op jit(solution)/shard_map/ppermute | solution.py:36
  176.3 22.2 %collective-permute-start.19 = (bf16[32,4096]{1,0:T(8,128)(2,1)S(1)}, bf16[32,4096]{1,0:T(8,128)(2,1)S(1)}, u32[]{:S(2)}, u32[]{:S(2)}) collective-permute-start(bf16[32,4096]{1,0:T(8,128)(2,1)S(1)} %get-tuple-element.13), channel_id=1, source_target_pairs={{0,2},{2,4},{4,6},{6,0},{1,3},{3,5},{5,7},{7,1},{8,10},{10,12},{12... | collective-permute-start | bytes 786440 | tf_op jit(solution)/shard_map/ppermute | solution.py:36
  178.6 19.9 %collective-permute-start.18 = (bf16[32,4096]{1,0:T(8,128)(2,1)S(1)}, bf16[32,4096]{1,0:T(8,128)(2,1)S(1)}, u32[]{:S(2)}, u32[]{:S(2)}) collective-permute-start(bf16[32,4096]{1,0:T(8,128)(2,1)S(1)} %get-tuple-element.11), channel_id=1, source_target_pairs={{0,4},{2,6},{4,0},{6,2},{1,5},{3,7},{5,1},{7,3},{8,12},{10,14},{12... | collective-permute-start | bytes 786440 | tf_op jit(solution)/shard_map/ppermute | solution.py:36

commit v3 on v2

--- a/solution.py
+++ b/solution.py
@@ -17,6 +17,7 @@
 P_DEV = LEAF * LEAVES_DEV
 ROWS = D + RHS
 N_DEV = 128
+LEVELS = 7
 SIZES = {"z": 4, "x": 4, "y": 4, "core": 2}
 AXES = ("z", "x", "y", "core")
 DEPTH = D + 16
@@ -26,8 +27,8 @@
 FAR_SCALE = 4.0 / math.sqrt(P_DEV * N_DEV)
 LINE = (2, 1, 3, 0)
 CLASS = LEAVES_DEV // 2
-LISTS = (192, 32, 24, 8)
-STARTS = (0, 192, 224, 248)
+LISTS = (64, 128, 32, 32)
+STARTS = (0, 64, 192, 224)
 SPARE = 2 * len(LINE) * LEAVES_DEV
 
 
@@ -109,34 +110,66 @@
     )(points, weights)
 
 
-def far_kernel(points_ref, node_ref, far_ref, target_aug, source_aug):
+def far_kernel(me_ref, points_ref, partner_ref, skel_ref, far_ref, coords, heavy, folded, sem, target_aug, source_aug):
+    me = me_ref[0]
+    half = SKEL // 2
+    copies = [pltpu.make_async_copy(skel_ref.at[:, D:ROWS, :], folded, sem.at[0])]
+    spans = []
+    for level in range(1, LEVELS):
+        low = ((me >> level) ^ 1) << level
+        for side in range(2):
+            start = low + side * (1 << (level - 1))
+            cols = slice(side * half, (side + 1) * half)
+            spans.append((level, cols, start))
+            copies.append(
+                pltpu.make_async_copy(
+                    skel_ref.at[start, 0:D, :], coords.at[level, :, cols], sem.at[len(copies)]
+                )
+            )
+    for copy in copies:
+        copy.start()
     for leaf in range(LEAVES_DEV):
         cols = slice(leaf * LEAF, (leaf + 1) * LEAF)
         put_points(target_aug.at[:, cols], points_ref[:, cols], 3)
+    coords[0] = partner_ref[0:D, :]
+    heavy[0] = partner_ref[D:ROWS, :]
     far_ref[...] = jnp.zeros_like(far_ref)
-
-    @pl.loop(0, node_ref.shape[0])
+    for copy in copies:
+        copy.wait()
+    for level, cols, start in spans:
+
+        def add(at, total, start=start):
+            return total + folded[start + at].astype(jnp.float32)
+
+        total = lax.fori_loop(0, 1 << (level - 1), add, jnp.zeros((RHS, half), jnp.float32))
+        heavy[level, :, cols] = total.astype(jnp.bfloat16)
+
+    @pl.loop(0, LEVELS)
     def _(level):
-        put_points(source_aug, node_ref[level, 0:D], 0)
-        far_ref[...] += tile_apply(source_aug[...], target_aug[...], node_ref[level, D:ROWS])
+        put_points(source_aug, coords[level], 0)
+        far_ref[...] += tile_apply(source_aug[...], target_aug[...], heavy[level])
 
     far_ref[...] = far_ref[...] * FAR_SCALE
 
 
-def far_terms(points, nodes):
-    levels = nodes.shape[0]
+def far_terms(me, points, partner, skeletons):
+    half = SKEL // 2
     return pl.pallas_call(
         far_kernel,
         out_shape=jax.ShapeDtypeStruct((RHS, P_DEV), jnp.float32),
-        in_specs=[VMEM, VMEM],
+        in_specs=[SMEM, VMEM, VMEM, ANY],
         out_specs=VMEM,
         scratch_shapes=[
+            pltpu.VMEM((LEVELS, D, SKEL), jnp.bfloat16),
+            pltpu.VMEM((LEVELS, RHS, SKEL), jnp.bfloat16),
+            pltpu.VMEM((N_DEV, RHS, half), jnp.bfloat16),
+            pltpu.SemaphoreType.DMA((2 * LEVELS - 1,)),
             pltpu.VMEM((DEPTH, P_DEV), jnp.bfloat16),
             pltpu.VMEM((DEPTH, SKEL), jnp.bfloat16),
         ],
         compiler_params=pltpu.CompilerParams(vmem_limit_bytes=24 << 20),
-        cost_estimate=cost(levels * SKEL * P_DEV, 2 << 20),
-    )(points, nodes)
+        cost_estimate=cost(LEVELS * SKEL * P_DEV, 4 << 20),
+    )(me, points, partner, skeletons)
 
 
 def near_kernel(first, devices, n_source, seeded, pair_ref, count_ref, target_ref, *refs):
@@ -150,10 +183,10 @@
     def fetch(group, slot):
         for unit in range(UNROLL):
             code = pair_ref[group * UNROLL + unit]
-            target = jnp.minimum(code // (32 * CLASS), SPARE - 1)
+            target = code // (256 * CLASS)
             start = pl.multiple_of(target % LEAVES_DEV * LEAF, LEAF)
             pltpu.make_async_copy(
-                target_ref.at[target // LEAVES_DEV, :, pl.ds(start, LEAF)],
+                target_ref.at[code // (32 * CLASS) % 8, :, pl.ds(start, LEAF)],
                 target_buf.at[slot, unit],
                 sem.at[slot, unit, 1],
             ).start()
@@ -199,7 +232,7 @@
 
         arrive(slot)
         for unit in range(UNROLL):
-            target = pair_ref[group * UNROLL + unit] // (32 * CLASS)
+            target = pair_ref[group * UNROLL + unit] // (256 * CLASS)
             put_points(source_aug.at[unit], buf[slot, unit, 0:D], 0)
             put_points(target_aug.at[unit], target_buf[slot, unit], 3)
             acc[jnp.minimum(target - first * LEAVES_DEV, leaves)] += tile_apply(
@@ -237,33 +270,13 @@
     return summed.astype(jnp.bfloat16)
 
 
-def fold_node(node):
-    half = SKEL // 2
-    return jnp.concatenate([node[:D, :half], fold(node[D:])], axis=0)
-
-
-def sibling_nodes(base, place):
-    found = []
-    current = base
-    steps = [("core", 1)] + [(axis, bit) for axis in ("y", "x", "z") for bit in (1, 2)]
-    for level, (axis, bit) in enumerate(steps):
-        partner = swap(current, axis, bit)
-        found.append(partner)
-        if level + 1 < len(steps):
-            upper = (place[axis] // bit) % 2
-            mine, theirs = fold_node(current), fold_node(partner)
-            current = jnp.concatenate(
-                [jnp.where(upper == 0, mine, theirs), jnp.where(upper == 0, theirs, mine)], axis=1
-            )
-    return jnp.stack(found)
-
-
 def pair_lists(near_leaf, near_count, place):
-    rows, counts = [], []
+    rows, counts, lines = [], [], []
     for core in (1 - place["core"], place["core"]):
         for by in LINE:
             y = (place["y"] + by) % SIZES["y"]
             device = ((place["z"] * 4 + place["x"]) * 4 + y) * 2 + core
+            lines.append(y * 2 + core)
             rows.append(lax.dynamic_slice_in_dim(near_leaf, device * LEAVES_DEV, LEAVES_DEV))
             counts.append(lax.dynamic_slice_in_dim(near_count, device * LEAVES_DEV, LEAVES_DEV))
     leaf_ids = jnp.concatenate(rows, axis=0).reshape(-1)
@@ -275,13 +288,14 @@
     on_z = place["core"] == 0
     inner, outer = jnp.where(on_z, back_z, back_x), jnp.where(on_z, back_x, back_z)
     inner, outer = (jnp.where(back == 0, 0, jnp.where(back == 1, 1, 5 - back)) for back in (inner, outer))
-    which = outer * 2 + (owner % 2 != place["core"]).astype(jnp.int32)
-    late = which >= 6
+    other = (owner % 2 != place["core"]).astype(jnp.int32)
     at = jnp.arange(leaf_ids.shape[0], dtype=jnp.int32)
     target = at // NEAR
-    code = ((target * 8 + jnp.where(late, which - 6, which)) * 4 + inner) * CLASS + local % CLASS
-    group = jnp.where(target < 32, 1, jnp.where(target < 56, 2, 3))
-    group = jnp.where(valid, jnp.where(late, group, 0), -1)
+    line = jnp.repeat(jnp.stack(lines), LEAVES_DEV * NEAR, total_repeat_length=leaf_ids.shape[0])
+    which = jnp.where((outer == 1) | (outer == 2), outer - 1 + 2 * other, other)
+    code = (((target * 8 + line) * 8 + which) * 4 + inner) * CLASS + local % CLASS
+    group = jnp.where(outer == 0, 0, jnp.where(outer < 3, 1, jnp.where(target < SPARE // 2, 2, 3)))
+    group = jnp.where(valid, group, -1)
     rank = jnp.sum(((group[None, :] == group[:, None]) & (at[None, :] < at[:, None])).astype(jnp.int32), axis=1)
     base = jnp.zeros_like(group)
     for index, start in enumerate(STARTS):
@@ -290,7 +304,7 @@
     place_at = jnp.arange(sum(LISTS), dtype=jnp.int32)
     hit = goal[None, :] == place_at[:, None]
     packed = jnp.sum(jnp.where(hit, code[None, :] + 1, 0), axis=1)
-    packed = jnp.where(packed == 0, SPARE * 32 * CLASS, packed - 1)
+    packed = jnp.where(packed == 0, SPARE * 256 * CLASS, packed - 1)
     totals = jnp.sum((group[None, :] == jnp.arange(len(LISTS), dtype=jnp.int32)[:, None]).astype(jnp.int32), axis=1)
     return (
         [packed[s : s + n] for s, n in zip(STARTS, LISTS)],
@@ -299,10 +313,13 @@
 
 
 def spread(own, other, stage):
-    ahead, ahead_other = ring(own, 1, stage), ring(other, 1, stage)
-    behind_other, behind = ring(other, -1, stage), ring(own, -1, stage)
-    across, across_other = ring(ahead, 1, stage), ring(behind_other, -1, stage)
-    return (own, ahead, behind, across), (other, ahead_other, behind_other, across_other)
+    ahead, behind_other = ring(own, 1, stage), ring(other, -1, stage)
+    ahead_other, behind = ring(other, 1, stage), ring(own, -1, stage)
+    return (ahead, behind), (ahead_other, behind_other)
+
+
+def spread_on(own, other, stage):
+    return ring(own[0], 1, stage), ring(other[1], -1, stage)
 
 
 def per_device(points, weights, skel_index, assign, near_leaf, near_count):
@@ -315,34 +332,43 @@
             [lax.dynamic_slice_in_dim(a, which * width, width, axis=1) for a in (points, weights)], axis=0
         )
 
-    own, other = spread(leaf_class(core), swap(leaf_class(1 - core), "core", 1), 0)
-    own, other = spread(jnp.stack(own), jnp.stack(other), 1)
-
-    line = jnp.stack([shift(points, "y", -by) if by else points for by in LINE])
-    targets = jnp.concatenate([swap(line, "core", 1), line], axis=0)
+    targets = lax.all_gather(points, ("y", "core"))
+    mine, theirs = leaf_class(core), leaf_class(1 - core)
+    theirs = swap(theirs, "core", 1)
+    own, other = spread(mine, theirs, 0)
+    own_far, other_far = spread_on(own, other, 0)
+    _, assign, skel_index = lax.optimization_barrier((own[0], assign, skel_index))
+    own_line = jnp.stack([mine, *own, own_far])
+    other_line = jnp.stack([theirs, *other, other_far])
+    own, other = spread(own_line, other_line, 1)
 
     member = (assign[None, :] == jnp.arange(SKEL, dtype=jnp.int32)[:, None]).astype(jnp.bfloat16)
     base_weights = lax.dot_general(
         weights, member, (((1,), (1,)), ((), ())), preferred_element_type=jnp.float32
-    )
-    base = jnp.concatenate([points[:, skel_index], base_weights.astype(jnp.bfloat16)], axis=0)
-    nodes = sibling_nodes(base, place)
+    ).astype(jnp.bfloat16)
+    base = jnp.concatenate([points[:, skel_index], base_weights], axis=0)
+    folded = jnp.concatenate([base[:D, : SKEL // 2], fold(base_weights)], axis=0)
+    skeletons = lax.all_gather(folded, AXES)
+    me = ((place["z"] * 4 + place["x"]) * 4 + place["y"]) * 2 + core
+    far_field = far_terms(me.reshape(1), points, swap(base, "core", 1), skeletons)
     self_sum = self_terms(points, weights)
-    far_field = far_terms(points, nodes)
 
     pairs, totals = pair_lists(near_leaf, near_count, place)
-    early = [own[0], other[0], own[1], other[1], own[2], other[2]]
-    late = [own[3], other[3]]
-    early_sum = near_part(pairs[0], totals[0], targets, early, 0, 8, None, jnp.float32, 72)
-    early_sum, late = lax.optimization_barrier((early_sum, late))
-    across = near_part(pairs[1], totals[1], targets, late, 0, 4, early_sum[0:4], jnp.bfloat16, 12)
+    seed = near_part(pairs[0], totals[0], targets, [own_line, other_line], 0, 8, None, jnp.float32, 24)
+    seed, own, other = lax.optimization_barrier((seed, own, other))
+    late = spread_on(own, other, 1)
+    seed = near_part(pairs[1], totals[1], targets, [*own, *other], 0, 8, seed, jnp.float32, 48)
+    across = near_part(pairs[2], totals[2], targets, late, 0, 4, seed[0:4], jnp.bfloat16, 12)
     across = swap(across, "core", 1)
-    along = near_part(pairs[2], totals[2], targets, late, 4, 3, early_sum[4:7], jnp.float32, 9)
-    home = near_part(pairs[3], totals[3], targets, late, 7, 1, early_sum[7:8], jnp.float32, 3)
-    near_sum = self_sum + home[0] + across[3].astype(jnp.float32)
-    for at, by in enumerate(LINE[:3]):
-        part = (along[at] + across[at].astype(jnp.float32)).astype(jnp.bfloat16)
-        near_sum = near_sum + shift(part, "y", by).astype(jnp.float32)
+    along = near_part(pairs[3], totals[3], targets, late, 4, 4, seed[4:8], jnp.float32, 12)
+    parts = [
+        shift((along[at] + across[at].astype(jnp.float32)).astype(jnp.bfloat16), "y", by)
+        for at, by in enumerate(LINE[:3])
+    ]
+    near_sum = self_sum + along[3] + across[3].astype(jnp.float32)
+    near_sum, parts, far_field = lax.optimization_barrier((near_sum, parts, far_field))
+    for part in parts:
+        near_sum = near_sum + part.astype(jnp.float32)
     return (near_sum * NEAR_SCALE, far_field)
 
 

time: 201 us -> 167 us (0.83)
  the two profiles are of different devices: /device:TPU:0 before, /device:TPU:4 now
where the time goes in v3:
time: 167 us
  Pallas kernels  59.6 us (36%)
  waiting for transfers between devices  42.4 us (25%)
  starting transfers between devices  26.1 us (16%)
  between operations  14.5 us (9%)
  local copies, waits for them, and re-layouts  13 us (8%)
  other arithmetic  9.48 us (6%)
    pallas_call x4, Pallas kernels, near_part(): pl.pallas_call(functools.partial(near_kernel, first, devices, len(sources...  40.9 us
    ppermute x12, waiting for transfers between devices, ring(): return lax.ppermute(block, AXES, route)  39.9 us
    pallas_call x1, Pallas kernels, far_terms(): pl.pallas_call(far_kernel, out_shape=jax.ShapeDtypeStruct((RHS, P_DEV), j...  16 us
    ppermute x12, starting transfers between devices, ring(): return lax.ppermute(block, AXES, route)  15.7 us
    ppermute x3, starting transfers between devices, shift(): lax.ppermute(block, axis, [(i, (i + by) % count) for i in range(count)])  9.54 us
    unnamed x43, local copies, waits for them, and re-layouts  7.72 us
  transfers between devices with their start and end apart: 20, of which 8 were waited for; matrix products, arithmetic and copies ran while one was open for 9% of the time, Pallas kernels for 36%

profile of v3, /device:TPU:4, one launch (start us, length us, event | category | flops | bytes accessed | tf_op | source)
XLA Modules:
  0.0 166.7 jit_solution(16990934279141198808)
XLA Ops:
  7.2 0.7 all-gather.5.cloned.1.call-update
  8.0 1.0 constant_dynamic-slice_fusion
  9.0 1.1 constant_dynamic-slice_fusion.1
  10.1 0.8 fusion.42
  10.9 1.9 %collective-permute-start = (bf16[96,2048]{1,0:T(8,128)(2,1)}, bf16[96,2048]{1,0:T(8,128)(2,1)S(1)}, u32[]{:S(2)}, u32[]{:S(2)}) collective-permute-start(bf16[96,2048]{1,0:T(8,128)(2,1)} %get-tuple-element.48), channel_id=1, source_target_pairs={{0,32},{1,9},{2,34},{3,11},{4,36},{5,13},{6,38},{7,15},{8,40},{9,1... | collective-permute-start | bytes 1179656 | tf_op jit(solution)/shard_map/ppermute | solution.py:54
  12.8 0.5 copy.14
  13.3 7.6 %collective-permute-done = bf16[96,2048]{1,0:T(8,128)(2,1)S(1)} collective-permute-done((bf16[96,2048]{1,0:T(8,128)(2,1)}, bf16[96,2048]{1,0:T(8,128)(2,1)S(1)}, u32[]{:S(2)}, u32[]{:S(2)}) %collective-permute-start) | collective-permute-done | bytes 393248 | tf_op jit(solution)/shard_map/ppermute | solution.py:54
  20.9 1.3 gather_fusion
  22.4 1.5 fusion.4
  24.0 0.6 pad_maximum_fusion.5
  24.8 1.8 %collective-permute-done.3 = bf16[96,2048]{1,0:T(8,128)(2,1)} collective-permute-done((bf16[96,2048]{1,0:T(8,128)(2,1)S(1)}, bf16[96,2048]{1,0:T(8,128)(2,1)}, u32[]{:S(2)}, u32[]{:S(2)}) %collective-permute-start.3) | collective-permute-done | bytes 393248 | tf_op jit(solution)/shard_map/ppermute | solution.py:42
  26.6 2.0 %collective-permute-start.5 = (bf16[96,2048]{1,0:T(8,128)(2,1)}, bf16[96,2048]{1,0:T(8,128)(2,1)}, u32[]{:S(2)}, u32[]{:S(2)}) collective-permute-start(bf16[96,2048]{1,0:T(8,128)(2,1)} %collective-permute-done.3), channel_id=1, source_target_pairs={{0,96},{1,25},{2,98},{3,27},{4,100},{5,29},{6,102},{7,31},{8,104},... | collective-permute-start | bytes 1179656 | tf_op jit(solution)/shard_map/ppermute | solution.py:54
  28.6 0.4 collective-permute-start.1
  29.0 1.6 collective-permute-start.2
  30.8 3.8 %collective-permute-done.5 = bf16[96,2048]{1,0:T(8,128)(2,1)} collective-permute-done((bf16[96,2048]{1,0:T(8,128)(2,1)}, bf16[96,2048]{1,0:T(8,128)(2,1)}, u32[]{:S(2)}, u32[]{:S(2)}) %collective-permute-start.5) | collective-permute-done | bytes 393248 | tf_op jit(solution)/shard_map/ppermute | solution.py:54
  34.7 3.2 %collective-permute-start.6 = (bf16[96,2048]{1,0:T(8,128)(2,1)}, bf16[96,2048]{1,0:T(8,128)(2,1)S(1)}, u32[]{:S(2)}, u32[]{:S(2)}) collective-permute-start(bf16[96,2048]{1,0:T(8,128)(2,1)} %collective-permute-done.5), channel_id=1, source_target_pairs={{0,96},{1,25},{2,98},{3,27},{4,100},{5,29},{6,102},{7,31},{8,104},... | collective-permute-start | bytes 1179656 | tf_op jit(solution)/shard_map/ppermute | solution.py:54
  38.0 0.9 collective-permute-done.1
  38.9 1.4 pad_maximum_fusion.refs_0_
  40.3 1.3 collective-permute-start.7
  41.5 0.8 collective-permute-start.8
  42.4 1.9 %collective-permute-done.6 = bf16[96,2048]{1,0:T(8,128)(2,1)S(1)} collective-permute-done((bf16[96,2048]{1,0:T(8,128)(2,1)}, bf16[96,2048]{1,0:T(8,128)(2,1)S(1)}, u32[]{:S(2)}, u32[]{:S(2)}) %collective-permute-start.6) | collective-permute-done | bytes 393248 | tf_op jit(solution)/shard_map/ppermute | solution.py:54
  44.3 2.5 %pad_maximum_fusion.1.refs_1_ = bf16[4,96,2048]{2,1,0:T(8,128)(2,1)} fusion(bf16[1,96,2048]{2,1,0:T(8,128)(2,1)S(1)} %bitcast.42, bf16[1,96,2048]{2,1,0:T(8,128)(2,1)} %bitcast.7, bf16[1,96,2048]{2,1,0:T(8,128)(2,1)S(1)} %bitcast.41, bf16[1,96,2048]{2,1,0:T(8,128)(2,1)} %bitcast.5), kind=kLoop, calls=%fused_computation.8 | loop fusion | flops 2359296 | bytes 3145728 | tf_op jit(solution)/shard_map/stack | solution.py:342
  46.8 0.5 collective-permute-start.10
  47.4 1.5 collective-permute-start.9
  49.4 0.4 convert_reduce_fusion
  49.9 0.2 select_reduce_fusion
  50.1 0.1 convert_reduce_fusion.1
  50.2 0.6 fusion.47
  50.8 2.2 %copy-done = bf16[512,4096]{1,0:T(8,128)(2,1)S(1)} copy-done((bf16[512,4096]{1,0:T(8,128)(2,1)S(1)}, bf16[512,4096]{1,0:T(8,128)(2,1)}, u32[]{:S(2)}) %copy-start) | copy-done | bytes 4194328
  53.0 10.3 %shard_map.78.refs_4_ = f32[8,32,4096]{2,1,0:T(8,128)S(1)} custom-call(s32[64]{0:T(128)S(1)} %slice.81.pair_ref, s32[1]{0:T(128)} %get-tuple-element.71.count_ref, bf16[8,64,4096]{2,1,0:T(8,128)(2,1)S(1)} %bitcast.33, bf16[4,96,2048]{2,1,0:T(8,128)(2,1)S(1)} %pad_maximum_fusion.refs_0_, bf16[4,96,2048]{2,1,0:T(8,128)(2,1)} %pad_maximum_fusion.1.refs_1_), custom_call_target="tpu_custom_call" | custom-call | flops 1409286144 | bytes 8388608 | tf_op jit(solution)/shard_map/pallas_call | solution.py:249
  63.4 16.0 %collective-permute-done.10.refs_3_ = bf16[4,96,2048]{2,1,0:T(8,128)(2,1)} collective-permute-done((bf16[4,96,2048]{2,1,0:T(8,128)(2,1)}, bf16[4,96,2048]{2,1,0:T(8,128)(2,1)}, u32[]{:S(2)}, u32[]{:S(2)}) %collective-permute-start.10) | collective-permute-done | bytes 1572896 | tf_op jit(solution)/shard_map/ppermute | solution.py:54
  79.4 2.4 %collective-permute-start.11 = (bf16[4,96,2048]{2,1,0:T(8,128)(2,1)}, bf16[4,96,2048]{2,1,0:T(8,128)(2,1)S(1)}, u32[]{:S(2)}, u32[]{:S(2)}) collective-permute-start(bf16[4,96,2048]{2,1,0:T(8,128)(2,1)} %collective-permute-done.7.refs_0_), channel_id=1, source_target_pairs={{0,8},{1,33},{2,10},{3,35},{4,12},{5,37},{6,14},{7,39},{8,16},{9,4... | collective-permute-start | bytes 4718600 | tf_op jit(solution)/shard_map/ppermute | solution.py:54
  82.0 16.4 %shard_map.79 = f32[8,32,4096]{2,1,0:T(8,128)S(1)} custom-call(s32[128]{0:T(128)S(1)} %slice.83.pair_ref, s32[1]{0:T(128)} %get-tuple-element.70.count_ref, bf16[8,64,4096]{2,1,0:T(8,128)(2,1)S(1)} %bitcast.34, bf16[4,96,2048]{2,1,0:T(8,128)(2,1)} %collective-permute-done.7.refs_0_, bf16[4,96,2048]{2,1,0:T(8,128)(2,1)} %collective-permute-done.8.refs_1_, ...), custom_call_target="tpu_custom_call" | custom-call | flops 2818572288 | bytes 8388608 | tf_op jit(solution)/shard_map/pallas_call | solution.py:249
  98.4 0.3 fusion.44
  98.7 6.1 %collective-permute-done.11.refs_0_ = bf16[4,96,2048]{2,1,0:T(8,128)(2,1)S(1)} collective-permute-done((bf16[4,96,2048]{2,1,0:T(8,128)(2,1)}, bf16[4,96,2048]{2,1,0:T(8,128)(2,1)S(1)}, u32[]{:S(2)}, u32[]{:S(2)}) %collective-permute-start.11) | collective-permute-done | bytes 1572896 | tf_op jit(solution)/shard_map/ppermute | solution.py:54
  104.8 3.5 %collective-permute-done.12.refs_1_ = bf16[4,96,2048]{2,1,0:T(8,128)(2,1)S(1)} collective-permute-done((bf16[4,96,2048]{2,1,0:T(8,128)(2,1)}, bf16[4,96,2048]{2,1,0:T(8,128)(2,1)S(1)}, u32[]{:S(2)}, u32[]{:S(2)}) %collective-permute-start.12) | collective-permute-done | bytes 1572896 | tf_op jit(solution)/shard_map/ppermute | solution.py:54
  108.3 7.5 %shard_map.81 = bf16[4,32,4096]{2,1,0:T(8,128)(2,1)} custom-call(s32[32]{0:T(128)S(1)} %get-tuple-element.67.pair_ref, s32[1]{0:T(128)} %get-tuple-element.69.count_ref, bf16[8,64,4096]{2,1,0:T(8,128)(2,1)S(1)} %bitcast.35, bf16[4,96,2048]{2,1,0:T(8,128)(2,1)S(1)} %collective-permute-done.11.refs_0_, ...), custom_call_target="tpu_custom_call" | custom-call | flops 704643072 | bytes 8388608 | tf_op jit(solution)/shard_map/pallas_call | solution.py:249
  116.0 2.8 %shard_map.77 = f32[32,4096]{1,0:T(8,128)S(1)} custom-call(bf16[64,4096]{1,0:T(8,128)(2,1)S(1)} %copy-done.7, bf16[32,4096]{1,0:T(8,128)(2,1)S(1)} %copy-done.8), custom_call_target="tpu_custom_call" | custom-call | flops 469762048 | bytes 2097152 | tf_op jit(solution)/shard_map/pallas_call | solution.py:102
  118.8 0.6 collective-permute-start.17
  119.3 2.2 %copy-done.2 = bf16[512,4096]{1,0:T(8,128)(2,1)S(1)} copy-done((bf16[512,4096]{1,0:T(8,128)(2,1)S(1)}, bf16[512,4096]{1,0:T(8,128)(2,1)}, u32[]{:S(2)}) %copy-start.2) | copy-done | bytes 4194328
  121.5 6.6 %shard_map.80 = f32[4,32,4096]{2,1,0:T(8,128)S(1)} custom-call(s32[32]{0:T(128)S(1)} %get-tuple-element.68.pair_ref, s32[1]{0:T(128)} %get-tuple-element.72.count_ref, bf16[8,64,4096]{2,1,0:T(8,128)(2,1)S(1)} %bitcast.36, bf16[4,96,2048]{2,1,0:T(8,128)(2,1)S(1)} %copy-done.4, bf16[4,96,2048]{2,1,0:T(8,128)(2,1)S(1)} %copy-done.6, ...), custom_call_target="tpu_custom_call" | custom-call | flops 704643072 | bytes 8388608 | tf_op jit(solution)/shard_map/pallas_call | solution.py:249
  128.2 1.3 fusion.12
  129.5 6.3 %collective-permute-start.14 = (bf16[32,4096]{1,0:T(8,128)(2,1)S(1)}, bf16[32,4096]{1,0:T(8,128)(2,1)S(1)}, u32[]{:S(2)}, u32[]{:S(2)}) collective-permute-start(bf16[32,4096]{1,0:T(8,128)(2,1)S(1)} %get-tuple-element.44), channel_id=1, source_target_pairs={{0,4},{2,6},{4,0},{6,2},{1,5},{3,7},{5,1},{7,3},{8,12},{10,14},{12... | collective-permute-start | bytes 786440 | tf_op jit(solution)/shard_map/ppermute | solution.py:37
  135.8 3.2 %collective-permute-start.16 = (bf16[32,4096]{1,0:T(8,128)(2,1)S(1)}, bf16[32,4096]{1,0:T(8,128)(2,1)S(1)}, u32[]{:S(2)}, u32[]{:S(2)}) collective-permute-start(bf16[32,4096]{1,0:T(8,128)(2,1)S(1)} %get-tuple-element.42), channel_id=1, source_target_pairs={{0,6},{2,0},{4,2},{6,4},{1,7},{3,1},{5,3},{7,5},{8,14},{10,8},{12,... | collective-permute-start | bytes 786440 | tf_op jit(solution)/shard_map/ppermute | solution.py:37
  139.0 1.0 fusion.9
  140.1 2.8 %copy-done.9 = bf16[12288,256]{1,0:T(8,128)(2,1)S(1)} copy-done((bf16[12288,256]{1,0:T(8,128)(2,1)S(1)}, bf16[12288,256]{1,0:T(8,128)(2,1)}, u32[]{:S(2)}) %copy-start.9) | copy-done | bytes 6291480
  142.9 16.0 %shard_map.82 = f32[32,4096]{1,0:T(8,128)} custom-call(s32[1]{0:T(128)} %bitcast.14.me_ref, bf16[64,4096]{1,0:T(8,128)(2,1)S(1)} %copy-done.7, bf16[96,512]{1,0:T(8,128)(2,1)S(1)} %collective-permute-done.17.partner_ref, bf16[128,96,256]{2,1,0:T(8,128)(2,1)S(1)} %bitcast.37), custom_call_target="tpu_custom_call" | custom-call | flops 3288334336 | bytes 4194304 | tf_op jit(solution)/shard_map/pallas_call | solution.py:157
  158.9 0.9 add_multiply_fusion
  (81 shorter events, 1.6 us)
Async XLA Ops:
  7.2 5.7 %copy-start.7 = (bf16[64,4096]{1,0:T(8,128)(2,1)S(1)}, bf16[64,4096]{1,0:T(8,128)(2,1)}, u32[]{:S(2)}) copy-start(bf16[64,4096]{1,0:T(8,128)(2,1)} %points_ref.3) | copy-start | bytes 1572868
  7.2 43.7 %all-gather.5.cloned.1.call-start = ((), (), s32[]{:S(2)}) async-start(), calls=%async_computation | async-start | bytes 4718592 | tf_op jit(solution)/shard_map/all_gather | solution.py:335
  7.9 132.2 %all-gather.7.cloned.1.call-start = ((), (), s32[]{:S(2)}) async-start(), calls=%async_computation.1 | async-start | bytes 6340608 | tf_op jit(solution)/shard_map/all_gather | solution.py:351
  10.0 10.9 %copy-start.12 = (s32[512]{0:T(512)S(1)}, s32[512]{0:T(512)}, u32[]{:S(2)}) copy-start(s32[512]{0:T(512)} %param.10) | copy-start | bytes 6148
  10.0 12.3 %copy-start.8 = (bf16[32,4096]{1,0:T(8,128)(2,1)S(1)}, bf16[32,4096]{1,0:T(8,128)(2,1)}, u32[]{:S(2)}) copy-start(bf16[32,4096]{1,0:T(8,128)(2,1)} %weights_ref.1) | copy-start | bytes 786436
  10.1 12.3 %copy-start.20 = (s32[4096]{0:T(1024)S(1)}, s32[4096]{0:T(1024)}, u32[]{:S(2)}) copy-start(s32[4096]{0:T(1024)} %param.11) | copy-start | bytes 49156
  10.9 10.0 %collective-permute-start = (bf16[96,2048]{1,0:T(8,128)(2,1)}, bf16[96,2048]{1,0:T(8,128)(2,1)S(1)}, u32[]{:S(2)}, u32[]{:S(2)}) collective-permute-start(bf16[96,2048]{1,0:T(8,128)(2,1)} %get-tuple-element.48), channel_id=1, source_target_pairs={{0,32},{1,9},{2,34},{3,11},{4,36},{5,13},{6,38},{7,15},{8,40},{9,1... | collective-permute-start | bytes 1179656 | tf_op jit(solution)/shard_map/ppermute | solution.py:54
  22.4 8.2 %copy-start.11 = (s32[1024]{0:T(1024)S(1)}, s32[1024]{0:T(1024)}, u32[]{:S(2)}) copy-start(s32[1024]{0:T(1024)} %param.13) | copy-start | bytes 12292
  24.7 1.9 %collective-permute-start.3 = (bf16[96,2048]{1,0:T(8,128)(2,1)S(1)}, bf16[96,2048]{1,0:T(8,128)(2,1)}, u32[]{:S(2)}, u32[]{:S(2)}) collective-permute-start(bf16[96,2048]{1,0:T(8,128)(2,1)S(1)} %pad_maximum_fusion.3), channel_id=1, source_target_pairs={{0,1},{1,0},{2,3},{3,2},{4,5},{5,4},{6,7},{7,6},{8,9},{9,8},{10,11... | collective-permute-start | bytes 1179656 | tf_op jit(solution)/shard_map/ppermute | solution.py:42
  26.6 8.1 %collective-permute-start.5 = (bf16[96,2048]{1,0:T(8,128)(2,1)}, bf16[96,2048]{1,0:T(8,128)(2,1)}, u32[]{:S(2)}, u32[]{:S(2)}) collective-permute-start(bf16[96,2048]{1,0:T(8,128)(2,1)} %collective-permute-done.3), channel_id=1, source_target_pairs={{0,96},{1,25},{2,98},{3,27},{4,100},{5,29},{6,102},{7,31},{8,104},... | collective-permute-start | bytes 1179656 | tf_op jit(solution)/shard_map/ppermute | solution.py:54
  28.6 10.3 %collective-permute-start.1 = (bf16[96,2048]{1,0:T(8,128)(2,1)}, bf16[96,2048]{1,0:T(8,128)(2,1)}, u32[]{:S(2)}, u32[]{:S(2)}) collective-permute-start(bf16[96,2048]{1,0:T(8,128)(2,1)} %get-tuple-element.48), channel_id=1, source_target_pairs={{0,96},{1,25},{2,98},{3,27},{4,100},{5,29},{6,102},{7,31},{8,104},... | collective-permute-start | bytes 1179656 | tf_op jit(solution)/shard_map/ppermute | solution.py:54
  29.0 9.9 %collective-permute-start.2 = (bf16[96,2048]{1,0:T(8,128)(2,1)S(1)}, bf16[96,2048]{1,0:T(8,128)(2,1)}, u32[]{:S(2)}, u32[]{:S(2)}) collective-permute-start(bf16[96,2048]{1,0:T(8,128)(2,1)S(1)} %collective-permute-done), channel_id=1, source_target_pairs={{0,32},{1,9},{2,34},{3,11},{4,36},{5,13},{6,38},{7,15},{8,40},{9,1... | collective-permute-start | bytes 1179656 | tf_op jit(solution)/shard_map/ppermute | solution.py:54
  30.8 11.5 %collective-permute-start.4 = (bf16[96,2048]{1,0:T(8,128)(2,1)}, bf16[96,2048]{1,0:T(8,128)(2,1)S(1)}, u32[]{:S(2)}, u32[]{:S(2)}) collective-permute-start(bf16[96,2048]{1,0:T(8,128)(2,1)} %collective-permute-done.3), channel_id=1, source_target_pairs={{0,32},{1,9},{2,34},{3,11},{4,36},{5,13},{6,38},{7,15},{8,40},{9,1... | collective-permute-start | bytes 1179656 | tf_op jit(solution)/shard_map/ppermute | solution.py:54
  34.7 9.6 %collective-permute-start.6 = (bf16[96,2048]{1,0:T(8,128)(2,1)}, bf16[96,2048]{1,0:T(8,128)(2,1)S(1)}, u32[]{:S(2)}, u32[]{:S(2)}) collective-permute-start(bf16[96,2048]{1,0:T(8,128)(2,1)} %collective-permute-done.5), channel_id=1, source_target_pairs={{0,96},{1,25},{2,98},{3,27},{4,100},{5,29},{6,102},{7,31},{8,104},... | collective-permute-start | bytes 1179656 | tf_op jit(solution)/shard_map/ppermute | solution.py:54
  40.3 23.1 %collective-permute-start.7 = (bf16[4,96,2048]{2,1,0:T(8,128)(2,1)S(1)}, bf16[4,96,2048]{2,1,0:T(8,128)(2,1)}, u32[]{:S(2)}, u32[]{:S(2)}) collective-permute-start(bf16[4,96,2048]{2,1,0:T(8,128)(2,1)S(1)} %pad_maximum_fusion.refs_0_), channel_id=1, source_target_pairs={{0,8},{1,33},{2,10},{3,35},{4,12},{5,37},{6,14},{7,39},{8,16},{9,4... | collective-permute-start | bytes 4718600 | tf_op jit(solution)/shard_map/ppermute | solution.py:54
  41.5 21.9 %collective-permute-start.8 = (bf16[4,96,2048]{2,1,0:T(8,128)(2,1)S(1)}, bf16[4,96,2048]{2,1,0:T(8,128)(2,1)}, u32[]{:S(2)}, u32[]{:S(2)}) collective-permute-start(bf16[4,96,2048]{2,1,0:T(8,128)(2,1)S(1)} %pad_maximum_fusion.refs_0_), channel_id=1, source_target_pairs={{0,24},{1,97},{2,26},{3,99},{4,28},{5,101},{6,30},{7,103},{8,0},{9... | collective-permute-start | bytes 4718600 | tf_op jit(solution)/shard_map/ppermute | solution.py:54
  44.2 4.6 %copy-start.10 = (s32[1024,12]{0,1:T(8,128)S(1)}, s32[1024,12]{0,1:T(8,128)}, u32[]{:S(2)}) copy-start(s32[1024,12]{0,1:T(8,128)} %param.12) | copy-start | bytes 147460
  44.3 5.6 %copy-start.13 = (pred[768]{0:T(1024)(128)(4,1)S(1)}, pred[768]{0:T(1024)(128)(4,1)}, u32[]{:S(2)}) copy-start(pred[768]{0:T(1024)(128)(4,1)} %constant.295) | copy-start | bytes 2308
  44.3 5.6 %copy-start.14 = (pred[768]{0:T(1024)(128)(4,1)S(1)}, pred[768]{0:T(1024)(128)(4,1)}, u32[]{:S(2)}) copy-start(pred[768]{0:T(1024)(128)(4,1)} %constant.296) | copy-start | bytes 2308
  44.3 5.6 %copy-start.15 = (pred[768]{0:T(1024)(128)(4,1)S(1)}, pred[768]{0:T(1024)(128)(4,1)}, u32[]{:S(2)}) copy-start(pred[768]{0:T(1024)(128)(4,1)} %constant.297) | copy-start | bytes 2308
  44.3 5.6 %copy-start.16 = (pred[768]{0:T(1024)(128)(4,1)S(1)}, pred[768]{0:T(1024)(128)(4,1)}, u32[]{:S(2)}) copy-start(pred[768]{0:T(1024)(128)(4,1)} %constant.298) | copy-start | bytes 2308
  44.3 5.6 %copy-start.17 = (pred[768]{0:T(1024)(128)(4,1)S(1)}, pred[768]{0:T(1024)(128)(4,1)}, u32[]{:S(2)}) copy-start(pred[768]{0:T(1024)(128)(4,1)} %constant.299) | copy-start | bytes 2308
  44.3 5.6 %copy-start.18 = (pred[768]{0:T(1024)(128)(4,1)S(1)}, pred[768]{0:T(1024)(128)(4,1)}, u32[]{:S(2)}) copy-start(pred[768]{0:T(1024)(128)(4,1)} %constant.300) | copy-start | bytes 2308
  44.3 5.6 %copy-start.19 = (pred[768]{0:T(1024)(128)(4,1)S(1)}, pred[768]{0:T(1024)(128)(4,1)}, u32[]{:S(2)}) copy-start(pred[768]{0:T(1024)(128)(4,1)} %constant.301) | copy-start | bytes 2308
  46.8 32.6 %collective-permute-start.10 = (bf16[4,96,2048]{2,1,0:T(8,128)(2,1)}, bf16[4,96,2048]{2,1,0:T(8,128)(2,1)}, u32[]{:S(2)}, u32[]{:S(2)}) collective-permute-start(bf16[4,96,2048]{2,1,0:T(8,128)(2,1)} %pad_maximum_fusion.1.refs_1_), channel_id=1, source_target_pairs={{0,24},{1,97},{2,26},{3,99},{4,28},{5,101},{6,30},{7,103},{8,0},{9... | collective-permute-start | bytes 4718600 | tf_op jit(solution)/shard_map/ppermute | solution.py:54
  47.4 32.1 %collective-permute-start.9 = (bf16[4,96,2048]{2,1,0:T(8,128)(2,1)}, bf16[4,96,2048]{2,1,0:T(8,128)(2,1)}, u32[]{:S(2)}, u32[]{:S(2)}) collective-permute-start(bf16[4,96,2048]{2,1,0:T(8,128)(2,1)} %pad_maximum_fusion.1.refs_1_), channel_id=1, source_target_pairs={{0,8},{1,33},{2,10},{3,35},{4,12},{5,37},{6,14},{7,39},{8,16},{9,4... | collective-permute-start | bytes 4718600 | tf_op jit(solution)/shard_map/ppermute | solution.py:54
  50.8 2.2 %copy-start = (bf16[512,4096]{1,0:T(8,128)(2,1)S(1)}, bf16[512,4096]{1,0:T(8,128)(2,1)}, u32[]{:S(2)}) copy-start(bf16[512,4096]{1,0:T(8,128)(2,1)} %all-gather.5.cloned.1.call-done) | copy-start | bytes 12582916
  53.0 28.9 %copy-start.1 = (bf16[512,4096]{1,0:T(8,128)(2,1)S(1)}, bf16[512,4096]{1,0:T(8,128)(2,1)}, u32[]{:S(2)}) copy-start(bf16[512,4096]{1,0:T(8,128)(2,1)} %all-gather.5.cloned.1.call-done) | copy-start | bytes 12582916
  79.4 25.4 %collective-permute-start.11 = (bf16[4,96,2048]{2,1,0:T(8,128)(2,1)}, bf16[4,96,2048]{2,1,0:T(8,128)(2,1)S(1)}, u32[]{:S(2)}, u32[]{:S(2)}) collective-permute-start(bf16[4,96,2048]{2,1,0:T(8,128)(2,1)} %collective-permute-done.7.refs_0_), channel_id=1, source_target_pairs={{0,8},{1,33},{2,10},{3,35},{4,12},{5,37},{6,14},{7,39},{8,16},{9,4... | collective-permute-start | bytes 4718600 | tf_op jit(solution)/shard_map/ppermute | solution.py:54
  81.8 26.5 %collective-permute-start.12 = (bf16[4,96,2048]{2,1,0:T(8,128)(2,1)}, bf16[4,96,2048]{2,1,0:T(8,128)(2,1)S(1)}, u32[]{:S(2)}, u32[]{:S(2)}) collective-permute-start(bf16[4,96,2048]{2,1,0:T(8,128)(2,1)} %collective-permute-done.10.refs_3_), channel_id=1, source_target_pairs={{0,24},{1,97},{2,26},{3,99},{4,28},{5,101},{6,30},{7,103},{8,0},{9... | collective-permute-start | bytes 4718600 | tf_op jit(solution)/shard_map/ppermute | solution.py:54
  104.8 11.1 %copy-start.3 = (bf16[4,96,2048]{2,1,0:T(8,128)(2,1)}, bf16[4,96,2048]{2,1,0:T(8,128)(2,1)S(1)}, u32[]{:S(2)}) copy-start(bf16[4,96,2048]{2,1,0:T(8,128)(2,1)S(1)} %collective-permute-done.11.refs_0_) | copy-start | bytes 4718596
  108.3 7.6 %copy-start.5 = (bf16[4,96,2048]{2,1,0:T(8,128)(2,1)}, bf16[4,96,2048]{2,1,0:T(8,128)(2,1)S(1)}, u32[]{:S(2)}) copy-start(bf16[4,96,2048]{2,1,0:T(8,128)(2,1)S(1)} %collective-permute-done.12.refs_1_) | copy-start | bytes 4718596
  115.9 12.3 %collective-permute-start.13 = (bf16[4,32,4096]{2,1,0:T(8,128)(2,1)}, bf16[4,32,4096]{2,1,0:T(8,128)(2,1)}, u32[]{:S(2)}, u32[]{:S(2)}) collective-permute-start(bf16[4,32,4096]{2,1,0:T(8,128)(2,1)} %shard_map.81), channel_id=1, source_target_pairs={{0,1},{1,0},{2,3},{3,2},{4,5},{5,4},{6,7},{7,6},{8,9},{9,8},{10,11... | collective-permute-start | bytes 3145736 | tf_op jit(solution)/shard_map/ppermute | solution.py:42
  116.0 3.4 %copy-start.4 = (bf16[4,96,2048]{2,1,0:T(8,128)(2,1)S(1)}, bf16[4,96,2048]{2,1,0:T(8,128)(2,1)}, u32[]{:S(2)}) copy-start(bf16[4,96,2048]{2,1,0:T(8,128)(2,1)} %copy-done.3) | copy-start | bytes 4718596
  116.0 3.3 %copy-start.6 = (bf16[4,96,2048]{2,1,0:T(8,128)(2,1)S(1)}, bf16[4,96,2048]{2,1,0:T(8,128)(2,1)}, u32[]{:S(2)}) copy-start(bf16[4,96,2048]{2,1,0:T(8,128)(2,1)} %copy-done.5) | copy-start | bytes 4718596
  118.8 21.3 %collective-permute-start.17 = (bf16[96,512]{1,0:T(8,128)(2,1)S(1)}, bf16[96,512]{1,0:T(8,128)(2,1)S(1)}, u32[]{:S(2)}, u32[]{:S(2)}) collective-permute-start(bf16[96,512]{1,0:T(8,128)(2,1)S(1)} %pad_maximum_fusion.4), channel_id=1, source_target_pairs={{0,1},{1,0},{2,3},{3,2},{4,5},{5,4},{6,7},{7,6},{8,9},{9,8},{10,11... | collective-permute-start | bytes 294920 | tf_op jit(solution)/shard_map/ppermute | solution.py:42
  119.3 2.2 %copy-start.2 = (bf16[512,4096]{1,0:T(8,128)(2,1)S(1)}, bf16[512,4096]{1,0:T(8,128)(2,1)}, u32[]{:S(2)}) copy-start(bf16[512,4096]{1,0:T(8,128)(2,1)} %all-gather.5.cloned.1.call-done) | copy-start | bytes 12582916
  129.5 29.4 %collective-permute-start.14 = (bf16[32,4096]{1,0:T(8,128)(2,1)S(1)}, bf16[32,4096]{1,0:T(8,128)(2,1)S(1)}, u32[]{:S(2)}, u32[]{:S(2)}) collective-permute-start(bf16[32,4096]{1,0:T(8,128)(2,1)S(1)} %get-tuple-element.44), channel_id=1, source_target_pairs={{0,4},{2,6},{4,0},{6,2},{1,5},{3,7},{5,1},{7,3},{8,12},{10,14},{12... | collective-permute-start | bytes 786440 | tf_op jit(solution)/shard_map/ppermute | solution.py:37
  135.8 23.1 %collective-permute-start.15 = (bf16[32,4096]{1,0:T(8,128)(2,1)S(1)}, bf16[32,4096]{1,0:T(8,128)(2,1)S(1)}, u32[]{:S(2)}, u32[]{:S(2)}) collective-permute-start(bf16[32,4096]{1,0:T(8,128)(2,1)S(1)} %get-tuple-element.43), channel_id=1, source_target_pairs={{0,2},{2,4},{4,6},{6,0},{1,3},{3,5},{5,7},{7,1},{8,10},{10,12},{12... | collective-permute-start | bytes 786440 | tf_op jit(solution)/shard_map/ppermute | solution.py:37
  135.8 23.1 %collective-permute-start.16 = (bf16[32,4096]{1,0:T(8,128)(2,1)S(1)}, bf16[32,4096]{1,0:T(8,128)(2,1)S(1)}, u32[]{:S(2)}, u32[]{:S(2)}) collective-permute-start(bf16[32,4096]{1,0:T(8,128)(2,1)S(1)} %get-tuple-element.42), channel_id=1, source_target_pairs={{0,6},{2,0},{4,2},{6,4},{1,7},{3,1},{5,3},{7,5},{8,14},{10,8},{12,... | collective-permute-start | bytes 786440 | tf_op jit(solution)/shard_map/ppermute | solution.py:37
  140.1 2.8 %copy-start.9 = (bf16[12288,256]{1,0:T(8,128)(2,1)S(1)}, bf16[12288,256]{1,0:T(8,128)(2,1)}, u32[]{:S(2)}) copy-start(bf16[12288,256]{1,0:T(8,128)(2,1)} %all-gather.7.cloned.1.call-done) | copy-start | bytes 18874372
Sparse Core Ops, SparseCore 0:
  9.7 34.4 all-gather.4
  47.9 68.1 all-gather.6

commit v4 on v2

v4 whole, which is shorter than its diff:
```python
import functools
import math

import jax
import jax.numpy as jnp
from jax import lax
from jax.experimental import pallas as pl
from jax.experimental.pallas import tpu as pltpu
from jax.sharding import Mesh, PartitionSpec as P

D = 64
RHS = 32
LEAF = 512
SKEL = 512
NEAR = 12
LEAVES_DEV = 8
P_DEV = LEAF * LEAVES_DEV
ROWS = D + RHS
N_DEV = 128
SIZES = {"z": 4, "x": 4, "y": 4, "core": 2}
AXES = ("z", "x", "y", "core")
DEPTH = D + 16
UNROLL = 4
GAIN = 2.0 * math.log2(math.e) / D
NEAR_SCALE = 4.0 / math.sqrt(LEAF * (NEAR + 1))
FAR_SCALE = 4.0 / math.sqrt(P_DEV * N_DEV)
CLASS = LEAVES_DEV // 2
LISTS = (96, 128, 32)
STARTS = (0, 96, 224)
SPARE = 8 * LEAVES_DEV


def shift(block, axis, by):
    count = SIZES[axis]
    return lax.ppermute(block, axis, [(i, (i + by) % count) for i in range(count)])


def swap(block, axis, bit):
    count = SIZES[axis]
    return lax.ppermute(block, axis, [(i, i ^ bit) for i in range(count)])


def ring(block, by, stage):
    route = []
    for flat in range(N_DEV):
        z, x, y, core = flat // 32, flat // 8 % 4, flat // 2 % 4, flat % 2
        if core == stage:
            z = (z + by) % 4
        else:
            x = (x + by) % 4
        route.append((flat, ((z * 4 + x) * 4 + y) * 2 + core))
    return lax.ppermute(block, AXES, route)


def put_points(aug, coords, first):
    width = coords.shape[1]
    aug[0:D, :] = coords
    wide = coords.astype(jnp.float32)
    rest = jnp.sum(wide * wide, axis=0, keepdims=True) * -0.5
    row = lax.broadcasted_iota(jnp.int32, (16, width), 0)
    rows = jnp.where(row < 6, 1.0, 0.0)
    for part in range(3):
        piece = rest.astype(jnp.bfloat16).astype(jnp.float32)
        rest = rest - piece
        rows = jnp.where(row == first + part, piece, rows)
    aug[D:, :] = rows.astype(jnp.bfloat16)


def tile_apply(source_aug, target_aug, source_w):
    power = lax.dot_general(
        source_aug, target_aug, (((0,), (0,)), ((), ())), preferred_element_type=jnp.float32
    )
    tile = jnp.exp2(power * GAIN).astype(jnp.bfloat16)
    return jnp.dot(source_w, tile, preferred_element_type=jnp.float32)


def cost(entries, moved):
    return pl.CostEstimate(
        flops=int(entries) * 16 * (DEPTH + RHS), transcendentals=int(entries), bytes_accessed=moved
    )


VMEM = pl.BlockSpec(memory_space=pltpu.VMEM)
SMEM = pl.BlockSpec(memory_space=pltpu.SMEM)
ANY = pl.BlockSpec(memory_space=pl.ANY)


def self_kernel(points_ref, weights_ref, out_ref, target_aug, source_aug):
    @pl.loop(0, LEAVES_DEV // UNROLL)
    def _(group):
        for unit in range(UNROLL):
            start = pl.multiple_of((group * UNROLL + unit) * LEAF, LEAF)
            cols = pl.ds(start, LEAF)
            put_points(source_aug.at[unit], points_ref[:, cols], 0)
            put_points(target_aug.at[unit], points_ref[:, cols], 3)
            out_ref[:, cols] = tile_apply(source_aug[unit], target_aug[unit], weights_ref[:, cols])


def self_terms(points, weights):
    return pl.pallas_call(
        self_kernel,
        out_shape=jax.ShapeDtypeStruct((RHS, P_DEV), jnp.float32),
        in_specs=[VMEM, VMEM],
        out_specs=VMEM,
        scratch_shapes=[pltpu.VMEM((UNROLL, DEPTH, LEAF), jnp.bfloat16)] * 2,
        compiler_params=pltpu.CompilerParams(vmem_limit_bytes=24 << 20),
        cost_estimate=cost(LEAF * P_DEV, 2 << 20),
    )(points, weights)


def put_node(ref, coords_ref, heavy_ref, start, depth):
    half = SKEL // 2
    for side in range(2):
        cols = slice(side * half, (side + 1) * half)
        lead = start + side * (1 << (depth - 1))
        coords_ref[:, cols] = ref[lead, 0:D, 0:half]
        total = jnp.zeros((RHS, half), jnp.float32)
        for at in range(1 << (depth - 1)):
            heavy = ref[lead + at, D:ROWS].astype(jnp.float32)
            total = total + (heavy if ref.shape[-1] == half else heavy[:, :half] + heavy[:, half:])
        heavy_ref[:, cols] = total.astype(jnp.bfloat16)


def merge_kernel(nodes_ref, node_ref, out_ref):
    half = SKEL // 2
    put_node(nodes_ref, node_ref.at[0:D], node_ref.at[D:ROWS], 0, 3)
    heavy = node_ref[D:ROWS].astype(jnp.float32)
    out_ref[0, 0:D] = node_ref[0:D, 0:half]
    out_ref[0, D:ROWS] = (heavy[:, :half] + heavy[:, half:]).astype(jnp.bfloat16)
    for copy in range(1, 16):
        out_ref[copy] = out_ref[0]


def merge(nodes):
    return pl.pallas_call(
        merge_kernel,
        out_shape=(
            jax.ShapeDtypeStruct((ROWS, SKEL), jnp.bfloat16),
            jax.ShapeDtypeStruct((16, ROWS, SKEL // 2), jnp.bfloat16),
        ),
        in_specs=[VMEM],
        out_specs=(VMEM, VMEM),
        compiler_params=pltpu.CompilerParams(vmem_limit_bytes=8 << 20),
        cost_estimate=cost(0, 1 << 20),
    )(nodes)


def far_kernel(depths, seeded, place_ref, points_ref, sibling_ref, nodes_ref, *refs):
    if seeded:
        seed_ref, refs = refs[0], refs[1:]
    far_ref, coords, heavy, target_aug, source_aug = refs
    for leaf in range(LEAVES_DEV):
        cols = slice(leaf * LEAF, (leaf + 1) * LEAF)
        put_points(target_aug.at[:, cols], points_ref[:, cols], 3)
    coords[0] = sibling_ref[0:D]
    heavy[0] = sibling_ref[D:ROWS]
    for depth in range(1, depths):
        start = ((place_ref[0] >> depth) ^ 1) << depth
        put_node(nodes_ref, coords.at[depth], heavy.at[depth], start, depth)
    far_ref[...] = seed_ref[...] if seeded else jnp.zeros_like(far_ref)

    @pl.loop(0, depths)
    def _(at):
        put_points(source_aug, coords[at], 0)
        far_ref[...] += tile_apply(source_aug[...], target_aug[...], heavy[at])

    if seeded:
        far_ref[...] = far_ref[...] * FAR_SCALE


def far_terms(place, points, sibling, nodes, depths, seed=None):
    seeds = [] if seed is None else [seed]
    return pl.pallas_call(
        functools.partial(far_kernel, depths, seed is not None),
        out_shape=jax.ShapeDtypeStruct((RHS, P_DEV), jnp.float32),
        in_specs=[SMEM, VMEM, VMEM, VMEM] + [VMEM] * len(seeds),
        out_specs=VMEM,
        scratch_shapes=[
            pltpu.VMEM((depths, D, SKEL), jnp.bfloat16),
            pltpu.VMEM((depths, RHS, SKEL), jnp.bfloat16),
            pltpu.VMEM((DEPTH, P_DEV), jnp.bfloat16),
            pltpu.VMEM((DEPTH, SKEL), jnp.bfloat16),
        ],
        compiler_params=pltpu.CompilerParams(vmem_limit_bytes=24 << 20),
        cost_estimate=cost(depths * SKEL * P_DEV, 4 << 20),
    )(place.reshape(1), points, sibling, nodes, *seeds)


def near_kernel(first, devices, n_source, seeded, pair_ref, count_ref, other_ref, line_ref, *refs):
    source_refs, refs = refs[:n_source], refs[n_source:]
    if seeded:
        seed_ref, refs = refs[0], refs[1:]
    out_ref, buf, target_buf, sem, whole_sem, target_aug, source_aug, acc = refs
    groups = (count_ref[0] + (UNROLL - 1)) // UNROLL

    def fetch(group, slot):
        for unit in range(UNROLL):
            code = pair_ref[group * UNROLL + unit]
            target = jnp.minimum(code // (32 * CLASS), SPARE - 1)
            start = pl.multiple_of(target % LEAVES_DEV * LEAF, LEAF)
            device = target // LEAVES_DEV
            for ref, here in ((other_ref, device < 4), (line_ref, device >= 4)):

                @pl.when(here)
                def _(ref=ref):
                    pltpu.make_async_copy(
                        ref.at[device % 4, :, pl.ds(start, LEAF)],
                        target_buf.at[slot, unit],
                        sem.at[slot, unit, 1],
                    ).start()

            which = code // (4 * CLASS) % 8
            start = pl.multiple_of(code % CLASS * LEAF, LEAF)
            for at in range(n_source):

                @pl.when(which == at)
                def _():
                    pltpu.make_async_copy(
                        source_refs[at].at[code // CLASS % 4, :, pl.ds(start, LEAF)],
                        buf.at[slot, unit],
                        sem.at[slot, unit, 0],
                    ).start()

    def arrive(slot):
        for unit in range(UNROLL):
            pltpu.make_async_copy(
                source_refs[0].at[0, :, pl.ds(0, LEAF)], buf.at[slot, unit], sem.at[slot, unit, 0]
            ).wait()
            pltpu.make_async_copy(
                line_ref.at[0, :, pl.ds(0, LEAF)], target_buf.at[slot, unit], sem.at[slot, unit, 1]
            ).wait()

    @pl.when(groups > 0)
    def _():
        fetch(0, 0)

    total = acc.at[pl.ds(0, devices)]
    if seeded:
        seed = pltpu.make_async_copy(seed_ref, total, whole_sem)
        seed.start()
        seed.wait()
    else:
        acc[...] = jnp.zeros_like(acc)

    @pl.loop(0, groups)
    def _(group):
        slot = group % 2

        @pl.when(group + 1 < groups)
        def _():
            fetch(group + 1, 1 - slot)

        arrive(slot)
        for unit in range(UNROLL):
            target = pair_ref[group * UNROLL + unit] // (32 * CLASS)
            put_points(source_aug.at[unit], buf[slot, unit, 0:D], 0)
            put_points(target_aug.at[unit], target_buf[slot, unit], 3)
            start = pl.multiple_of(target % LEAVES_DEV * LEAF, LEAF)
            acc[jnp.minimum(target // LEAVES_DEV - first, devices), :, pl.ds(start, LEAF)] += tile_apply(
                source_aug[unit], target_aug[unit], buf[slot, unit, D:ROWS]
            )

    if out_ref.dtype == jnp.float32:
        result = pltpu.make_async_copy(total, out_ref, whole_sem)
        result.start()
        result.wait()
    else:
        out_ref[...] = total[...].astype(out_ref.dtype)


def near_part(pairs, count, targets, sources, first, devices, seed, dtype, expected):
    seeds = [] if seed is None else [seed]
    return pl.pallas_call(
        functools.partial(near_kernel, first, devices, len(sources), seed is not None),
        out_shape=jax.ShapeDtypeStruct((devices, RHS, P_DEV), dtype),
        in_specs=[SMEM, SMEM, ANY, ANY] + [ANY] * len(sources) + [ANY] * len(seeds),
        out_specs=ANY if dtype == jnp.float32 else VMEM,
        scratch_shapes=[
            pltpu.VMEM((2, UNROLL, ROWS, LEAF), jnp.bfloat16),
            pltpu.VMEM((2, UNROLL, D, LEAF), jnp.bfloat16),
            pltpu.SemaphoreType.DMA((2, UNROLL, 2)),
            pltpu.SemaphoreType.DMA,
            pltpu.VMEM((UNROLL, DEPTH, LEAF), jnp.bfloat16),
            pltpu.VMEM((UNROLL, DEPTH, LEAF), jnp.bfloat16),
            pltpu.VMEM((devices + 1, RHS, P_DEV), jnp.float32),
        ],
        compiler_params=pltpu.CompilerParams(vmem_limit_bytes=32 << 20),
        cost_estimate=cost(expected * LEAF * LEAF, 8 << 20),
    )(pairs, count, *targets, *sources, *seeds)


def exchange(copies, axis):
    return lax.all_to_all(copies, axis, split_axis=0, concat_axis=0, tiled=True)


def everyone(block, axes):
    count = math.prod(SIZES[axis] for axis in axes)
    return exchange(jnp.broadcast_to(block[None], (count, *block.shape)), axes)


def pair_lists(near_leaf, near_count, place):
    rows, counts = [], []
    for core in (1 - place["core"], place["core"]):
        for y in range(SIZES["y"]):
            device = ((place["z"] * 4 + place["x"]) * 4 + y) * 2 + core
            rows.append(lax.dynamic_slice_in_dim(near_leaf, device * LEAVES_DEV, LEAVES_DEV))
            counts.append(lax.dynamic_slice_in_dim(near_count, device * LEAVES_DEV, LEAVES_DEV))
    leaf_ids = jnp.concatenate(rows, axis=0).reshape(-1)
    used = jnp.arange(NEAR, dtype=jnp.int32)[None, :] < jnp.concatenate(counts, axis=0)[:, None]
    used = used.reshape(-1)
    owner, local = leaf_ids // LEAVES_DEV, leaf_ids % LEAVES_DEV
    valid = used & (owner // 2 % 4 == place["y"]) & (local // CLASS == place["core"])
    back_z, back_x = (place["z"] - owner // 32) % 4, (place["x"] - owner // 8) % 4
    on_z = place["core"] == 0
    inner, outer = jnp.where(on_z, back_z, back_x), jnp.where(on_z, back_x, back_z)
    inner, outer = (jnp.where(back == 0, 0, jnp.where(back == 1, 1, 5 - back)) for back in (inner, outer))
    other = (owner % 2 != place["core"]).astype(jnp.int32)
    at = jnp.arange(leaf_ids.shape[0], dtype=jnp.int32)
    target = at // NEAR
    first = target < SPARE // 2
    which = outer * 2 + other - jnp.where((outer == 3) & ~first, 6, 0)
    code = ((target * 8 + which) * 4 + inner) * CLASS + local % CLASS
    group = jnp.where(first, 1, jnp.where(outer == 3, 2, 0))
    group = jnp.where(valid, group, -1)
    rank = jnp.sum(((group[None, :] == group[:, None]) & (at[None, :] < at[:, None])).astype(jnp.int32), axis=1)
    base = jnp.zeros_like(group)
    for index, start in enumerate(STARTS):
        base = jnp.where(group == index, start, base)
    goal = jnp.where(valid, base + rank, -1)
    place_at = jnp.arange(sum(LISTS), dtype=jnp.int32)
    hit = goal[None, :] == place_at[:, None]
    packed = jnp.sum(jnp.where(hit, code[None, :] + 1, 0), axis=1)
    packed = jnp.where(packed == 0, SPARE * 32 * CLASS, packed - 1)
    totals = jnp.sum((group[None, :] == jnp.arange(len(LISTS), dtype=jnp.int32)[:, None]).astype(jnp.int32), axis=1)
    return (
        [packed[s : s + n] for s, n in zip(STARTS, LISTS)],
        [totals[i : i + 1] for i in range(len(LISTS))],
    )


def spread(own, other, stage):
    ahead, behind_other = ring(own, 1, stage), ring(other, -1, stage)
    ahead_other, behind = ring(other, 1, stage), ring(own, -1, stage)
    return (ahead, behind), (ahead_other, behind_other)


def spread_on(own, other, stage):
    return ring(own[0], 1, stage), ring(other[1], -1, stage)


def leaf_class(points, weights, which):
    width = CLASS * LEAF
    return jnp.concatenate(
        [lax.dynamic_slice_in_dim(a, which * width, width, axis=1) for a in (points, weights)], axis=0
    )


def per_device(points, weights, skel_index, assign, near_leaf, near_count):
    place = {axis: lax.axis_index(axis) for axis in AXES}
    core = place["core"]
    mine = leaf_class(points, weights, core)
    theirs = swap(leaf_class(points, weights, 1 - core), "core", 1)
    own, other = spread(mine, theirs, 0)
    _, _, points_later = lax.optimization_barrier((own, other, points))
    own_far, other_far = spread_on(own, other, 0)
    line = everyone(points_later, ("y",))
    own_far, other_far = lax.optimization_barrier((own_far, other_far))
    own_line = jnp.stack([mine, *own, own_far])
    other_line = jnp.stack([theirs, *other, other_far])
    own, other = spread(own_line, other_line, 1)

    _, _, assign, skel_index = lax.optimization_barrier((own_line, other_line, assign, skel_index))
    member = (assign[None, :] == jnp.arange(SKEL, dtype=jnp.int32)[:, None]).astype(jnp.bfloat16)
    base_weights = lax.dot_general(
        weights, member, (((1,), (1,)), ((), ())), preferred_element_type=jnp.float32
    ).astype(jnp.bfloat16)
    base = jnp.concatenate([points[:, skel_index], base_weights], axis=0)
    near_nodes = everyone(base, ("y", "core"))
    targets = (swap(line, "core", 1), line)
    node, copies = merge(near_nodes)
    in_line = place["y"] * 2 + core
    core_sibling = lax.dynamic_index_in_dim(near_nodes, in_line ^ 1, 0, keepdims=False)

    pairs, totals = pair_lists(near_leaf, near_count, place)
    early = [own_line, other_line, own[0], other[0], own[1], other[1]]
    late = spread_on(own, other, 1)
    home = near_part(pairs[0], totals[0], (line, line), early, 4, 4, None, jnp.float32, 36)
    cross_pairs, home, copies, node = lax.optimization_barrier((pairs[1], home, copies, node))
    x_sibling = swap(node, "x", 1)
    wide_nodes = exchange(copies, ("z", "x"))
    across = near_part(cross_pairs, totals[1], targets, [*early, *late], 0, 4, None, jnp.bfloat16, 48)
    last_pairs, across, x_sibling, wide_nodes = lax.optimization_barrier((pairs[2], across, x_sibling, wide_nodes))
    across = swap(across, "core", 1)
    home = near_part(last_pairs, totals[2], (line, line), late, 4, 4, home, jnp.float32, 12)
    parts = exchange((home + across.astype(jnp.float32)).astype(jnp.bfloat16), "y")
    _, points_later = lax.optimization_barrier((home, points))
    self_sum = self_terms(points_later, weights)
    far_field = far_terms(in_line, points, core_sibling, near_nodes, 3)
    far_field = far_terms(place["z"] * 4 + place["x"], points, x_sibling, wide_nodes, 4, far_field)
    parts, far_field, self_sum = lax.optimization_barrier((parts, far_field, self_sum))
    near_sum = self_sum + jnp.sum(parts.astype(jnp.float32), axis=0)
    return (near_sum * NEAR_SCALE, far_field)


def solution(mesh):
    grid = Mesh(mesh.devices.reshape([SIZES[axis] for axis in AXES]), AXES)
    split = P(None, AXES)
    return jax.shard_map(
        per_device,
        mesh=grid,
        in_specs=(split, split, P(AXES), P(AXES), P(), P()),
        out_specs=(split, split),
        check_vma=False,
    )
```

time: 201 us -> 164 us (0.82)
  waiting for transfers between devices: 80 us -> 34.3 us
  local copies, waits for them, and re-layouts: 8.18 us -> 15.5 us
  other arithmetic: 5.96 us -> 8.31 us
    ppermute x10 -> x4, waiting for transfers between devices: 40.8 us -> 0.01 us  [swap(): return lax.ppermute(block, axis, [(i, i ^ bit) for i in range(count)])]
    all_to_all x0 -> x4, starting transfers between devices: none -> 23 us  [exchange(): return lax.all_to_all(copies, axis, split_axis=0, concat_axis=0, tiled=True)]
    ppermute x12, waiting for transfers between devices: 39.3 us -> 20.2 us  [ring(): return lax.ppermute(block, AXES, route)]
    ppermute x6 -> x0, starting transfers between devices: 14.9 us -> none  [shift(): lax.ppermute(block, axis, [(i, (i + by) % count) for i in range(count)])]
    all_to_all x0 -> x4, waiting for transfers between devices: none -> 14.1 us  [exchange(): return lax.all_to_all(copies, axis, split_axis=0, concat_axis=0, tiled=True)]
    ppermute x10 -> x4, starting transfers between devices: 12.6 us -> 2.42 us  [swap(): return lax.ppermute(block, axis, [(i, i ^ bit) for i in range(count)])]
    unnamed x31 -> x39, local copies, waits for them, and re-layouts: 1.93 us -> 6.66 us
    broadcast_in_dim x0 -> x2, local copies, waits for them, and re-layouts: none -> 2.58 us  [everyone(): return exchange(jnp.broadcast_to(block[None], (count, *block.shape)), axes)]
  transfers between devices with their start and end apart: 28 -> 20, of which waited for: 9 -> 8; matrix products, arithmetic and copies ran while one was open for 7% -> 10% of each run, Pallas kernels for 30% -> 37%
where the time goes in v4:
time: 164 us; the launch traced here: 163 us
  Pallas kernels  60.2 us (37%)
  starting transfers between devices  42.1 us (26%)
  waiting for transfers between devices  34.3 us (21%)
  local copies, waits for them, and re-layouts  15.5 us (9%)
  other arithmetic  8.31 us (5%)
    pallas_call x3, Pallas kernels, near_part(): pl.pallas_call(functools.partial(near_kernel, first, devices, len(sources...  41.2 us
    all_to_all x4, starting transfers between devices, exchange(): return lax.all_to_all(copies, axis, split_axis=0, concat_axis=0, tiled=True)  23 us
    ppermute x12, waiting for transfers between devices, ring(): return lax.ppermute(block, AXES, route)  20.2 us
    ppermute x12, starting transfers between devices, ring(): return lax.ppermute(block, AXES, route)  16.7 us
    pallas_call x2, Pallas kernels, far_terms(): pl.pallas_call(functools.partial(far_kernel, depths, seed is not None), o...  16.2 us
    all_to_all x4, waiting for transfers between devices, exchange(): return lax.all_to_all(copies, axis, split_axis=0, concat_axis=0, tiled=True)  14.1 us
    unnamed x39, local copies, waits for them, and re-layouts  6.66 us
  transfers between devices with their start and end apart: 20, of which 8 were waited for; matrix products, arithmetic and copies ran while one was open for 10% of the time, Pallas kernels for 37%

profile of v4, /device:TPU:0, one launch (start us, length us, event | category | flops | bytes accessed | tf_op | source)
XLA Modules:
  0.0 162.9 jit_solution(8340765481978227204)
XLA Ops:
  0.6 1.0 constant_dynamic-slice_fusion
  1.7 1.1 constant_dynamic-slice_fusion.1
  3.0 4.2 %collective-permute-start.1 = (bf16[96,2048]{1,0:T(8,128)(2,1)S(1)}, bf16[96,2048]{1,0:T(8,128)(2,1)S(1)}, u32[]{:S(2)}, u32[]{:S(2)}) collective-permute-start(bf16[96,2048]{1,0:T(8,128)(2,1)S(1)} %get-tuple-element.46), channel_id=1, source_target_pairs={{0,96},{1,25},{2,98},{3,27},{4,100},{5,29},{6,102},{7,31},{8,104},... | collective-permute-start | bytes 1179656 | tf_op jit(solution)/shard_map/ppermute | solution.py:52
  7.2 3.2 %collective-permute-start.4 = (bf16[96,2048]{1,0:T(8,128)(2,1)S(1)}, bf16[96,2048]{1,0:T(8,128)(2,1)S(1)}, u32[]{:S(2)}, u32[]{:S(2)}) collective-permute-start(bf16[96,2048]{1,0:T(8,128)(2,1)S(1)} %collective-permute-done.2), channel_id=1, source_target_pairs={{0,96},{1,25},{2,98},{3,27},{4,100},{5,29},{6,102},{7,31},{8,104},... | collective-permute-start | bytes 1179656 | tf_op jit(solution)/shard_map/ppermute | solution.py:52
  10.6 1.3 copy.16
  12.0 0.1 lt.150
  12.6 3.7 %collective-permute-done = bf16[96,2048]{1,0:T(8,128)(2,1)} collective-permute-done((bf16[96,2048]{1,0:T(8,128)(2,1)S(1)}, bf16[96,2048]{1,0:T(8,128)(2,1)}, u32[]{:S(2)}, u32[]{:S(2)}) %collective-permute-start) | collective-permute-done | bytes 393248 | tf_op jit(solution)/shard_map/ppermute | solution.py:52
  16.3 0.4 collective-permute-done.4
  16.7 3.7 %collective-permute-done.3 = bf16[96,2048]{1,0:T(8,128)(2,1)S(1)} collective-permute-done((bf16[96,2048]{1,0:T(8,128)(2,1)S(1)}, bf16[96,2048]{1,0:T(8,128)(2,1)S(1)}, u32[]{:S(2)}, u32[]{:S(2)}) %collective-permute-start.3) | collective-permute-done | bytes 393248 | tf_op jit(solution)/shard_map/ppermute | solution.py:52
  20.4 1.6 broadcast_in_dim.77
  22.0 4.5 %all-to-all-start = ((bf16[4,64,4096]{2,1,0:T(8,128)(2,1)}), bf16[4,64,4096]{2,1,0:T(8,128)(2,1)S(1)}, u32[]{:S(2)}, u32[]{:S(2)}) async-start(bf16[4,64,4096]{2,1,0:T(8,128)(2,1)} %broadcast_in_dim.77), calls=%async_computation | async-start | bytes 4194304 | tf_op jit(solution)/shard_map/all_to_all | solution.py:293
  26.6 0.4 convert_reduce_fusion
  26.9 7.6 %collective-permute-done.6 = bf16[96,2048]{1,0:T(8,128)(2,1)S(1)} collective-permute-done((bf16[96,2048]{1,0:T(8,128)(2,1)}, bf16[96,2048]{1,0:T(8,128)(2,1)S(1)}, u32[]{:S(2)}, u32[]{:S(2)}) %collective-permute-start.6) | collective-permute-done | bytes 393248 | tf_op jit(solution)/shard_map/ppermute | solution.py:52
  34.5 2.6 %pad_maximum_fusion.1.refs_1_ = bf16[4,96,2048]{2,1,0:T(8,128)(2,1)} fusion(bf16[1,96,2048]{2,1,0:T(8,128)(2,1)S(1)} %bitcast.21, bf16[1,96,2048]{2,1,0:T(8,128)(2,1)} %bitcast.19, bf16[1,96,2048]{2,1,0:T(8,128)(2,1)} %bitcast.20, bf16[1,96,2048]{2,1,0:T(8,128)(2,1)} %bitcast.18), kind=kLoop, calls=%fused_computation.10 | loop fusion | flops 2359296 | bytes 3145728 | tf_op jit(solution)/shard_map/stack | solution.py:369
  37.1 2.8 %collective-permute-start.10 = (bf16[4,96,2048]{2,1,0:T(8,128)(2,1)}, bf16[4,96,2048]{2,1,0:T(8,128)(2,1)}, u32[]{:S(2)}, u32[]{:S(2)}) collective-permute-start(bf16[4,96,2048]{2,1,0:T(8,128)(2,1)} %pad_maximum_fusion.1.refs_1_), channel_id=1, source_target_pairs={{0,24},{1,97},{2,26},{3,99},{4,28},{5,101},{6,30},{7,103},{8,0},{9... | collective-permute-start | bytes 4718600 | tf_op jit(solution)/shard_map/ppermute | solution.py:52
  39.9 2.5 %pad_maximum_fusion.refs_0_ = bf16[4,96,2048]{2,1,0:T(8,128)(2,1)} fusion(bf16[1,96,2048]{2,1,0:T(8,128)(2,1)} %bitcast.3, bf16[1,96,2048]{2,1,0:T(8,128)(2,1)S(1)} %bitcast.17, bf16[1,96,2048]{2,1,0:T(8,128)(2,1)} %bitcast.1, bf16[1,96,2048]{2,1,0:T(8,128)(2,1)S(1)} %get-tuple-element.45), kind=kLoop, calls=%fused_computation.9 | loop fusion | flops 2359296 | bytes 3145728 | tf_op jit(solution)/shard_map/stack | solution.py:368
  42.3 3.2 %collective-permute-start.9 = (bf16[4,96,2048]{2,1,0:T(8,128)(2,1)}, bf16[4,96,2048]{2,1,0:T(8,128)(2,1)}, u32[]{:S(2)}, u32[]{:S(2)}) collective-permute-start(bf16[4,96,2048]{2,1,0:T(8,128)(2,1)} %pad_maximum_fusion.refs_0_), channel_id=1, source_target_pairs={{0,24},{1,97},{2,26},{3,99},{4,28},{5,101},{6,30},{7,103},{8,0},{9... | collective-permute-start | bytes 4718600 | tf_op jit(solution)/shard_map/ppermute | solution.py:52
  45.6 1.5 fusion.4
  47.1 0.1 copy.17
  47.3 2.4 %gather_fusion = bf16[512,64]{1,0:T(8,128)(2,1)S(1)} fusion(bf16[64,4096]{0,1:T(8,128)(2,1)} %copy.16, s32[1024]{0:T(1024)S(1)} %pad_clamp_fusion), kind=kCustom, calls=%fused_computation | custom fusion | bytes 133120 | tf_op jit(solution)/shard_map/gather | solution.py:377
  49.9 1.1 all-to-all-done.other_ref.line_ref
  51.1 1.0 broadcast_in_dim.79
  52.1 3.7 %all-to-all-start.1 = ((bf16[8,96,512]{2,1,0:T(8,128)(2,1)}), bf16[8,96,512]{2,1,0:T(8,128)(2,1)S(1)}, u32[]{:S(2)}, u32[]{:S(2)}) async-start(bf16[8,96,512]{2,1,0:T(8,128)(2,1)} %broadcast_in_dim.79), calls=%async_computation.1 | async-start | bytes 1572864 | tf_op jit(solution)/shard_map/all_to_all | solution.py:293
  55.8 0.2 select_reduce_fusion
  55.9 0.6 collective-permute-start.11
  56.8 0.6 fusion.34
  57.4 11.5 %all-to-all-done.1.nodes_ref = bf16[8,96,512]{2,1,0:T(8,128)(2,1)S(1)} async-done(((bf16[8,96,512]{2,1,0:T(8,128)(2,1)}), bf16[8,96,512]{2,1,0:T(8,128)(2,1)S(1)}, u32[]{:S(2)}, u32[]{:S(2)}) %all-to-all-start.1) | async-done | bytes 786464 | tf_op jit(solution)/shard_map/all_to_all | solution.py:293
  69.0 0.9 copy-done.1
  69.9 0.6 copy-done.7
  70.5 3.3 %collective-permute-start.13 = (bf16[4,96,2048]{2,1,0:T(8,128)(2,1)}, bf16[4,96,2048]{2,1,0:T(8,128)(2,1)}, u32[]{:S(2)}, u32[]{:S(2)}) collective-permute-start(bf16[4,96,2048]{2,1,0:T(8,128)(2,1)} %collective-permute-done.10.refs_5_), channel_id=1, source_target_pairs={{0,24},{1,97},{2,26},{3,99},{4,28},{5,101},{6,30},{7,103},{8,0},{9... | collective-permute-start | bytes 4718600 | tf_op jit(solution)/shard_map/ppermute | solution.py:52
  73.8 4.8 %collective-permute-done.7.refs_2_ = bf16[4,96,2048]{2,1,0:T(8,128)(2,1)} collective-permute-done((bf16[4,96,2048]{2,1,0:T(8,128)(2,1)}, bf16[4,96,2048]{2,1,0:T(8,128)(2,1)}, u32[]{:S(2)}, u32[]{:S(2)}) %collective-permute-start.7) | collective-permute-done | bytes 1572896 | tf_op jit(solution)/shard_map/ppermute | solution.py:52
  78.7 16.7 %shard_map.77.refs_2_ = f32[4,32,4096]{2,1,0:T(8,128)S(1)} custom-call(s32[96]{0:T(128)S(1)} %slice.20.pair_ref, s32[1]{0:T(128)} %get-tuple-element.69.count_ref, bf16[4,64,4096]{2,1,0:T(8,128)(2,1)S(1)} %all-to-all-done.other_ref.line_ref, bf16[4,64,4096]{2,1,0:T(8,128)(2,1)S(1)} %all-to-all-done.other_ref.line_ref, ...), custom_call_target="tpu_custom_call" | custom-call | flops 16911433728 | bytes 8388608 | tf_op jit(solution)/shard_map/pallas_call | solution.py:273
  95.4 1.3 copy-done.8
  96.7 4.3 %all-to-all-start.2 = ((bf16[16,96,256]{2,1,0:T(8,128)(2,1)}), bf16[16,96,256]{2,1,0:T(8,128)(2,1)}, u32[]{:S(2)}, u32[]{:S(2)}) async-start(bf16[16,96,256]{2,1,0:T(8,128)(2,1)} %copy-done.1), calls=%async_computation.2 | async-start | bytes 1572864 | tf_op jit(solution)/shard_map/all_to_all | solution.py:293
  101.0 1.8 %collective-permute-start.14 = (bf16[96,512]{1,0:T(8,128)(2,1)}, bf16[96,512]{1,0:T(8,128)(2,1)S(1)}, u32[]{:S(2)}, u32[]{:S(2)}) collective-permute-start(bf16[96,512]{1,0:T(8,128)(2,1)} %copy-done.7), channel_id=1, source_target_pairs={{0,8},{8,0},{16,24},{24,16},{1,9},{9,1},{17,25},{25,17},{2,10},{10... | collective-permute-start | bytes 294920 | tf_op jit(solution)/shard_map/ppermute | solution.py:40
  102.7 17.5 %shard_map.79 = bf16[4,32,4096]{2,1,0:T(8,128)(2,1)S(1)} custom-call(s32[128]{0:T(128)S(1)} %slice.19.pair_ref, s32[1]{0:T(128)} %get-tuple-element.68.count_ref, bf16[4,64,4096]{2,1,0:T(8,128)(2,1)} %collective-permute-done.11.other_ref, bf16[4,64,4096]{2,1,0:T(8,128)(2,1)S(1)} %all-to-all-done.other_ref.line_ref, ...), custom_call_target="tpu_custom_call" | custom-call | flops 22548578304 | bytes 8388608 | tf_op jit(solution)/shard_map/pallas_call | solution.py:273
  120.3 1.0 copy-done.4
  121.3 0.6 copy-done.5
  121.9 6.1 %shard_map.81.refs_0_ = f32[32,4096]{1,0:T(8,128)S(1)} custom-call(s32[1]{0:T(128)} %bitcast.11.place_ref, bf16[64,4096]{1,0:T(8,128)(2,1)S(1)} %copy-done, bf16[96,512]{1,0:T(8,128)(2,1)S(1)} %dynamic-slice_bitcast_fusion.sibling_ref, bf16[8,96,512]{2,1,0:T(8,128)(2,1)S(1)} %all-to-all-done.1.nodes_ref), custom_call_target="tpu_custom_call" | custom-call | flops 11274289152 | bytes 4194304 | tf_op jit(solution)/shard_map/pallas_call | solution.py:173
  128.0 0.8 copy-done.10
  128.8 7.0 %shard_map.80 = f32[4,32,4096]{2,1,0:T(8,128)S(1)} custom-call(s32[32]{0:T(128)S(1)} %slice.18.pair_ref, s32[1]{0:T(128)} %get-tuple-element.67.count_ref, bf16[4,64,4096]{2,1,0:T(8,128)(2,1)S(1)} %all-to-all-done.other_ref.line_ref, bf16[4,64,4096]{2,1,0:T(8,128)(2,1)S(1)} %all-to-all-done.other_ref.line_ref, ...), custom_call_target="tpu_custom_call" | custom-call | flops 5637144576 | bytes 8388608 | tf_op jit(solution)/shard_map/pallas_call | solution.py:273
  135.8 1.2 add_convert_fusion
  137.0 10.5 %all-to-all-start.3 = ((bf16[4,32,4096]{2,1,0:T(8,128)(2,1)}), bf16[4,32,4096]{2,1,0:T(8,128)(2,1)S(1)}, u32[]{:S(2)}, u32[]{:S(2)}) async-start(bf16[4,32,4096]{2,1,0:T(8,128)(2,1)} %add_convert_fusion), calls=%async_computation.3 | async-start | bytes 2097152 | tf_op jit(solution)/shard_map/all_to_all | solution.py:293
  147.5 10.1 %shard_map.82 = f32[32,4096]{1,0:T(8,128)} custom-call(s32[1]{0:T(128)} %bitcast.10.place_ref, bf16[64,4096]{1,0:T(8,128)(2,1)S(1)} %copy-done, bf16[96,512]{1,0:T(8,128)(2,1)S(1)} %copy-done.6, bf16[16,96,256]{2,1,0:T(8,128)(2,1)} %all-to-all-done.2.nodes_ref, f32[32,4096]{1,0:T(8,128)S(1)} %copy-done.11), custom_call_target="tpu_custom_call" | custom-call | flops 15032385536 | bytes 4194304 | tf_op jit(solution)/shard_map/pallas_call | solution.py:173
  157.6 2.8 %shard_map.83 = f32[32,4096]{1,0:T(8,128)S(1)} custom-call(bf16[64,4096]{1,0:T(8,128)(2,1)S(1)} %copy-done, bf16[32,4096]{1,0:T(8,128)(2,1)S(1)} %copy-done.3), custom_call_target="tpu_custom_call" | custom-call | flops 3758096384 | bytes 2097152 | tf_op jit(solution)/shard_map/pallas_call | solution.py:100
  160.4 1.5 all-to-all-done.3
  161.8 0.2 convert_reduce_fusion.1
  162.0 0.9 add_multiply_fusion
  (75 shorter events, 1.6 us)
Async XLA Ops:
  1.6 8.8 %copy-start.16 = (s32[1024]{0:T(1024)S(1)}, s32[1024]{0:T(1024)}, u32[]{:S(2)}) copy-start(s32[1024]{0:T(1024)} %param.11) | copy-start | bytes 12292
  1.6 8.9 %copy-start = (bf16[64,4096]{1,0:T(8,128)(2,1)S(1)}, bf16[64,4096]{1,0:T(8,128)(2,1)}, u32[]{:S(2)}) copy-start(bf16[64,4096]{1,0:T(8,128)(2,1)} %points_ref.4) | copy-start | bytes 1572868
  2.8 9.3 %copy-start.15 = (s32[1024,12]{0,1:T(8,128)S(1)}, s32[1024,12]{0,1:T(8,128)}, u32[]{:S(2)}) copy-start(s32[1024,12]{0,1:T(8,128)} %param.10) | copy-start | bytes 147460
  2.8 4.4 %collective-permute-start.2 = (bf16[96,2048]{1,0:T(8,128)(2,1)S(1)}, bf16[96,2048]{1,0:T(8,128)(2,1)S(1)}, u32[]{:S(2)}, u32[]{:S(2)}) collective-permute-start(bf16[96,2048]{1,0:T(8,128)(2,1)S(1)} %pad_maximum_fusion.3), channel_id=1, source_target_pairs={{0,1},{1,0},{2,3},{3,2},{4,5},{5,4},{6,7},{7,6},{8,9},{9,8},{10,11... | collective-permute-start | bytes 1179656 | tf_op jit(solution)/shard_map/ppermute | solution.py:40
  3.0 13.3 %collective-permute-start.1 = (bf16[96,2048]{1,0:T(8,128)(2,1)S(1)}, bf16[96,2048]{1,0:T(8,128)(2,1)S(1)}, u32[]{:S(2)}, u32[]{:S(2)}) collective-permute-start(bf16[96,2048]{1,0:T(8,128)(2,1)S(1)} %get-tuple-element.46), channel_id=1, source_target_pairs={{0,96},{1,25},{2,98},{3,27},{4,100},{5,29},{6,102},{7,31},{8,104},... | collective-permute-start | bytes 1179656 | tf_op jit(solution)/shard_map/ppermute | solution.py:52
  7.2 9.1 %collective-permute-start = (bf16[96,2048]{1,0:T(8,128)(2,1)S(1)}, bf16[96,2048]{1,0:T(8,128)(2,1)}, u32[]{:S(2)}, u32[]{:S(2)}) collective-permute-start(bf16[96,2048]{1,0:T(8,128)(2,1)S(1)} %get-tuple-element.46), channel_id=1, source_target_pairs={{0,32},{1,9},{2,34},{3,11},{4,36},{5,13},{6,38},{7,15},{8,40},{9,1... | collective-permute-start | bytes 1179656 | tf_op jit(solution)/shard_map/ppermute | solution.py:52
  7.2 14.8 %copy-start.12 = (bf16[96,2048]{1,0:T(8,128)(2,1)}, bf16[96,2048]{1,0:T(8,128)(2,1)S(1)}, u32[]{:S(2)}) copy-start(bf16[96,2048]{1,0:T(8,128)(2,1)S(1)} %collective-permute-done.2) | copy-start | bytes 1179652
  7.2 9.5 %collective-permute-start.4 = (bf16[96,2048]{1,0:T(8,128)(2,1)S(1)}, bf16[96,2048]{1,0:T(8,128)(2,1)S(1)}, u32[]{:S(2)}, u32[]{:S(2)}) collective-permute-start(bf16[96,2048]{1,0:T(8,128)(2,1)S(1)} %collective-permute-done.2), channel_id=1, source_target_pairs={{0,96},{1,25},{2,98},{3,27},{4,100},{5,29},{6,102},{7,31},{8,104},... | collective-permute-start | bytes 1179656 | tf_op jit(solution)/shard_map/ppermute | solution.py:52
  10.5 10.0 %collective-permute-start.3 = (bf16[96,2048]{1,0:T(8,128)(2,1)S(1)}, bf16[96,2048]{1,0:T(8,128)(2,1)S(1)}, u32[]{:S(2)}, u32[]{:S(2)}) collective-permute-start(bf16[96,2048]{1,0:T(8,128)(2,1)S(1)} %collective-permute-done.2), channel_id=1, source_target_pairs={{0,32},{1,9},{2,34},{3,11},{4,36},{5,13},{6,38},{7,15},{8,40},{9,1... | collective-permute-start | bytes 1179656 | tf_op jit(solution)/shard_map/ppermute | solution.py:52
  16.3 10.6 %collective-permute-start.5 = (bf16[96,2048]{1,0:T(8,128)(2,1)}, bf16[96,2048]{1,0:T(8,128)(2,1)}, u32[]{:S(2)}, u32[]{:S(2)}) collective-permute-start(bf16[96,2048]{1,0:T(8,128)(2,1)} %collective-permute-done), channel_id=1, source_target_pairs={{0,32},{1,9},{2,34},{3,11},{4,36},{5,13},{6,38},{7,15},{8,40},{9,1... | collective-permute-start | bytes 1179656 | tf_op jit(solution)/shard_map/ppermute | solution.py:52
  16.7 5.3 %copy-start.13 = (bf16[96,2048]{1,0:T(8,128)(2,1)}, bf16[96,2048]{1,0:T(8,128)(2,1)S(1)}, u32[]{:S(2)}) copy-start(bf16[96,2048]{1,0:T(8,128)(2,1)S(1)} %collective-permute-done.4) | copy-start | bytes 1179652
  20.4 1.6 copy-start.14
  22.0 29.0 %all-to-all-start = ((bf16[4,64,4096]{2,1,0:T(8,128)(2,1)}), bf16[4,64,4096]{2,1,0:T(8,128)(2,1)S(1)}, u32[]{:S(2)}, u32[]{:S(2)}) async-start(bf16[4,64,4096]{2,1,0:T(8,128)(2,1)} %broadcast_in_dim.77), calls=%async_computation | async-start | bytes 4194304 | tf_op jit(solution)/shard_map/all_to_all | solution.py:293
  26.5 8.0 %collective-permute-start.6 = (bf16[96,2048]{1,0:T(8,128)(2,1)}, bf16[96,2048]{1,0:T(8,128)(2,1)S(1)}, u32[]{:S(2)}, u32[]{:S(2)}) collective-permute-start(bf16[96,2048]{1,0:T(8,128)(2,1)} %copy-done.13), channel_id=1, source_target_pairs={{0,96},{1,25},{2,98},{3,27},{4,100},{5,29},{6,102},{7,31},{8,104},... | collective-permute-start | bytes 1179656 | tf_op jit(solution)/shard_map/ppermute | solution.py:52
  37.1 33.4 %collective-permute-start.10 = (bf16[4,96,2048]{2,1,0:T(8,128)(2,1)}, bf16[4,96,2048]{2,1,0:T(8,128)(2,1)}, u32[]{:S(2)}, u32[]{:S(2)}) collective-permute-start(bf16[4,96,2048]{2,1,0:T(8,128)(2,1)} %pad_maximum_fusion.1.refs_1_), channel_id=1, source_target_pairs={{0,24},{1,97},{2,26},{3,99},{4,28},{5,101},{6,30},{7,103},{8,0},{9... | collective-permute-start | bytes 4718600 | tf_op jit(solution)/shard_map/ppermute | solution.py:52
  39.9 38.8 %collective-permute-start.8 = (bf16[4,96,2048]{2,1,0:T(8,128)(2,1)}, bf16[4,96,2048]{2,1,0:T(8,128)(2,1)}, u32[]{:S(2)}, u32[]{:S(2)}) collective-permute-start(bf16[4,96,2048]{2,1,0:T(8,128)(2,1)} %pad_maximum_fusion.1.refs_1_), channel_id=1, source_target_pairs={{0,8},{1,33},{2,10},{3,35},{4,12},{5,37},{6,14},{7,39},{8,16},{9,4... | collective-permute-start | bytes 4718600 | tf_op jit(solution)/shard_map/ppermute | solution.py:52
  39.9 5.7 %copy-start.2 = (bf16[32,4096]{1,0:T(8,128)(2,1)S(1)}, bf16[32,4096]{1,0:T(8,128)(2,1)}, u32[]{:S(2)}) copy-start(bf16[32,4096]{1,0:T(8,128)(2,1)} %weights_ref.1) | copy-start | bytes 786436
  39.9 5.7 %copy-start.18 = (s32[4096]{0:T(1024)S(1)}, s32[4096]{0:T(1024)}, u32[]{:S(2)}) copy-start(s32[4096]{0:T(1024)} %param.9) | copy-start | bytes 49156
  42.3 4.9 %copy-start.17 = (s32[512]{0:T(512)S(1)}, s32[512]{0:T(512)}, u32[]{:S(2)}) copy-start(s32[512]{0:T(512)} %param.8) | copy-start | bytes 6148
  42.3 36.3 %collective-permute-start.9 = (bf16[4,96,2048]{2,1,0:T(8,128)(2,1)}, bf16[4,96,2048]{2,1,0:T(8,128)(2,1)}, u32[]{:S(2)}, u32[]{:S(2)}) collective-permute-start(bf16[4,96,2048]{2,1,0:T(8,128)(2,1)} %pad_maximum_fusion.refs_0_), channel_id=1, source_target_pairs={{0,24},{1,97},{2,26},{3,99},{4,28},{5,101},{6,30},{7,103},{8,0},{9... | collective-permute-start | bytes 4718600 | tf_op jit(solution)/shard_map/ppermute | solution.py:52
  45.6 33.1 %collective-permute-start.7 = (bf16[4,96,2048]{2,1,0:T(8,128)(2,1)}, bf16[4,96,2048]{2,1,0:T(8,128)(2,1)}, u32[]{:S(2)}, u32[]{:S(2)}) collective-permute-start(bf16[4,96,2048]{2,1,0:T(8,128)(2,1)} %pad_maximum_fusion.refs_0_), channel_id=1, source_target_pairs={{0,8},{1,33},{2,10},{3,35},{4,12},{5,37},{6,14},{7,39},{8,16},{9,4... | collective-permute-start | bytes 4718600 | tf_op jit(solution)/shard_map/ppermute | solution.py:52
  52.1 16.8 %all-to-all-start.1 = ((bf16[8,96,512]{2,1,0:T(8,128)(2,1)}), bf16[8,96,512]{2,1,0:T(8,128)(2,1)S(1)}, u32[]{:S(2)}, u32[]{:S(2)}) async-start(bf16[8,96,512]{2,1,0:T(8,128)(2,1)} %broadcast_in_dim.79), calls=%async_computation.1 | async-start | bytes 1572864 | tf_op jit(solution)/shard_map/all_to_all | solution.py:293
  55.9 46.8 %collective-permute-start.11 = (bf16[4,64,4096]{2,1,0:T(8,128)(2,1)S(1)}, bf16[4,64,4096]{2,1,0:T(8,128)(2,1)}, u32[]{:S(2)}, u32[]{:S(2)}) collective-permute-start(bf16[4,64,4096]{2,1,0:T(8,128)(2,1)S(1)} %all-to-all-done.other_ref.line_ref), channel_id=1, source_target_pairs={{0,1},{1,0},{2,3},{3,2},{4,5},{5,4},{6,7},{7,6},{8,9},{9,8},{10,11... | collective-permute-start | bytes 6291464 | tf_op jit(solution)/shard_map/ppermute | solution.py:40
  69.0 0.9 copy-start.1
  69.9 0.6 copy-start.7
  70.5 32.2 %collective-permute-start.13 = (bf16[4,96,2048]{2,1,0:T(8,128)(2,1)}, bf16[4,96,2048]{2,1,0:T(8,128)(2,1)}, u32[]{:S(2)}, u32[]{:S(2)}) collective-permute-start(bf16[4,96,2048]{2,1,0:T(8,128)(2,1)} %collective-permute-done.10.refs_5_), channel_id=1, source_target_pairs={{0,24},{1,97},{2,26},{3,99},{4,28},{5,101},{6,30},{7,103},{8,0},{9... | collective-permute-start | bytes 4718600 | tf_op jit(solution)/shard_map/ppermute | solution.py:52
  78.6 24.1 %collective-permute-start.12 = (bf16[4,96,2048]{2,1,0:T(8,128)(2,1)}, bf16[4,96,2048]{2,1,0:T(8,128)(2,1)}, u32[]{:S(2)}, u32[]{:S(2)}) collective-permute-start(bf16[4,96,2048]{2,1,0:T(8,128)(2,1)} %collective-permute-done.7.refs_2_), channel_id=1, source_target_pairs={{0,8},{1,33},{2,10},{3,35},{4,12},{5,37},{6,14},{7,39},{8,16},{9,4... | collective-permute-start | bytes 4718600 | tf_op jit(solution)/shard_map/ppermute | solution.py:52
  95.3 1.3 copy-start.8
  96.7 25.2 %all-to-all-start.2 = ((bf16[16,96,256]{2,1,0:T(8,128)(2,1)}), bf16[16,96,256]{2,1,0:T(8,128)(2,1)}, u32[]{:S(2)}, u32[]{:S(2)}) async-start(bf16[16,96,256]{2,1,0:T(8,128)(2,1)} %copy-done.1), calls=%async_computation.2 | async-start | bytes 1572864 | tf_op jit(solution)/shard_map/all_to_all | solution.py:293
  101.0 20.3 %collective-permute-start.14 = (bf16[96,512]{1,0:T(8,128)(2,1)}, bf16[96,512]{1,0:T(8,128)(2,1)S(1)}, u32[]{:S(2)}, u32[]{:S(2)}) collective-permute-start(bf16[96,512]{1,0:T(8,128)(2,1)} %copy-done.7), channel_id=1, source_target_pairs={{0,8},{8,0},{16,24},{24,16},{1,9},{9,1},{17,25},{25,17},{2,10},{10... | collective-permute-start | bytes 294920 | tf_op jit(solution)/shard_map/ppermute | solution.py:40
  120.3 1.0 copy-start.4
  121.3 0.6 copy-start.5
  121.9 13.9 %collective-permute-start.15 = (bf16[4,32,4096]{2,1,0:T(8,128)(2,1)}, bf16[4,32,4096]{2,1,0:T(8,128)(2,1)S(1)}, u32[]{:S(2)}, u32[]{:S(2)}) collective-permute-start(bf16[4,32,4096]{2,1,0:T(8,128)(2,1)} %copy-done.4), channel_id=1, source_target_pairs={{0,1},{1,0},{2,3},{3,2},{4,5},{5,4},{6,7},{7,6},{8,9},{9,8},{10,11... | collective-permute-start | bytes 3145736 | tf_op jit(solution)/shard_map/ppermute | solution.py:40
  121.9 6.9 %copy-start.9 = (f32[4,32,4096]{2,1,0:T(8,128)S(1)}, f32[4,32,4096]{2,1,0:T(8,128)}, u32[]{:S(2)}) copy-start(f32[4,32,4096]{2,1,0:T(8,128)} %copy-done.8) | copy-start | bytes 6291460
  128.0 0.8 copy-start.10
  137.0 10.5 %copy-start.6 = (bf16[96,512]{1,0:T(8,128)(2,1)S(1)}, bf16[96,512]{1,0:T(8,128)(2,1)}, u32[]{:S(2)}) copy-start(bf16[96,512]{1,0:T(8,128)(2,1)} %copy-done.5) | copy-start | bytes 294916
  137.0 10.5 %copy-start.11 = (f32[32,4096]{1,0:T(8,128)S(1)}, f32[32,4096]{1,0:T(8,128)}, u32[]{:S(2)}) copy-start(f32[32,4096]{1,0:T(8,128)} %copy-done.10) | copy-start | bytes 1572868
  137.0 24.9 %all-to-all-start.3 = ((bf16[4,32,4096]{2,1,0:T(8,128)(2,1)}), bf16[4,32,4096]{2,1,0:T(8,128)(2,1)S(1)}, u32[]{:S(2)}, u32[]{:S(2)}) async-start(bf16[4,32,4096]{2,1,0:T(8,128)(2,1)} %add_convert_fusion), calls=%async_computation.3 | async-start | bytes 2097152 | tf_op jit(solution)/shard_map/all_to_all | solution.py:293
  147.5 10.1 %copy-start.3 = (bf16[32,4096]{1,0:T(8,128)(2,1)S(1)}, bf16[32,4096]{1,0:T(8,128)(2,1)}, u32[]{:S(2)}) copy-start(bf16[32,4096]{1,0:T(8,128)(2,1)} %weights_ref.1) | copy-start | bytes 786436

commit v5 on v4

--- a/solution.py
+++ b/solution.py
@@ -361,9 +361,8 @@
     mine = leaf_class(points, weights, core)
     theirs = swap(leaf_class(points, weights, 1 - core), "core", 1)
     own, other = spread(mine, theirs, 0)
-    _, _, points_later = lax.optimization_barrier((own, other, points))
     own_far, other_far = spread_on(own, other, 0)
-    line = everyone(points_later, ("y",))
+    line = everyone(points, ("y",))
     own_far, other_far = lax.optimization_barrier((own_far, other_far))
     own_line = jnp.stack([mine, *own, own_far])
     other_line = jnp.stack([theirs, *other, other_far])
@@ -384,7 +383,9 @@
     pairs, totals = pair_lists(near_leaf, near_count, place)
     early = [own_line, other_line, own[0], other[0], own[1], other[1]]
     late = spread_on(own, other, 1)
-    home = near_part(pairs[0], totals[0], (line, line), early, 4, 4, None, jnp.float32, 36)
+    self_sum = self_terms(points, weights)
+    home_pairs, self_sum = lax.optimization_barrier((pairs[0], self_sum))
+    home = near_part(home_pairs, totals[0], (line, line), early, 4, 4, None, jnp.float32, 36)
     cross_pairs, home, copies, node = lax.optimization_barrier((pairs[1], home, copies, node))
     x_sibling = swap(node, "x", 1)
     wide_nodes = exchange(copies, ("z", "x"))
@@ -392,10 +393,11 @@
     last_pairs, across, x_sibling, wide_nodes = lax.optimization_barrier((pairs[2], across, x_sibling, wide_nodes))
     across = swap(across, "core", 1)
     home = near_part(last_pairs, totals[2], (line, line), late, 4, 4, home, jnp.float32, 12)
-    parts = exchange((home + across.astype(jnp.float32)).astype(jnp.bfloat16), "y")
+    parts = (home + across.astype(jnp.float32)).astype(jnp.bfloat16)
+    parts, points_last = lax.optimization_barrier((parts, points))
+    parts = exchange(parts, "y")
     _, points_later = lax.optimization_barrier((home, points))
-    self_sum = self_terms(points_later, weights)
-    far_field = far_terms(in_line, points, core_sibling, near_nodes, 3)
+    far_field = far_terms(in_line, points_last, core_sibling, near_nodes, 3)
     far_field = far_terms(place["z"] * 4 + place["x"], points, x_sibling, wide_nodes, 4, far_field)
     parts, far_field, self_sum = lax.optimization_barrier((parts, far_field, self_sum))
     near_sum = self_sum + jnp.sum(parts.astype(jnp.float32), axis=0)

time: 164 us -> 161 us (0.982)
  the two profiles are of different devices: /device:TPU:0 before, /device:TPU:12 now
where the time goes in v5:
time: 161 us
  Pallas kernels  57.3 us (36%)
  starting transfers between devices  47.7 us (30%)
  waiting for transfers between devices  23.6 us (15%)
  local copies, waits for them, and re-layouts  17.4 us (11%)
  other arithmetic  12.4 us (8%)
    pallas_call x3, Pallas kernels, near_part(): pl.pallas_call(functools.partial(near_kernel, first, devices, len(sources...  37.7 us
    all_to_all x4, starting transfers between devices, exchange(): return lax.all_to_all(copies, axis, split_axis=0, concat_axis=0, tiled=True)  27.2 us
    ppermute x12, waiting for transfers between devices, ring(): return lax.ppermute(block, AXES, route)  17.5 us
    pallas_call x2, Pallas kernels, far_terms(): pl.pallas_call(functools.partial(far_kernel, depths, seed is not None), o...  16.1 us
    ppermute x12, starting transfers between devices, ring(): return lax.ppermute(block, AXES, route)  14.3 us
    unnamed x31, local copies, waits for them, and re-layouts  8.53 us
    ppermute x4, starting transfers between devices, swap(): return lax.ppermute(block, axis, [(i, i ^ bit) for i in range(count)])  6.17 us
    all_to_all x4, waiting for transfers between devices, exchange(): return lax.all_to_all(copies, axis, split_axis=0, concat_axis=0, tiled=True)  6.1 us
  transfers between devices with their start and end apart: 20, of which 5 were waited for; matrix products, arithmetic and copies ran while one was open for 10% of the time, Pallas kernels for 36%

profile of v5, /device:TPU:12, one launch (start us, length us, event | category | flops | bytes accessed | tf_op | source)
XLA Modules:
  0.0 160.9 jit_solution(9448803711846873870)
XLA Ops:
  0.6 1.0 constant_dynamic-slice_fusion
  1.6 1.1 constant_dynamic-slice_fusion.1
  2.8 0.8 pad_maximum_fusion.3
  3.6 0.8 fusion.30
  4.4 1.9 %collective-permute-start = (bf16[96,2048]{1,0:T(8,128)(2,1)}, bf16[96,2048]{1,0:T(8,128)(2,1)}, u32[]{:S(2)}, u32[]{:S(2)}) collective-permute-start(bf16[96,2048]{1,0:T(8,128)(2,1)} %get-tuple-element.50), channel_id=1, source_target_pairs={{0,32},{1,9},{2,34},{3,11},{4,36},{5,13},{6,38},{7,15},{8,40},{9,1... | collective-permute-start | bytes 1179656 | tf_op jit(solution)/shard_map/ppermute | solution.py:52
  6.3 2.1 %collective-permute-start.1 = (bf16[96,2048]{1,0:T(8,128)(2,1)}, bf16[96,2048]{1,0:T(8,128)(2,1)}, u32[]{:S(2)}, u32[]{:S(2)}) collective-permute-start(bf16[96,2048]{1,0:T(8,128)(2,1)} %get-tuple-element.50), channel_id=1, source_target_pairs={{0,96},{1,25},{2,98},{3,27},{4,100},{5,29},{6,102},{7,31},{8,104},... | collective-permute-start | bytes 1179656 | tf_op jit(solution)/shard_map/ppermute | solution.py:52
  8.4 1.6 broadcast_in_dim.77
  10.0 5.0 %all-to-all-start = ((bf16[4,64,4096]{2,1,0:T(8,128)(2,1)}), bf16[4,64,4096]{2,1,0:T(8,128)(2,1)S(1)}, u32[]{:S(2)}, u32[]{:S(2)}) async-start(bf16[4,64,4096]{2,1,0:T(8,128)(2,1)} %broadcast_in_dim.77), calls=%async_computation | async-start | bytes 4194304 | tf_op jit(solution)/shard_map/all_to_all | solution.py:293
  15.3 2.1 %collective-permute-start.4 = (bf16[96,2048]{1,0:T(8,128)(2,1)S(1)}, bf16[96,2048]{1,0:T(8,128)(2,1)}, u32[]{:S(2)}, u32[]{:S(2)}) collective-permute-start(bf16[96,2048]{1,0:T(8,128)(2,1)S(1)} %collective-permute-done.3), channel_id=1, source_target_pairs={{0,96},{1,25},{2,98},{3,27},{4,100},{5,29},{6,102},{7,31},{8,104},... | collective-permute-start | bytes 1179656 | tf_op jit(solution)/shard_map/ppermute | solution.py:52
  18.1 5.1 %collective-permute-done.4 = bf16[96,2048]{1,0:T(8,128)(2,1)} collective-permute-done((bf16[96,2048]{1,0:T(8,128)(2,1)S(1)}, bf16[96,2048]{1,0:T(8,128)(2,1)}, u32[]{:S(2)}, u32[]{:S(2)}) %collective-permute-start.4) | collective-permute-done | bytes 393248 | tf_op jit(solution)/shard_map/ppermute | solution.py:52
  23.2 3.2 %collective-permute-start.5 = (bf16[96,2048]{1,0:T(8,128)(2,1)}, bf16[96,2048]{1,0:T(8,128)(2,1)}, u32[]{:S(2)}, u32[]{:S(2)}) collective-permute-start(bf16[96,2048]{1,0:T(8,128)(2,1)} %collective-permute-done.4), channel_id=1, source_target_pairs={{0,96},{1,25},{2,98},{3,27},{4,100},{5,29},{6,102},{7,31},{8,104},... | collective-permute-start | bytes 1179656 | tf_op jit(solution)/shard_map/ppermute | solution.py:52
  26.4 0.4 convert_reduce_fusion
  26.8 1.3 copy.16
  28.2 3.9 %collective-permute-done.5 = bf16[96,2048]{1,0:T(8,128)(2,1)} collective-permute-done((bf16[96,2048]{1,0:T(8,128)(2,1)}, bf16[96,2048]{1,0:T(8,128)(2,1)}, u32[]{:S(2)}, u32[]{:S(2)}) %collective-permute-start.5) | collective-permute-done | bytes 393248 | tf_op jit(solution)/shard_map/ppermute | solution.py:52
  32.1 2.6 %pad_maximum_fusion.refs_0_ = bf16[4,96,2048]{2,1,0:T(8,128)(2,1)} fusion(bf16[1,96,2048]{2,1,0:T(8,128)(2,1)} %bitcast.3, bf16[1,96,2048]{2,1,0:T(8,128)(2,1)} %bitcast.2, bf16[1,96,2048]{2,1,0:T(8,128)(2,1)} %bitcast.1, bf16[1,96,2048]{2,1,0:T(8,128)(2,1)S(1)} %get-tuple-element.49), kind=kLoop, calls=%fused_computation.9 | loop fusion | flops 2359296 | bytes 3145728 | tf_op jit(solution)/shard_map/stack | solution.py:367
  34.7 1.2 collective-permute-start.7
  35.9 0.8 collective-permute-start.9
  36.7 2.2 %collective-permute-done.6 = bf16[96,2048]{1,0:T(8,128)(2,1)S(1)} collective-permute-done((bf16[96,2048]{1,0:T(8,128)(2,1)S(1)}, bf16[96,2048]{1,0:T(8,128)(2,1)S(1)}, u32[]{:S(2)}, u32[]{:S(2)}) %collective-permute-start.6) | collective-permute-done | bytes 393248 | tf_op jit(solution)/shard_map/ppermute | solution.py:52
  38.9 2.6 %pad_maximum_fusion.1.refs_1_ = bf16[4,96,2048]{2,1,0:T(8,128)(2,1)} fusion(bf16[1,96,2048]{2,1,0:T(8,128)(2,1)} %bitcast.7, bf16[1,96,2048]{2,1,0:T(8,128)(2,1)} %bitcast.6, bf16[1,96,2048]{2,1,0:T(8,128)(2,1)S(1)} %bitcast.18, bf16[1,96,2048]{2,1,0:T(8,128)(2,1)S(1)} %bitcast.17), kind=kLoop, calls=%fused_computation.10 | loop fusion | flops 2359296 | bytes 3145728 | tf_op jit(solution)/shard_map/stack | solution.py:368
  41.4 2.0 %collective-permute-start.10 = (bf16[4,96,2048]{2,1,0:T(8,128)(2,1)}, bf16[4,96,2048]{2,1,0:T(8,128)(2,1)}, u32[]{:S(2)}, u32[]{:S(2)}) collective-permute-start(bf16[4,96,2048]{2,1,0:T(8,128)(2,1)} %pad_maximum_fusion.1.refs_1_), channel_id=1, source_target_pairs={{0,24},{1,97},{2,26},{3,99},{4,28},{5,101},{6,30},{7,103},{8,0},{9... | collective-permute-start | bytes 4718600 | tf_op jit(solution)/shard_map/ppermute | solution.py:52
  43.7 1.5 fusion.4
  45.4 2.4 %gather_fusion = bf16[512,64]{1,0:T(8,128)(2,1)S(1)} fusion(bf16[64,4096]{0,1:T(8,128)(2,1)} %copy.16, s32[1024]{0:T(1024)S(1)} %pad_clamp_fusion), kind=kCustom, calls=%fused_computation | custom fusion | bytes 133120 | tf_op jit(solution)/shard_map/gather | solution.py:376
  48.0 1.0 broadcast_in_dim.79
  49.0 4.8 %all-to-all-start.1 = ((bf16[8,96,512]{2,1,0:T(8,128)(2,1)}), bf16[8,96,512]{2,1,0:T(8,128)(2,1)S(1)}, u32[]{:S(2)}, u32[]{:S(2)}) async-start(bf16[8,96,512]{2,1,0:T(8,128)(2,1)} %broadcast_in_dim.79), calls=%async_computation.1 | async-start | bytes 1572864 | tf_op jit(solution)/shard_map/all_to_all | solution.py:293
  54.1 0.9 copy-done.5
  55.0 2.8 %shard_map.77 = f32[32,4096]{1,0:T(8,128)S(1)} custom-call(bf16[64,4096]{1,0:T(8,128)(2,1)S(1)} %copy-done, bf16[32,4096]{1,0:T(8,128)(2,1)S(1)} %copy-done.5), custom_call_target="tpu_custom_call" | custom-call | flops 3758096384 | bytes 2097152 | tf_op jit(solution)/shard_map/pallas_call | solution.py:100
  57.8 0.8 copy-done.2
  58.7 0.7 fusion.34
  59.4 6.1 %all-to-all-done.1.nodes_ref = bf16[8,96,512]{2,1,0:T(8,128)(2,1)S(1)} async-done(((bf16[8,96,512]{2,1,0:T(8,128)(2,1)}), bf16[8,96,512]{2,1,0:T(8,128)(2,1)S(1)}, u32[]{:S(2)}, u32[]{:S(2)}) %all-to-all-start.1) | async-done | bytes 786464 | tf_op jit(solution)/shard_map/all_to_all | solution.py:293
  65.5 0.7 shard_map.79
  66.2 0.9 copy-done.1
  67.1 6.3 %collective-permute-done.10.refs_5_ = bf16[4,96,2048]{2,1,0:T(8,128)(2,1)} collective-permute-done((bf16[4,96,2048]{2,1,0:T(8,128)(2,1)}, bf16[4,96,2048]{2,1,0:T(8,128)(2,1)}, u32[]{:S(2)}, u32[]{:S(2)}) %collective-permute-start.10) | collective-permute-done | bytes 1572896 | tf_op jit(solution)/shard_map/ppermute | solution.py:52
  73.4 0.8 collective-permute-start.13
  74.3 11.8 %shard_map.78.refs_2_ = f32[4,32,4096]{2,1,0:T(8,128)S(1)} custom-call(s32[96]{0:T(128)S(1)} %slice.20.pair_ref, s32[1]{0:T(128)} %get-tuple-element.73.count_ref, bf16[4,64,4096]{2,1,0:T(8,128)(2,1)S(1)} %all-to-all-done.other_ref.line_ref, bf16[4,64,4096]{2,1,0:T(8,128)(2,1)S(1)} %all-to-all-done.other_ref.line_ref, ...), custom_call_target="tpu_custom_call" | custom-call | flops 16911433728 | bytes 8388608 | tf_op jit(solution)/shard_map/pallas_call | solution.py:273
  86.1 1.3 copy-done.9
  87.4 6.0 %collective-permute-start.14 = (bf16[96,512]{1,0:T(8,128)(2,1)}, bf16[96,512]{1,0:T(8,128)(2,1)S(1)}, u32[]{:S(2)}, u32[]{:S(2)}) collective-permute-start(bf16[96,512]{1,0:T(8,128)(2,1)} %get-tuple-element.31), channel_id=1, source_target_pairs={{0,8},{8,0},{16,24},{24,16},{1,9},{9,1},{17,25},{25,17},{2,10},{10... | collective-permute-start | bytes 294920 | tf_op jit(solution)/shard_map/ppermute | solution.py:40
  93.4 6.9 %all-to-all-start.2 = ((bf16[16,96,256]{2,1,0:T(8,128)(2,1)}), bf16[16,96,256]{2,1,0:T(8,128)(2,1)}, u32[]{:S(2)}, u32[]{:S(2)}) async-start(bf16[16,96,256]{2,1,0:T(8,128)(2,1)} %copy-done.1), calls=%async_computation.2 | async-start | bytes 1572864 | tf_op jit(solution)/shard_map/all_to_all | solution.py:293
  100.3 18.9 %shard_map.80 = bf16[4,32,4096]{2,1,0:T(8,128)(2,1)S(1)} custom-call(s32[128]{0:T(128)S(1)} %slice.19.pair_ref, s32[1]{0:T(128)} %get-tuple-element.72.count_ref, bf16[4,64,4096]{2,1,0:T(8,128)(2,1)} %collective-permute-done.11.other_ref, bf16[4,64,4096]{2,1,0:T(8,128)(2,1)S(1)} %all-to-all-done.other_ref.line_ref, ...), custom_call_target="tpu_custom_call" | custom-call | flops 22548578304 | bytes 8388608 | tf_op jit(solution)/shard_map/pallas_call | solution.py:273
  119.2 1.0 copy-done.6
  120.2 0.6 copy-done.7
  120.9 1.6 copy-done.10
  122.4 7.0 %shard_map.81 = f32[4,32,4096]{2,1,0:T(8,128)S(1)} custom-call(s32[32]{0:T(128)S(1)} %slice.18.pair_ref, s32[1]{0:T(128)} %get-tuple-element.71.count_ref, bf16[4,64,4096]{2,1,0:T(8,128)(2,1)S(1)} %all-to-all-done.other_ref.line_ref, bf16[4,64,4096]{2,1,0:T(8,128)(2,1)S(1)} %all-to-all-done.other_ref.line_ref, ...), custom_call_target="tpu_custom_call" | custom-call | flops 5637144576 | bytes 8388608 | tf_op jit(solution)/shard_map/pallas_call | solution.py:273
  129.5 2.4 %add_convert_fusion = bf16[4,32,4096]{2,1,0:T(8,128)(2,1)} fusion(f32[4,32,4096]{2,1,0:T(8,128)S(1)} %shard_map.81, bf16[4,32,4096]{2,1,0:T(8,128)(2,1)} %collective-permute-done.15), kind=kLoop, calls=%fused_computation.8 | loop fusion | flops 1572864 | bytes 4194304 | tf_op jit(solution)/shard_map/convert_element_type | solution.py:396
  131.9 10.5 %all-to-all-start.3 = ((bf16[4,32,4096]{2,1,0:T(8,128)(2,1)}), bf16[4,32,4096]{2,1,0:T(8,128)(2,1)}, u32[]{:S(2)}, u32[]{:S(2)}) async-start(bf16[4,32,4096]{2,1,0:T(8,128)(2,1)} %add_convert_fusion), calls=%async_computation.3 | async-start | bytes 2097152 | tf_op jit(solution)/shard_map/all_to_all | solution.py:293
  142.4 6.1 %shard_map.82.refs_0_ = f32[32,4096]{1,0:T(8,128)S(1)} custom-call(s32[1]{0:T(128)} %bitcast.11.place_ref, bf16[64,4096]{1,0:T(8,128)(2,1)S(1)} %copy-done, bf16[96,512]{1,0:T(8,128)(2,1)S(1)} %dynamic-slice_bitcast_fusion.sibling_ref, bf16[8,96,512]{2,1,0:T(8,128)(2,1)S(1)} %all-to-all-done.1.nodes_ref), custom_call_target="tpu_custom_call" | custom-call | flops 11274289152 | bytes 4194304 | tf_op jit(solution)/shard_map/pallas_call | solution.py:173
  148.5 10.0 %shard_map.83 = f32[32,4096]{1,0:T(8,128)} custom-call(s32[1]{0:T(128)} %bitcast.10.place_ref, bf16[64,4096]{1,0:T(8,128)(2,1)S(1)} %copy-done, bf16[96,512]{1,0:T(8,128)(2,1)S(1)} %copy-done.8, bf16[16,96,256]{2,1,0:T(8,128)(2,1)} %all-to-all-done.2.nodes_ref, f32[32,4096]{1,0:T(8,128)S(1)} %shard_map.82.refs_0_), custom_call_target="tpu_custom_call" | custom-call | flops 15032385536 | bytes 4194304 | tf_op jit(solution)/shard_map/pallas_call | solution.py:173
  158.5 1.5 convert_reduce_fusion.1
  160.0 0.9 add_multiply_fusion
  (67 shorter events, 2.0 us)
Async XLA Ops:
  1.6 6.8 %copy-start = (bf16[64,4096]{1,0:T(8,128)(2,1)S(1)}, bf16[64,4096]{1,0:T(8,128)(2,1)}, u32[]{:S(2)}) copy-start(bf16[64,4096]{1,0:T(8,128)(2,1)} %points_ref.4) | copy-start | bytes 1572868
  3.6 11.7 %collective-permute-start.3 = (bf16[96,2048]{1,0:T(8,128)(2,1)}, bf16[96,2048]{1,0:T(8,128)(2,1)S(1)}, u32[]{:S(2)}, u32[]{:S(2)}) collective-permute-start(bf16[96,2048]{1,0:T(8,128)(2,1)} %pad_maximum_fusion.3), channel_id=1, source_target_pairs={{0,1},{1,0},{2,3},{3,2},{4,5},{5,4},{6,7},{7,6},{8,9},{9,8},{10,11... | collective-permute-start | bytes 1179656 | tf_op jit(solution)/shard_map/ppermute | solution.py:40
  4.4 13.6 %collective-permute-start = (bf16[96,2048]{1,0:T(8,128)(2,1)}, bf16[96,2048]{1,0:T(8,128)(2,1)}, u32[]{:S(2)}, u32[]{:S(2)}) collective-permute-start(bf16[96,2048]{1,0:T(8,128)(2,1)} %get-tuple-element.50), channel_id=1, source_target_pairs={{0,32},{1,9},{2,34},{3,11},{4,36},{5,13},{6,38},{7,15},{8,40},{9,1... | collective-permute-start | bytes 1179656 | tf_op jit(solution)/shard_map/ppermute | solution.py:52
  6.3 25.7 %collective-permute-start.1 = (bf16[96,2048]{1,0:T(8,128)(2,1)}, bf16[96,2048]{1,0:T(8,128)(2,1)}, u32[]{:S(2)}, u32[]{:S(2)}) collective-permute-start(bf16[96,2048]{1,0:T(8,128)(2,1)} %get-tuple-element.50), channel_id=1, source_target_pairs={{0,96},{1,25},{2,98},{3,27},{4,100},{5,29},{6,102},{7,31},{8,104},... | collective-permute-start | bytes 1179656 | tf_op jit(solution)/shard_map/ppermute | solution.py:52
  10.0 5.0 %copy-start.12 = (s32[1024]{0:T(1024)S(1)}, s32[1024]{0:T(1024)}, u32[]{:S(2)}) copy-start(s32[1024]{0:T(1024)} %param.11) | copy-start | bytes 12292
  10.0 7.5 %copy-start.11 = (s32[1024,12]{0,1:T(8,128)S(1)}, s32[1024,12]{0,1:T(8,128)}, u32[]{:S(2)}) copy-start(s32[1024,12]{0,1:T(8,128)} %param.10) | copy-start | bytes 147460
  10.0 38.0 %all-to-all-start = ((bf16[4,64,4096]{2,1,0:T(8,128)(2,1)}), bf16[4,64,4096]{2,1,0:T(8,128)(2,1)S(1)}, u32[]{:S(2)}, u32[]{:S(2)}) async-start(bf16[4,64,4096]{2,1,0:T(8,128)(2,1)} %broadcast_in_dim.77), calls=%async_computation | async-start | bytes 4194304 | tf_op jit(solution)/shard_map/all_to_all | solution.py:293
  15.3 8.0 %collective-permute-start.4 = (bf16[96,2048]{1,0:T(8,128)(2,1)S(1)}, bf16[96,2048]{1,0:T(8,128)(2,1)}, u32[]{:S(2)}, u32[]{:S(2)}) collective-permute-start(bf16[96,2048]{1,0:T(8,128)(2,1)S(1)} %collective-permute-done.3), channel_id=1, source_target_pairs={{0,96},{1,25},{2,98},{3,27},{4,100},{5,29},{6,102},{7,31},{8,104},... | collective-permute-start | bytes 1179656 | tf_op jit(solution)/shard_map/ppermute | solution.py:52
  18.0 10.2 %collective-permute-start.2 = (bf16[96,2048]{1,0:T(8,128)(2,1)}, bf16[96,2048]{1,0:T(8,128)(2,1)}, u32[]{:S(2)}, u32[]{:S(2)}) collective-permute-start(bf16[96,2048]{1,0:T(8,128)(2,1)} %collective-permute-done), channel_id=1, source_target_pairs={{0,32},{1,9},{2,34},{3,11},{4,36},{5,13},{6,38},{7,15},{8,40},{9,1... | collective-permute-start | bytes 1179656 | tf_op jit(solution)/shard_map/ppermute | solution.py:52
  23.2 8.8 %collective-permute-start.5 = (bf16[96,2048]{1,0:T(8,128)(2,1)}, bf16[96,2048]{1,0:T(8,128)(2,1)}, u32[]{:S(2)}, u32[]{:S(2)}) collective-permute-start(bf16[96,2048]{1,0:T(8,128)(2,1)} %collective-permute-done.4), channel_id=1, source_target_pairs={{0,96},{1,25},{2,98},{3,27},{4,100},{5,29},{6,102},{7,31},{8,104},... | collective-permute-start | bytes 1179656 | tf_op jit(solution)/shard_map/ppermute | solution.py:52
  28.1 10.7 %collective-permute-start.6 = (bf16[96,2048]{1,0:T(8,128)(2,1)S(1)}, bf16[96,2048]{1,0:T(8,128)(2,1)S(1)}, u32[]{:S(2)}, u32[]{:S(2)}) collective-permute-start(bf16[96,2048]{1,0:T(8,128)(2,1)S(1)} %collective-permute-done.3), channel_id=1, source_target_pairs={{0,32},{1,9},{2,34},{3,11},{4,36},{5,13},{6,38},{7,15},{8,40},{9,1... | collective-permute-start | bytes 1179656 | tf_op jit(solution)/shard_map/ppermute | solution.py:52
  34.7 32.4 %collective-permute-start.7 = (bf16[4,96,2048]{2,1,0:T(8,128)(2,1)}, bf16[4,96,2048]{2,1,0:T(8,128)(2,1)}, u32[]{:S(2)}, u32[]{:S(2)}) collective-permute-start(bf16[4,96,2048]{2,1,0:T(8,128)(2,1)} %pad_maximum_fusion.refs_0_), channel_id=1, source_target_pairs={{0,8},{1,33},{2,10},{3,35},{4,12},{5,37},{6,14},{7,39},{8,16},{9,4... | collective-permute-start | bytes 4718600 | tf_op jit(solution)/shard_map/ppermute | solution.py:52
  35.9 38.4 %collective-permute-start.9 = (bf16[4,96,2048]{2,1,0:T(8,128)(2,1)}, bf16[4,96,2048]{2,1,0:T(8,128)(2,1)}, u32[]{:S(2)}, u32[]{:S(2)}) collective-permute-start(bf16[4,96,2048]{2,1,0:T(8,128)(2,1)} %pad_maximum_fusion.refs_0_), channel_id=1, source_target_pairs={{0,24},{1,97},{2,26},{3,99},{4,28},{5,101},{6,30},{7,103},{8,0},{9... | collective-permute-start | bytes 4718600 | tf_op jit(solution)/shard_map/ppermute | solution.py:52
  38.9 4.8 %copy-start.4 = (bf16[32,4096]{1,0:T(8,128)(2,1)S(1)}, bf16[32,4096]{1,0:T(8,128)(2,1)}, u32[]{:S(2)}) copy-start(bf16[32,4096]{1,0:T(8,128)(2,1)} %weights_ref.1) | copy-start | bytes 786436
  38.9 4.8 %copy-start.14 = (s32[4096]{0:T(1024)S(1)}, s32[4096]{0:T(1024)}, u32[]{:S(2)}) copy-start(s32[4096]{0:T(1024)} %param.9) | copy-start | bytes 49156
  41.4 32.8 %collective-permute-start.8 = (bf16[4,96,2048]{2,1,0:T(8,128)(2,1)}, bf16[4,96,2048]{2,1,0:T(8,128)(2,1)}, u32[]{:S(2)}, u32[]{:S(2)}) collective-permute-start(bf16[4,96,2048]{2,1,0:T(8,128)(2,1)} %pad_maximum_fusion.1.refs_1_), channel_id=1, source_target_pairs={{0,8},{1,33},{2,10},{3,35},{4,12},{5,37},{6,14},{7,39},{8,16},{9,4... | collective-permute-start | bytes 4718600 | tf_op jit(solution)/shard_map/ppermute | solution.py:52
  41.4 32.0 %collective-permute-start.10 = (bf16[4,96,2048]{2,1,0:T(8,128)(2,1)}, bf16[4,96,2048]{2,1,0:T(8,128)(2,1)}, u32[]{:S(2)}, u32[]{:S(2)}) collective-permute-start(bf16[4,96,2048]{2,1,0:T(8,128)(2,1)} %pad_maximum_fusion.1.refs_1_), channel_id=1, source_target_pairs={{0,24},{1,97},{2,26},{3,99},{4,28},{5,101},{6,30},{7,103},{8,0},{9... | collective-permute-start | bytes 4718600 | tf_op jit(solution)/shard_map/ppermute | solution.py:52
  43.6 1.7 %copy-start.13 = (s32[512]{0:T(512)S(1)}, s32[512]{0:T(512)}, u32[]{:S(2)}) copy-start(s32[512]{0:T(512)} %param.8) | copy-start | bytes 6148
  49.0 16.5 %all-to-all-start.1 = ((bf16[8,96,512]{2,1,0:T(8,128)(2,1)}), bf16[8,96,512]{2,1,0:T(8,128)(2,1)S(1)}, u32[]{:S(2)}, u32[]{:S(2)}) async-start(bf16[8,96,512]{2,1,0:T(8,128)(2,1)} %broadcast_in_dim.79), calls=%async_computation.1 | async-start | bytes 1572864 | tf_op jit(solution)/shard_map/all_to_all | solution.py:293
  53.9 46.3 %collective-permute-start.11 = (bf16[4,64,4096]{2,1,0:T(8,128)(2,1)S(1)}, bf16[4,64,4096]{2,1,0:T(8,128)(2,1)}, u32[]{:S(2)}, u32[]{:S(2)}) collective-permute-start(bf16[4,64,4096]{2,1,0:T(8,128)(2,1)S(1)} %all-to-all-done.other_ref.line_ref), channel_id=1, source_target_pairs={{0,1},{1,0},{2,3},{3,2},{4,5},{5,4},{6,7},{7,6},{8,9},{9,8},{10,11... | collective-permute-start | bytes 6291464 | tf_op jit(solution)/shard_map/ppermute | solution.py:40
  54.1 0.9 copy-start.5
  57.8 0.8 copy-start.2
  66.2 0.9 copy-start.1
  67.1 33.2 %collective-permute-start.12 = (bf16[4,96,2048]{2,1,0:T(8,128)(2,1)}, bf16[4,96,2048]{2,1,0:T(8,128)(2,1)}, u32[]{:S(2)}, u32[]{:S(2)}) collective-permute-start(bf16[4,96,2048]{2,1,0:T(8,128)(2,1)} %collective-permute-done.7.refs_2_), channel_id=1, source_target_pairs={{0,8},{1,33},{2,10},{3,35},{4,12},{5,37},{6,14},{7,39},{8,16},{9,4... | collective-permute-start | bytes 4718600 | tf_op jit(solution)/shard_map/ppermute | solution.py:52
  73.4 26.8 %collective-permute-start.13 = (bf16[4,96,2048]{2,1,0:T(8,128)(2,1)}, bf16[4,96,2048]{2,1,0:T(8,128)(2,1)}, u32[]{:S(2)}, u32[]{:S(2)}) collective-permute-start(bf16[4,96,2048]{2,1,0:T(8,128)(2,1)} %collective-permute-done.10.refs_5_), channel_id=1, source_target_pairs={{0,24},{1,97},{2,26},{3,99},{4,28},{5,101},{6,30},{7,103},{8,0},{9... | collective-permute-start | bytes 4718600 | tf_op jit(solution)/shard_map/ppermute | solution.py:52
  86.1 1.3 copy-start.9
  87.4 32.8 %collective-permute-start.14 = (bf16[96,512]{1,0:T(8,128)(2,1)}, bf16[96,512]{1,0:T(8,128)(2,1)S(1)}, u32[]{:S(2)}, u32[]{:S(2)}) collective-permute-start(bf16[96,512]{1,0:T(8,128)(2,1)} %get-tuple-element.31), channel_id=1, source_target_pairs={{0,8},{8,0},{16,24},{24,16},{1,9},{9,1},{17,25},{25,17},{2,10},{10... | collective-permute-start | bytes 294920 | tf_op jit(solution)/shard_map/ppermute | solution.py:40
  93.4 27.4 %all-to-all-start.2 = ((bf16[16,96,256]{2,1,0:T(8,128)(2,1)}), bf16[16,96,256]{2,1,0:T(8,128)(2,1)}, u32[]{:S(2)}, u32[]{:S(2)}) async-start(bf16[16,96,256]{2,1,0:T(8,128)(2,1)} %copy-done.1), calls=%async_computation.2 | async-start | bytes 1572864 | tf_op jit(solution)/shard_map/all_to_all | solution.py:293
  119.2 1.0 copy-start.6
  120.2 0.6 copy-start.7
  120.8 8.6 %collective-permute-start.15 = (bf16[4,32,4096]{2,1,0:T(8,128)(2,1)}, bf16[4,32,4096]{2,1,0:T(8,128)(2,1)}, u32[]{:S(2)}, u32[]{:S(2)}) collective-permute-start(bf16[4,32,4096]{2,1,0:T(8,128)(2,1)} %copy-done.6), channel_id=1, source_target_pairs={{0,1},{1,0},{2,3},{3,2},{4,5},{5,4},{6,7},{7,6},{8,9},{9,8},{10,11... | collective-permute-start | bytes 3145736 | tf_op jit(solution)/shard_map/ppermute | solution.py:40
  120.9 1.6 copy-start.10
  131.9 26.6 %all-to-all-start.3 = ((bf16[4,32,4096]{2,1,0:T(8,128)(2,1)}), bf16[4,32,4096]{2,1,0:T(8,128)(2,1)}, u32[]{:S(2)}, u32[]{:S(2)}) async-start(bf16[4,32,4096]{2,1,0:T(8,128)(2,1)} %add_convert_fusion), calls=%async_computation.3 | async-start | bytes 2097152 | tf_op jit(solution)/shard_map/all_to_all | solution.py:293
  142.4 6.1 %copy-start.8 = (bf16[96,512]{1,0:T(8,128)(2,1)S(1)}, bf16[96,512]{1,0:T(8,128)(2,1)}, u32[]{:S(2)}) copy-start(bf16[96,512]{1,0:T(8,128)(2,1)} %copy-done.7) | copy-start | bytes 294916
  158.5 1.5 copy-start.3

commit v6 on v5

--- a/solution.py
+++ b/solution.py
@@ -186,7 +186,7 @@
     )(place.reshape(1), points, sibling, nodes, *seeds)
 
 
-def near_kernel(first, devices, n_source, seeded, pair_ref, count_ref, other_ref, line_ref, *refs):
+def near_kernel(first, devices, n_source, seeded, pair_ref, count_ref, target_ref, *refs):
     source_refs, refs = refs[:n_source], refs[n_source:]
     if seeded:
         seed_ref, refs = refs[0], refs[1:]
@@ -198,17 +198,11 @@
             code = pair_ref[group * UNROLL + unit]
             target = jnp.minimum(code // (32 * CLASS), SPARE - 1)
             start = pl.multiple_of(target % LEAVES_DEV * LEAF, LEAF)
-            device = target // LEAVES_DEV
-            for ref, here in ((other_ref, device < 4), (line_ref, device >= 4)):
-
-                @pl.when(here)
-                def _(ref=ref):
-                    pltpu.make_async_copy(
-                        ref.at[device % 4, :, pl.ds(start, LEAF)],
-                        target_buf.at[slot, unit],
-                        sem.at[slot, unit, 1],
-                    ).start()
-
+            pltpu.make_async_copy(
+                target_ref.at[target // LEAVES_DEV % 4, :, pl.ds(start, LEAF)],
+                target_buf.at[slot, unit],
+                sem.at[slot, unit, 1],
+            ).start()
             which = code // (4 * CLASS) % 8
             start = pl.multiple_of(code % CLASS * LEAF, LEAF)
             for at in range(n_source):
@@ -227,7 +221,7 @@
                 source_refs[0].at[0, :, pl.ds(0, LEAF)], buf.at[slot, unit], sem.at[slot, unit, 0]
             ).wait()
             pltpu.make_async_copy(
-                line_ref.at[0, :, pl.ds(0, LEAF)], target_buf.at[slot, unit], sem.at[slot, unit, 1]
+                target_ref.at[0, :, pl.ds(0, LEAF)], target_buf.at[slot, unit], sem.at[slot, unit, 1]
             ).wait()
 
     @pl.when(groups > 0)
@@ -273,7 +267,7 @@
     return pl.pallas_call(
         functools.partial(near_kernel, first, devices, len(sources), seed is not None),
         out_shape=jax.ShapeDtypeStruct((devices, RHS, P_DEV), dtype),
-        in_specs=[SMEM, SMEM, ANY, ANY] + [ANY] * len(sources) + [ANY] * len(seeds),
+        in_specs=[SMEM, SMEM, ANY] + [ANY] * len(sources) + [ANY] * len(seeds),
         out_specs=ANY if dtype == jnp.float32 else VMEM,
         scratch_shapes=[
             pltpu.VMEM((2, UNROLL, ROWS, LEAF), jnp.bfloat16),
@@ -284,9 +278,9 @@
             pltpu.VMEM((UNROLL, DEPTH, LEAF), jnp.bfloat16),
             pltpu.VMEM((devices + 1, RHS, P_DEV), jnp.float32),
         ],
-        compiler_params=pltpu.CompilerParams(vmem_limit_bytes=32 << 20),
+        compiler_params=pltpu.CompilerParams(vmem_limit_bytes=18 << 20),
         cost_estimate=cost(expected * LEAF * LEAF, 8 << 20),
-    )(pairs, count, *targets, *sources, *seeds)
+    )(pairs, count, targets, *sources, *seeds)
 
 
 def exchange(copies, axis):
@@ -375,7 +369,7 @@
     ).astype(jnp.bfloat16)
     base = jnp.concatenate([points[:, skel_index], base_weights], axis=0)
     near_nodes = everyone(base, ("y", "core"))
-    targets = (swap(line, "core", 1), line)
+    other_targets = swap(line, "core", 1)
     node, copies = merge(near_nodes)
     in_line = place["y"] * 2 + core
     core_sibling = lax.dynamic_index_in_dim(near_nodes, in_line ^ 1, 0, keepdims=False)
@@ -385,22 +379,23 @@
     late = spread_on(own, other, 1)
     self_sum = self_terms(points, weights)
     home_pairs, self_sum = lax.optimization_barrier((pairs[0], self_sum))
-    home = near_part(home_pairs, totals[0], (line, line), early, 4, 4, None, jnp.float32, 36)
+    home = near_part(home_pairs, totals[0], line, early, 4, 4, None, jnp.float32, 36)
     cross_pairs, home, copies, node = lax.optimization_barrier((pairs[1], home, copies, node))
     x_sibling = swap(node, "x", 1)
     wide_nodes = exchange(copies, ("z", "x"))
-    across = near_part(cross_pairs, totals[1], targets, [*early, *late], 0, 4, None, jnp.bfloat16, 48)
+    across = near_part(cross_pairs, totals[1], other_targets, [*early, *late], 0, 4, None, jnp.bfloat16, 48)
     last_pairs, across, x_sibling, wide_nodes = lax.optimization_barrier((pairs[2], across, x_sibling, wide_nodes))
     across = swap(across, "core", 1)
-    home = near_part(last_pairs, totals[2], (line, line), late, 4, 4, home, jnp.float32, 12)
+    home = near_part(last_pairs, totals[2], line, late, 4, 4, home, jnp.float32, 12)
     parts = (home + across.astype(jnp.float32)).astype(jnp.bfloat16)
     parts, points_last = lax.optimization_barrier((parts, points))
     parts = exchange(parts, "y")
-    _, points_later = lax.optimization_barrier((home, points))
     far_field = far_terms(in_line, points_last, core_sibling, near_nodes, 3)
     far_field = far_terms(place["z"] * 4 + place["x"], points, x_sibling, wide_nodes, 4, far_field)
     parts, far_field, self_sum = lax.optimization_barrier((parts, far_field, self_sum))
-    near_sum = self_sum + jnp.sum(parts.astype(jnp.float32), axis=0)
+    near_sum = self_sum
+    for y in range(SIZES["y"]):
+        near_sum = near_sum + parts[y].astype(jnp.float32)
     return (near_sum * NEAR_SCALE, far_field)
 
 

time: 161 us -> 163 us (1.012)
  the two profiles are of different devices: /device:TPU:12 before, /device:TPU:10 now
where the time goes in v6:
time: 163 us
  Pallas kernels  58.8 us (36%)
  starting transfers between devices  49.1 us (30%)
  waiting for transfers between devices  23.2 us (14%)
  local copies, waits for them, and re-layouts  17.4 us (11%)
  other arithmetic  12.3 us (8%)
    pallas_call x3, Pallas kernels, near_part(): pl.pallas_call(functools.partial(near_kernel, first, devices, len(sources...  39.2 us
    all_to_all x4, starting transfers between devices, exchange(): return lax.all_to_all(copies, axis, split_axis=0, concat_axis=0, tiled=True)  29.7 us
    ppermute x12, waiting for transfers between devices, ring(): return lax.ppermute(block, AXES, route)  17.1 us
    pallas_call x2, Pallas kernels, far_terms(): pl.pallas_call(functools.partial(far_kernel, depths, seed is not None), o...  16.1 us
    ppermute x12, starting transfers between devices, ring(): return lax.ppermute(block, AXES, route)  14.7 us
    unnamed x31, local copies, waits for them, and re-layouts  8.55 us
    all_to_all x4, waiting for transfers between devices, exchange(): return lax.all_to_all(copies, axis, split_axis=0, concat_axis=0, tiled=True)  6.12 us
    ppermute x4, starting transfers between devices, swap(): return lax.ppermute(block, axis, [(i, i ^ bit) for i in range(count)])  4.71 us
  transfers between devices with their start and end apart: 20, of which 5 were waited for; matrix products, arithmetic and copies ran while one was open for 10% of the time, Pallas kernels for 36%

profile of v6, /device:TPU:10, one launch (start us, length us, event | category | flops | bytes accessed | tf_op | source)
XLA Modules:
  0.0 163.3 jit_solution(4444199248856429453)
XLA Ops:
  0.6 1.0 constant_dynamic-slice_fusion
  1.6 1.1 constant_dynamic-slice_fusion.1
  2.8 0.8 pad_maximum_fusion.3
  3.6 0.8 fusion.31
  4.4 1.9 %collective-permute-start = (bf16[96,2048]{1,0:T(8,128)(2,1)}, bf16[96,2048]{1,0:T(8,128)(2,1)}, u32[]{:S(2)}, u32[]{:S(2)}) collective-permute-start(bf16[96,2048]{1,0:T(8,128)(2,1)} %get-tuple-element.50), channel_id=1, source_target_pairs={{0,32},{1,9},{2,34},{3,11},{4,36},{5,13},{6,38},{7,15},{8,40},{9,1... | collective-permute-start | bytes 1179656 | tf_op jit(solution)/shard_map/ppermute | solution.py:52
  6.3 2.1 %collective-permute-start.1 = (bf16[96,2048]{1,0:T(8,128)(2,1)}, bf16[96,2048]{1,0:T(8,128)(2,1)}, u32[]{:S(2)}, u32[]{:S(2)}) collective-permute-start(bf16[96,2048]{1,0:T(8,128)(2,1)} %get-tuple-element.50), channel_id=1, source_target_pairs={{0,96},{1,25},{2,98},{3,27},{4,100},{5,29},{6,102},{7,31},{8,104},... | collective-permute-start | bytes 1179656 | tf_op jit(solution)/shard_map/ppermute | solution.py:52
  8.4 1.6 broadcast_in_dim.77
  10.1 5.0 %all-to-all-start = ((bf16[4,64,4096]{2,1,0:T(8,128)(2,1)}), bf16[4,64,4096]{2,1,0:T(8,128)(2,1)S(1)}, u32[]{:S(2)}, u32[]{:S(2)}) async-start(bf16[4,64,4096]{2,1,0:T(8,128)(2,1)} %broadcast_in_dim.77), calls=%async_computation | async-start | bytes 4194304 | tf_op jit(solution)/shard_map/all_to_all | solution.py:287
  15.3 2.1 %collective-permute-start.4 = (bf16[96,2048]{1,0:T(8,128)(2,1)S(1)}, bf16[96,2048]{1,0:T(8,128)(2,1)}, u32[]{:S(2)}, u32[]{:S(2)}) collective-permute-start(bf16[96,2048]{1,0:T(8,128)(2,1)S(1)} %collective-permute-done.3), channel_id=1, source_target_pairs={{0,96},{1,25},{2,98},{3,27},{4,100},{5,29},{6,102},{7,31},{8,104},... | collective-permute-start | bytes 1179656 | tf_op jit(solution)/shard_map/ppermute | solution.py:52
  18.1 5.1 %collective-permute-done.4 = bf16[96,2048]{1,0:T(8,128)(2,1)} collective-permute-done((bf16[96,2048]{1,0:T(8,128)(2,1)S(1)}, bf16[96,2048]{1,0:T(8,128)(2,1)}, u32[]{:S(2)}, u32[]{:S(2)}) %collective-permute-start.4) | collective-permute-done | bytes 393248 | tf_op jit(solution)/shard_map/ppermute | solution.py:52
  23.2 3.2 %collective-permute-start.5 = (bf16[96,2048]{1,0:T(8,128)(2,1)}, bf16[96,2048]{1,0:T(8,128)(2,1)}, u32[]{:S(2)}, u32[]{:S(2)}) collective-permute-start(bf16[96,2048]{1,0:T(8,128)(2,1)} %collective-permute-done.4), channel_id=1, source_target_pairs={{0,96},{1,25},{2,98},{3,27},{4,100},{5,29},{6,102},{7,31},{8,104},... | collective-permute-start | bytes 1179656 | tf_op jit(solution)/shard_map/ppermute | solution.py:52
  26.8 1.3 copy.16
  28.2 3.9 %collective-permute-done.5 = bf16[96,2048]{1,0:T(8,128)(2,1)} collective-permute-done((bf16[96,2048]{1,0:T(8,128)(2,1)}, bf16[96,2048]{1,0:T(8,128)(2,1)}, u32[]{:S(2)}, u32[]{:S(2)}) %collective-permute-start.5) | collective-permute-done | bytes 393248 | tf_op jit(solution)/shard_map/ppermute | solution.py:52
  32.1 2.6 %pad_maximum_fusion.refs_0_ = bf16[4,96,2048]{2,1,0:T(8,128)(2,1)} fusion(bf16[1,96,2048]{2,1,0:T(8,128)(2,1)} %bitcast.3, bf16[1,96,2048]{2,1,0:T(8,128)(2,1)} %bitcast.2, bf16[1,96,2048]{2,1,0:T(8,128)(2,1)} %bitcast.1, bf16[1,96,2048]{2,1,0:T(8,128)(2,1)S(1)} %get-tuple-element.49), kind=kLoop, calls=%fused_computation.8 | loop fusion | flops 2359296 | bytes 3145728 | tf_op jit(solution)/shard_map/stack | solution.py:361
  34.7 1.5 collective-permute-start.7
  36.2 0.5 collective-permute-start.9
  36.7 2.9 %collective-permute-done.6 = bf16[96,2048]{1,0:T(8,128)(2,1)S(1)} collective-permute-done((bf16[96,2048]{1,0:T(8,128)(2,1)S(1)}, bf16[96,2048]{1,0:T(8,128)(2,1)S(1)}, u32[]{:S(2)}, u32[]{:S(2)}) %collective-permute-start.6) | collective-permute-done | bytes 393248 | tf_op jit(solution)/shard_map/ppermute | solution.py:52
  39.6 2.6 %pad_maximum_fusion.1.refs_1_ = bf16[4,96,2048]{2,1,0:T(8,128)(2,1)} fusion(bf16[1,96,2048]{2,1,0:T(8,128)(2,1)} %bitcast.7, bf16[1,96,2048]{2,1,0:T(8,128)(2,1)} %bitcast.6, bf16[1,96,2048]{2,1,0:T(8,128)(2,1)S(1)} %bitcast.30, bf16[1,96,2048]{2,1,0:T(8,128)(2,1)S(1)} %bitcast.29), kind=kLoop, calls=%fused_computation.9 | loop fusion | flops 2359296 | bytes 3145728 | tf_op jit(solution)/shard_map/stack | solution.py:362
  42.2 0.7 collective-permute-start.8
  42.9 1.3 collective-permute-start.10
  44.4 1.5 fusion.4
  46.2 2.4 %gather_fusion = bf16[512,64]{1,0:T(8,128)(2,1)S(1)} fusion(bf16[64,4096]{0,1:T(8,128)(2,1)} %copy.16, s32[1024]{0:T(1024)S(1)} %pad_clamp_fusion), kind=kCustom, calls=%fused_computation | custom fusion | bytes 133120 | tf_op jit(solution)/shard_map/gather | solution.py:370
  48.8 1.0 broadcast_in_dim.79
  49.8 4.8 %all-to-all-start.1 = ((bf16[8,96,512]{2,1,0:T(8,128)(2,1)}), bf16[8,96,512]{2,1,0:T(8,128)(2,1)S(1)}, u32[]{:S(2)}, u32[]{:S(2)}) async-start(bf16[8,96,512]{2,1,0:T(8,128)(2,1)} %broadcast_in_dim.79), calls=%async_computation.1 | async-start | bytes 1572864 | tf_op jit(solution)/shard_map/all_to_all | solution.py:287
  54.9 0.9 copy-done.5
  55.8 2.8 %shard_map.77 = f32[32,4096]{1,0:T(8,128)S(1)} custom-call(bf16[64,4096]{1,0:T(8,128)(2,1)S(1)} %copy-done, bf16[32,4096]{1,0:T(8,128)(2,1)S(1)} %copy-done.5), custom_call_target="tpu_custom_call" | custom-call | flops 3758096384 | bytes 2097152 | tf_op jit(solution)/shard_map/pallas_call | solution.py:100
  58.6 0.8 copy-done.2
  59.5 0.7 fusion.35
  60.2 6.1 %all-to-all-done.1.nodes_ref = bf16[8,96,512]{2,1,0:T(8,128)(2,1)S(1)} async-done(((bf16[8,96,512]{2,1,0:T(8,128)(2,1)}), bf16[8,96,512]{2,1,0:T(8,128)(2,1)S(1)}, u32[]{:S(2)}, u32[]{:S(2)}) %all-to-all-start.1) | async-done | bytes 786464 | tf_op jit(solution)/shard_map/all_to_all | solution.py:287
  66.3 0.7 shard_map.79
  67.0 0.9 copy-done.1
  67.9 0.7 collective-permute-start.12
  68.6 5.2 %collective-permute-done.10.refs_5_ = bf16[4,96,2048]{2,1,0:T(8,128)(2,1)} collective-permute-done((bf16[4,96,2048]{2,1,0:T(8,128)(2,1)}, bf16[4,96,2048]{2,1,0:T(8,128)(2,1)}, u32[]{:S(2)}, u32[]{:S(2)}) %collective-permute-start.10) | collective-permute-done | bytes 1572896 | tf_op jit(solution)/shard_map/ppermute | solution.py:52
  73.8 0.5 collective-permute-start.13
  74.3 14.9 %shard_map.78.refs_2_ = f32[4,32,4096]{2,1,0:T(8,128)S(1)} custom-call(s32[96]{0:T(128)S(1)} %slice.32.pair_ref, s32[1]{0:T(128)} %get-tuple-element.73.count_ref, bf16[4,64,4096]{2,1,0:T(8,128)(2,1)S(1)} %all-to-all-done.target_ref, bf16[4,96,2048]{2,1,0:T(8,128)(2,1)} %pad_maximum_fusion.refs_0_, bf16[4,96,2048]{2,1,0:T(8,128)(2,1)} %pad_maximum_fusion.1.refs_1_, ...), custom_call_target="tpu_custom_call" | custom-call | flops 16911433728 | bytes 8388608 | tf_op jit(solution)/shard_map/pallas_call | solution.py:267
  89.2 1.3 copy-done.9
  90.5 4.6 %collective-permute-start.14 = (bf16[96,512]{1,0:T(8,128)(2,1)}, bf16[96,512]{1,0:T(8,128)(2,1)S(1)}, u32[]{:S(2)}, u32[]{:S(2)}) collective-permute-start(bf16[96,512]{1,0:T(8,128)(2,1)} %get-tuple-element.31), channel_id=1, source_target_pairs={{0,8},{8,0},{16,24},{24,16},{1,9},{9,1},{17,25},{25,17},{2,10},{10... | collective-permute-start | bytes 294920 | tf_op jit(solution)/shard_map/ppermute | solution.py:40
  95.1 7.8 %all-to-all-start.2 = ((bf16[16,96,256]{2,1,0:T(8,128)(2,1)}), bf16[16,96,256]{2,1,0:T(8,128)(2,1)}, u32[]{:S(2)}, u32[]{:S(2)}) async-start(bf16[16,96,256]{2,1,0:T(8,128)(2,1)} %copy-done.1), calls=%async_computation.2 | async-start | bytes 1572864 | tf_op jit(solution)/shard_map/all_to_all | solution.py:287
  102.9 17.4 %shard_map.80 = bf16[4,32,4096]{2,1,0:T(8,128)(2,1)S(1)} custom-call(s32[128]{0:T(128)S(1)} %slice.31.pair_ref, s32[1]{0:T(128)} %get-tuple-element.72.count_ref, bf16[4,64,4096]{2,1,0:T(8,128)(2,1)} %collective-permute-done.11.target_ref, bf16[4,96,2048]{2,1,0:T(8,128)(2,1)} %pad_maximum_fusion.refs_0_, bf16[4,96,2048]{2,1,0:T(8,128)(2,1)} %pad_maximum_fusion.1.refs_1_, ...), custom_call_target="tpu_custom_call" | custom-call | flops 22548578304 | bytes 8388608 | tf_op jit(solution)/shard_map/pallas_call | solution.py:267
  120.3 1.0 copy-done.6
  121.3 0.6 copy-done.7
  121.9 1.6 copy-done.10
  123.5 6.9 %shard_map.81 = f32[4,32,4096]{2,1,0:T(8,128)S(1)} custom-call(s32[32]{0:T(128)S(1)} %slice.30.pair_ref, s32[1]{0:T(128)} %get-tuple-element.71.count_ref, bf16[4,64,4096]{2,1,0:T(8,128)(2,1)S(1)} %all-to-all-done.target_ref, bf16[4,96,2048]{2,1,0:T(8,128)(2,1)} %collective-permute-done.12.refs_6_.refs_0_, ...), custom_call_target="tpu_custom_call" | custom-call | flops 5637144576 | bytes 8388608 | tf_op jit(solution)/shard_map/pallas_call | solution.py:267
  130.5 2.5 %add_convert_fusion = bf16[4,32,4096]{2,1,0:T(8,128)(2,1)} fusion(f32[4,32,4096]{2,1,0:T(8,128)S(1)} %shard_map.81, bf16[4,32,4096]{2,1,0:T(8,128)(2,1)} %collective-permute-done.15), kind=kLoop, calls=%fused_computation.7 | loop fusion | flops 1572864 | bytes 4194304 | tf_op jit(solution)/shard_map/convert_element_type | solution.py:390
  132.9 12.0 %all-to-all-start.3 = ((bf16[4,32,4096]{2,1,0:T(8,128)(2,1)}), bf16[4,32,4096]{2,1,0:T(8,128)(2,1)}, u32[]{:S(2)}, u32[]{:S(2)}) async-start(bf16[4,32,4096]{2,1,0:T(8,128)(2,1)} %add_convert_fusion), calls=%async_computation.3 | async-start | bytes 2097152 | tf_op jit(solution)/shard_map/all_to_all | solution.py:287
  145.0 6.1 %shard_map.82.refs_0_ = f32[32,4096]{1,0:T(8,128)S(1)} custom-call(s32[1]{0:T(128)} %bitcast.11.place_ref, bf16[64,4096]{1,0:T(8,128)(2,1)S(1)} %copy-done, bf16[96,512]{1,0:T(8,128)(2,1)S(1)} %dynamic-slice_bitcast_fusion.sibling_ref, bf16[8,96,512]{2,1,0:T(8,128)(2,1)S(1)} %all-to-all-done.1.nodes_ref), custom_call_target="tpu_custom_call" | custom-call | flops 11274289152 | bytes 4194304 | tf_op jit(solution)/shard_map/pallas_call | solution.py:173
  151.0 10.1 %shard_map.83 = f32[32,4096]{1,0:T(8,128)} custom-call(s32[1]{0:T(128)} %bitcast.10.place_ref, bf16[64,4096]{1,0:T(8,128)(2,1)S(1)} %copy-done, bf16[96,512]{1,0:T(8,128)(2,1)S(1)} %copy-done.8, bf16[16,96,256]{2,1,0:T(8,128)(2,1)} %all-to-all-done.2.nodes_ref, f32[32,4096]{1,0:T(8,128)S(1)} %shard_map.82.refs_0_), custom_call_target="tpu_custom_call" | custom-call | flops 15032385536 | bytes 4194304 | tf_op jit(solution)/shard_map/pallas_call | solution.py:173
  161.1 2.1 %fusion.5 = f32[32,4096]{1,0:T(8,128)} fusion(f32[32,4096]{1,0:T(8,128)S(1)} %copy-done.3, bf16[4,32,4096]{2,1,0:T(8,128)(2,1)} %all-to-all-done.3), kind=kLoop, calls=%fused_computation.15 | loop fusion | flops 1179648 | bytes 2097152 | tf_op jit(solution)/shard_map/mul | solution.py:399
  (66 shorter events, 2.3 us)
Async XLA Ops:
  1.6 6.8 %copy-start = (bf16[64,4096]{1,0:T(8,128)(2,1)S(1)}, bf16[64,4096]{1,0:T(8,128)(2,1)}, u32[]{:S(2)}) copy-start(bf16[64,4096]{1,0:T(8,128)(2,1)} %points_ref.4) | copy-start | bytes 1572868
  3.6 11.7 %collective-permute-start.3 = (bf16[96,2048]{1,0:T(8,128)(2,1)}, bf16[96,2048]{1,0:T(8,128)(2,1)S(1)}, u32[]{:S(2)}, u32[]{:S(2)}) collective-permute-start(bf16[96,2048]{1,0:T(8,128)(2,1)} %pad_maximum_fusion.3), channel_id=1, source_target_pairs={{0,1},{1,0},{2,3},{3,2},{4,5},{5,4},{6,7},{7,6},{8,9},{9,8},{10,11... | collective-permute-start | bytes 1179656 | tf_op jit(solution)/shard_map/ppermute | solution.py:40
  4.4 13.6 %collective-permute-start = (bf16[96,2048]{1,0:T(8,128)(2,1)}, bf16[96,2048]{1,0:T(8,128)(2,1)}, u32[]{:S(2)}, u32[]{:S(2)}) collective-permute-start(bf16[96,2048]{1,0:T(8,128)(2,1)} %get-tuple-element.50), channel_id=1, source_target_pairs={{0,32},{1,9},{2,34},{3,11},{4,36},{5,13},{6,38},{7,15},{8,40},{9,1... | collective-permute-start | bytes 1179656 | tf_op jit(solution)/shard_map/ppermute | solution.py:52
  6.3 25.8 %collective-permute-start.1 = (bf16[96,2048]{1,0:T(8,128)(2,1)}, bf16[96,2048]{1,0:T(8,128)(2,1)}, u32[]{:S(2)}, u32[]{:S(2)}) collective-permute-start(bf16[96,2048]{1,0:T(8,128)(2,1)} %get-tuple-element.50), channel_id=1, source_target_pairs={{0,96},{1,25},{2,98},{3,27},{4,100},{5,29},{6,102},{7,31},{8,104},... | collective-permute-start | bytes 1179656 | tf_op jit(solution)/shard_map/ppermute | solution.py:52
  10.1 5.0 %copy-start.12 = (s32[1024]{0:T(1024)S(1)}, s32[1024]{0:T(1024)}, u32[]{:S(2)}) copy-start(s32[1024]{0:T(1024)} %param.11) | copy-start | bytes 12292
  10.1 7.5 %copy-start.11 = (s32[1024,12]{0,1:T(8,128)S(1)}, s32[1024,12]{0,1:T(8,128)}, u32[]{:S(2)}) copy-start(s32[1024,12]{0,1:T(8,128)} %param.10) | copy-start | bytes 147460
  10.1 38.7 %all-to-all-start = ((bf16[4,64,4096]{2,1,0:T(8,128)(2,1)}), bf16[4,64,4096]{2,1,0:T(8,128)(2,1)S(1)}, u32[]{:S(2)}, u32[]{:S(2)}) async-start(bf16[4,64,4096]{2,1,0:T(8,128)(2,1)} %broadcast_in_dim.77), calls=%async_computation | async-start | bytes 4194304 | tf_op jit(solution)/shard_map/all_to_all | solution.py:287
  15.3 8.0 %collective-permute-start.4 = (bf16[96,2048]{1,0:T(8,128)(2,1)S(1)}, bf16[96,2048]{1,0:T(8,128)(2,1)}, u32[]{:S(2)}, u32[]{:S(2)}) collective-permute-start(bf16[96,2048]{1,0:T(8,128)(2,1)S(1)} %collective-permute-done.3), channel_id=1, source_target_pairs={{0,96},{1,25},{2,98},{3,27},{4,100},{5,29},{6,102},{7,31},{8,104},... | collective-permute-start | bytes 1179656 | tf_op jit(solution)/shard_map/ppermute | solution.py:52
  18.0 10.2 %collective-permute-start.2 = (bf16[96,2048]{1,0:T(8,128)(2,1)}, bf16[96,2048]{1,0:T(8,128)(2,1)}, u32[]{:S(2)}, u32[]{:S(2)}) collective-permute-start(bf16[96,2048]{1,0:T(8,128)(2,1)} %collective-permute-done), channel_id=1, source_target_pairs={{0,32},{1,9},{2,34},{3,11},{4,36},{5,13},{6,38},{7,15},{8,40},{9,1... | collective-permute-start | bytes 1179656 | tf_op jit(solution)/shard_map/ppermute | solution.py:52
  23.2 8.8 %collective-permute-start.5 = (bf16[96,2048]{1,0:T(8,128)(2,1)}, bf16[96,2048]{1,0:T(8,128)(2,1)}, u32[]{:S(2)}, u32[]{:S(2)}) collective-permute-start(bf16[96,2048]{1,0:T(8,128)(2,1)} %collective-permute-done.4), channel_id=1, source_target_pairs={{0,96},{1,25},{2,98},{3,27},{4,100},{5,29},{6,102},{7,31},{8,104},... | collective-permute-start | bytes 1179656 | tf_op jit(solution)/shard_map/ppermute | solution.py:52
  28.2 11.5 %collective-permute-start.6 = (bf16[96,2048]{1,0:T(8,128)(2,1)S(1)}, bf16[96,2048]{1,0:T(8,128)(2,1)S(1)}, u32[]{:S(2)}, u32[]{:S(2)}) collective-permute-start(bf16[96,2048]{1,0:T(8,128)(2,1)S(1)} %collective-permute-done.3), channel_id=1, source_target_pairs={{0,32},{1,9},{2,34},{3,11},{4,36},{5,13},{6,38},{7,15},{8,40},{9,1... | collective-permute-start | bytes 1179656 | tf_op jit(solution)/shard_map/ppermute | solution.py:52
  34.7 33.2 %collective-permute-start.7 = (bf16[4,96,2048]{2,1,0:T(8,128)(2,1)}, bf16[4,96,2048]{2,1,0:T(8,128)(2,1)}, u32[]{:S(2)}, u32[]{:S(2)}) collective-permute-start(bf16[4,96,2048]{2,1,0:T(8,128)(2,1)} %pad_maximum_fusion.refs_0_), channel_id=1, source_target_pairs={{0,8},{1,33},{2,10},{3,35},{4,12},{5,37},{6,14},{7,39},{8,16},{9,4... | collective-permute-start | bytes 4718600 | tf_op jit(solution)/shard_map/ppermute | solution.py:52
  36.2 38.1 %collective-permute-start.9 = (bf16[4,96,2048]{2,1,0:T(8,128)(2,1)}, bf16[4,96,2048]{2,1,0:T(8,128)(2,1)}, u32[]{:S(2)}, u32[]{:S(2)}) collective-permute-start(bf16[4,96,2048]{2,1,0:T(8,128)(2,1)} %pad_maximum_fusion.refs_0_), channel_id=1, source_target_pairs={{0,24},{1,97},{2,26},{3,99},{4,28},{5,101},{6,30},{7,103},{8,0},{9... | collective-permute-start | bytes 4718600 | tf_op jit(solution)/shard_map/ppermute | solution.py:52
  39.6 4.8 %copy-start.4 = (bf16[32,4096]{1,0:T(8,128)(2,1)S(1)}, bf16[32,4096]{1,0:T(8,128)(2,1)}, u32[]{:S(2)}) copy-start(bf16[32,4096]{1,0:T(8,128)(2,1)} %weights_ref.1) | copy-start | bytes 786436
  39.6 4.8 %copy-start.14 = (s32[4096]{0:T(1024)S(1)}, s32[4096]{0:T(1024)}, u32[]{:S(2)}) copy-start(s32[4096]{0:T(1024)} %param.9) | copy-start | bytes 49156
  42.2 32.1 %collective-permute-start.8 = (bf16[4,96,2048]{2,1,0:T(8,128)(2,1)}, bf16[4,96,2048]{2,1,0:T(8,128)(2,1)}, u32[]{:S(2)}, u32[]{:S(2)}) collective-permute-start(bf16[4,96,2048]{2,1,0:T(8,128)(2,1)} %pad_maximum_fusion.1.refs_1_), channel_id=1, source_target_pairs={{0,8},{1,33},{2,10},{3,35},{4,12},{5,37},{6,14},{7,39},{8,16},{9,4... | collective-permute-start | bytes 4718600 | tf_op jit(solution)/shard_map/ppermute | solution.py:52
  42.9 30.8 %collective-permute-start.10 = (bf16[4,96,2048]{2,1,0:T(8,128)(2,1)}, bf16[4,96,2048]{2,1,0:T(8,128)(2,1)}, u32[]{:S(2)}, u32[]{:S(2)}) collective-permute-start(bf16[4,96,2048]{2,1,0:T(8,128)(2,1)} %pad_maximum_fusion.1.refs_1_), channel_id=1, source_target_pairs={{0,24},{1,97},{2,26},{3,99},{4,28},{5,101},{6,30},{7,103},{8,0},{9... | collective-permute-start | bytes 4718600 | tf_op jit(solution)/shard_map/ppermute | solution.py:52
  44.4 1.7 %copy-start.13 = (s32[512]{0:T(512)S(1)}, s32[512]{0:T(512)}, u32[]{:S(2)}) copy-start(s32[512]{0:T(512)} %param.8) | copy-start | bytes 6148
  49.8 16.5 %all-to-all-start.1 = ((bf16[8,96,512]{2,1,0:T(8,128)(2,1)}), bf16[8,96,512]{2,1,0:T(8,128)(2,1)S(1)}, u32[]{:S(2)}, u32[]{:S(2)}) async-start(bf16[8,96,512]{2,1,0:T(8,128)(2,1)} %broadcast_in_dim.79), calls=%async_computation.1 | async-start | bytes 1572864 | tf_op jit(solution)/shard_map/all_to_all | solution.py:287
  54.7 48.1 %collective-permute-start.11 = (bf16[4,64,4096]{2,1,0:T(8,128)(2,1)S(1)}, bf16[4,64,4096]{2,1,0:T(8,128)(2,1)}, u32[]{:S(2)}, u32[]{:S(2)}) collective-permute-start(bf16[4,64,4096]{2,1,0:T(8,128)(2,1)S(1)} %all-to-all-done.target_ref), channel_id=1, source_target_pairs={{0,1},{1,0},{2,3},{3,2},{4,5},{5,4},{6,7},{7,6},{8,9},{9,8},{10,11... | collective-permute-start | bytes 6291464 | tf_op jit(solution)/shard_map/ppermute | solution.py:40
  54.9 0.9 copy-start.5
  58.6 0.8 copy-start.2
  67.0 0.9 copy-start.1
  67.9 35.0 %collective-permute-start.12 = (bf16[4,96,2048]{2,1,0:T(8,128)(2,1)}, bf16[4,96,2048]{2,1,0:T(8,128)(2,1)}, u32[]{:S(2)}, u32[]{:S(2)}) collective-permute-start(bf16[4,96,2048]{2,1,0:T(8,128)(2,1)} %collective-permute-done.7.refs_2_), channel_id=1, source_target_pairs={{0,8},{1,33},{2,10},{3,35},{4,12},{5,37},{6,14},{7,39},{8,16},{9,4... | collective-permute-start | bytes 4718600 | tf_op jit(solution)/shard_map/ppermute | solution.py:52
  73.8 29.1 %collective-permute-start.13 = (bf16[4,96,2048]{2,1,0:T(8,128)(2,1)}, bf16[4,96,2048]{2,1,0:T(8,128)(2,1)}, u32[]{:S(2)}, u32[]{:S(2)}) collective-permute-start(bf16[4,96,2048]{2,1,0:T(8,128)(2,1)} %collective-permute-done.10.refs_5_), channel_id=1, source_target_pairs={{0,24},{1,97},{2,26},{3,99},{4,28},{5,101},{6,30},{7,103},{8,0},{9... | collective-permute-start | bytes 4718600 | tf_op jit(solution)/shard_map/ppermute | solution.py:52
  89.2 1.3 copy-start.9
  90.5 30.8 %collective-permute-start.14 = (bf16[96,512]{1,0:T(8,128)(2,1)}, bf16[96,512]{1,0:T(8,128)(2,1)S(1)}, u32[]{:S(2)}, u32[]{:S(2)}) collective-permute-start(bf16[96,512]{1,0:T(8,128)(2,1)} %get-tuple-element.31), channel_id=1, source_target_pairs={{0,8},{8,0},{16,24},{24,16},{1,9},{9,1},{17,25},{25,17},{2,10},{10... | collective-permute-start | bytes 294920 | tf_op jit(solution)/shard_map/ppermute | solution.py:40
  95.1 26.8 %all-to-all-start.2 = ((bf16[16,96,256]{2,1,0:T(8,128)(2,1)}), bf16[16,96,256]{2,1,0:T(8,128)(2,1)}, u32[]{:S(2)}, u32[]{:S(2)}) async-start(bf16[16,96,256]{2,1,0:T(8,128)(2,1)} %copy-done.1), calls=%async_computation.2 | async-start | bytes 1572864 | tf_op jit(solution)/shard_map/all_to_all | solution.py:287
  120.3 1.0 copy-start.6
  121.3 0.6 copy-start.7
  121.9 8.5 %collective-permute-start.15 = (bf16[4,32,4096]{2,1,0:T(8,128)(2,1)}, bf16[4,32,4096]{2,1,0:T(8,128)(2,1)}, u32[]{:S(2)}, u32[]{:S(2)}) collective-permute-start(bf16[4,32,4096]{2,1,0:T(8,128)(2,1)} %copy-done.6), channel_id=1, source_target_pairs={{0,1},{1,0},{2,3},{3,2},{4,5},{5,4},{6,7},{7,6},{8,9},{9,8},{10,11... | collective-permute-start | bytes 3145736 | tf_op jit(solution)/shard_map/ppermute | solution.py:40
  121.9 1.6 copy-start.10
  132.9 28.2 %all-to-all-start.3 = ((bf16[4,32,4096]{2,1,0:T(8,128)(2,1)}), bf16[4,32,4096]{2,1,0:T(8,128)(2,1)}, u32[]{:S(2)}, u32[]{:S(2)}) async-start(bf16[4,32,4096]{2,1,0:T(8,128)(2,1)} %add_convert_fusion), calls=%async_computation.3 | async-start | bytes 2097152 | tf_op jit(solution)/shard_map/all_to_all | solution.py:287
  145.0 6.1 %copy-start.8 = (bf16[96,512]{1,0:T(8,128)(2,1)S(1)}, bf16[96,512]{1,0:T(8,128)(2,1)}, u32[]{:S(2)}) copy-start(bf16[96,512]{1,0:T(8,128)(2,1)} %copy-done.7) | copy-start | bytes 294916
  151.0 10.1 %copy-start.3 = (f32[32,4096]{1,0:T(8,128)S(1)}, f32[32,4096]{1,0:T(8,128)}, u32[]{:S(2)}) copy-start(f32[32,4096]{1,0:T(8,128)} %copy-done.2) | copy-start | bytes 1572868
